TPU v7x, 32 devices: a whole 2x2x4 slice. The times are simulated.
32 devices in a mesh: dp: 4 (over y, core), row: 2 (over x), col: 4 (over z).
Axes of the slice: x: 2, y: 2, z: 4, core: 2. Of those that a mesh axis runs over, the one named last changes fastest.
Arguments:
- inputs: bfloat16 [4096, 768], P(('dp', 'col'), 'row'), may hold values from -6 to 6
- cotangent: bfloat16 [4096, 768], P(('dp', 'col'), 'row'), may hold values from -6 to 6
- routes: int32 [4096, 2], P('dp'), may hold values from 0 to 15, all different within a row; in each aligned block of 1024 rows (0 to 1023, 1024 to 2047, ...) at most 192 rows name the same one
- cont_lengths: int32 [4, 8], P('dp'), may hold values from 1 to 128, 512 in all within a row
- first_gain: float32 [768], P('row'), may hold values from 0.5 to 1.5
- attend_in: bfloat16 [768, 2304], P('row', 'col'), may hold values from -0.21875 to 0.21875
- attend_out: bfloat16 [768, 768], P('col', 'row'), may hold values from -0.875 to 0.875
- second_gain: float32 [768], P('row'), may hold values from 0.5 to 1.5
- router_weight: float32 [768, 16], P('row'), may hold values from -0.15625 to 0.15625
- shared_gate: bfloat16 [768, 2048], P('row', 'col'), may hold values from -0.21875 to 0.21875
- shared_up: bfloat16 [768, 2048], P('row', 'col'), may hold values from -0.21875 to 0.21875
- shared_down: bfloat16 [2048, 768], P('col', 'row'), may hold values from -0.25 to 0.25
- expert_gate: bfloat16 [16, 768, 2048], P(None, 'row', 'col'), may hold values from -0.21875 to 0.21875
- expert_up: bfloat16 [16, 768, 2048], P(None, 'row', 'col'), may hold values from -0.21875 to 0.21875
- expert_down: bfloat16 [16, 2048, 768], P(None, 'col', 'row'), may hold values from -1 to 1
Outputs:
- layer_out: bfloat16 [4096, 768], P(('dp', 'col'), 'row')
- input_grad: bfloat16 [4096, 768], P(('dp', 'col'), 'row')
- first_gain_grad: float32 [768], P('row')
- attend_in_grad: float32 [768, 2304], P('row', 'col')
- attend_out_grad: float32 [768, 768], P('col', 'row')
- second_gain_grad: float32 [768], P('row')
- router_grad: float32 [768, 16], P('row')
- shared_gate_grad: float32 [768, 2048], P('row', 'col')
- shared_up_grad: float32 [768, 2048], P('row', 'col')
- shared_down_grad: float32 [2048, 768], P('col', 'row')
- expert_gate_grad: float32 [16, 768, 2048], P(None, 'row', 'col')
- expert_up_grad: float32 [16, 768, 2048], P(None, 'row', 'col')
- expert_down_grad: float32 [16, 2048, 768], P(None, 'col', 'row')
- balance_loss: float32 [], replicated
Inputs may be any that keep to these rules, and one draw needn't show every extreme that they name: `routes`: in each aligned block of 1024 rows, the tokens of one index of dp, the two experts of a token differ and no expert is named by more than 192 entries; some expert is named by exactly 192. `cont_lengths`: each row sums to 512, and some entry equals 128.
All inputs are finite; a program needn't handle non-finite values.
Results may differ from a plain program's by a relative error of at most 0.023.
Values may be sent and summed in bfloat16 or wider, within the bound.
No kernel may reach another device: no remote copies, remote signals or barrier semaphores. Data moves between devices by JAX's collectives and lax.ppermute only.
A program may use at most 384 MiB of HBM per device.

v0:
```python
import jax
import jax.numpy as jnp
from jax import lax
from jax.sharding import PartitionSpec as P

HD = 64


EPSILON = 1e-05
HIGHEST = lax.Precision.HIGHEST


def for_sending(value):
    return jax.tree.map(lambda a: a.astype(jnp.bfloat16) if a.dtype == jnp.float32 else a, value)


def feature_sums(values):
    return lax.psum(values, "row")


def token_gather(values):
    return lax.all_gather(values, "col", axis=0, tiled=True)


def slot_gather(values):
    return jax.tree.map(
        lambda part, own: part.astype(own.dtype),
        lax.all_gather(for_sending(values), "row", axis=0, tiled=True),
        values,
    )


def row_partials(term_fn, row_count):
    return lax.psum_scatter(
        term_fn(jnp.int32(0), lax.axis_size("row") * row_count),
        "row",
        scatter_dimension=0,
        tiled=True,
    )


def col_partials(term_fn, row_count):
    return lax.psum_scatter(
        term_fn(jnp.int32(0), lax.axis_size("col") * row_count).astype(jnp.bfloat16),
        "col",
        scatter_dimension=0,
        tiled=True,
    ).astype(jnp.float32)


def token_stats(values):
    return lax.psum(values, ("dp", "col"))


def rows_of(source, row_start, row_count):
    return lax.dynamic_slice_in_dim(source, row_start, row_count, 0)


def angle_table(position):
    half_dim = HD // 2
    frequency = 10000.0 ** (-jnp.arange(half_dim, dtype=jnp.float32) * 2.0 / HD)
    return position.astype(jnp.float32)[:, None] * frequency[None, :]


def rotate(values, angles):
    half_dim = values.shape[-1] // 2
    cosine = jnp.cos(angles)[:, None, :]
    sine_part = jnp.sin(angles)[:, None, :]
    first_half = values[..., :half_dim]
    second_half = values[..., half_dim:]
    return jnp.concatenate(
        [
            first_half * cosine - second_half * sine_part,
            first_half * sine_part + second_half * cosine,
        ],
        -1,
    )


def token_layout(cont_lengths, offsets, group_len):
    prompt_len = group_len // 2
    group_ids = offsets // group_len
    inner_pos = offsets % group_len
    seg_ends = jnp.cumsum(cont_lengths, axis=1)
    seg_starts = seg_ends - cont_lengths
    group_pick = (
        group_ids[:, None] == jnp.arange(cont_lengths.shape[0], dtype=jnp.int32)[None, :]
    ).astype(jnp.int32)
    ends_own = jnp.sum(group_pick[:, :, None] * seg_ends[None, :, :], 1)
    starts_own = jnp.sum(group_pick[:, :, None] * seg_starts[None, :, :], 1)
    after_prompt = inner_pos - prompt_len
    segment = 1 + jnp.sum((after_prompt[:, None] >= ends_own).astype(jnp.int32), 1)
    segment = jnp.where(after_prompt < 0, 0, segment)
    slot_pick = segment[:, None] - 1 == jnp.arange(cont_lengths.shape[1], dtype=jnp.int32)[None, :]
    seg_begin = jnp.sum(jnp.where(slot_pick, starts_own, 0), 1)
    position = jnp.where(segment == 0, inner_pos, prompt_len + after_prompt - seg_begin)
    return (group_ids, segment, position)


def gate_up_grad(pre_gate, pre_up, hidden_grad):
    gate_sig = jax.nn.sigmoid(pre_gate)
    grad_gate = hidden_grad * pre_up * gate_sig * (1.0 + pre_gate * (1.0 - gate_sig))
    grad_up = hidden_grad * pre_gate * gate_sig
    return jnp.concatenate([grad_gate, grad_up], 1).astype(jnp.bfloat16)


def body(
    inputs,
    cotangent,
    routes,
    cont_lengths,
    first_gain,
    attend_in,
    attend_out,
    second_gain,
    router_weight,
    shared_gate,
    shared_up,
    shared_down,
    expert_gate,
    expert_up,
    expert_down,
):
    row_size = lax.axis_size("row")
    col_size = lax.axis_size("col")
    data_size = lax.axis_size("dp")
    row_index = lax.axis_index("row")
    col_index = lax.axis_index("col")
    tok_rest, feat_dev = inputs.shape
    feat_full = feat_dev * row_size
    tok_block = tok_rest * col_size
    tok_query = tok_block // row_size
    experts = expert_gate.shape[0]
    hidden_dev = expert_gate.shape[2]
    shared_dev = shared_gate.shape[1]
    head_cols = attend_in.shape[1]
    heads_dev = head_cols // (3 * HD)
    capacity = tok_block * 3 // experts
    slots_dev = experts * capacity // row_size
    group_len = tok_block // cont_lengths.shape[0]
    key_block = min(1024, tok_query)
    block_count = group_len // key_block
    score_scale = HD ** (-0.5)
    tokens_all = float(data_size * tok_block)
    group_base = row_index * tok_query // group_len * group_len
    inputs_f = inputs.astype(jnp.float32)
    squares_one = feature_sums(jnp.sum(inputs_f * inputs_f, 1))
    scale_one = lax.rsqrt(squares_one / feat_full + EPSILON)[:, None]
    normed_one = (inputs_f * scale_one * first_gain).astype(jnp.bfloat16)
    normed_all = token_gather(normed_one)

    def qkv_term(row_start, row_count):
        return jnp.dot(
            rows_of(normed_all, row_start, row_count), attend_in, preferred_element_type=jnp.float32
        )

    qkv_raw = row_partials(qkv_term, tok_query).reshape(tok_query, heads_dev, 3, HD)
    query_offsets = row_index * tok_query + jnp.arange(tok_query, dtype=jnp.int32)
    query_group, query_segment, query_position = token_layout(
        cont_lengths, query_offsets, group_len
    )
    key_group, key_segment, key_position = token_layout(
        cont_lengths, jnp.arange(tok_block, dtype=jnp.int32), group_len
    )
    query_angles = angle_table(query_position)
    queries = rotate(qkv_raw[:, :, 0], query_angles).astype(jnp.bfloat16)
    keys_own = rotate(qkv_raw[:, :, 1], query_angles).astype(jnp.bfloat16)
    values_own = qkv_raw[:, :, 2].astype(jnp.bfloat16)
    keys_all, values_all = slot_gather(
        (keys_own.reshape(tok_query, heads_dev * HD), values_own.reshape(tok_query, heads_dev * HD))
    )

    def block_scores(block_start):
        key_rows = rows_of(keys_all, block_start, key_block).reshape(key_block, heads_dev, HD)
        block_group = rows_of(key_group, block_start, key_block)
        block_segment = rows_of(key_segment, block_start, key_block)
        block_position = rows_of(key_position, block_start, key_block)
        visible = (
            (query_group[:, None] == block_group[None, :])
            & ((block_segment[None, :] == 0) | (block_segment[None, :] == query_segment[:, None]))
            & (block_position[None, :] <= query_position[:, None])
        )
        scores = (
            jnp.einsum("qhd,khd->hqk", queries, key_rows, preferred_element_type=jnp.float32)
            * score_scale
        )
        return (scores, visible[None], key_rows)

    def forward_step(carry, block_index):
        run_max, run_total, run_accum = carry
        block_start = group_base + block_index * key_block
        scores, mask_now, key_rows = block_scores(block_start)
        value_rows = (
            rows_of(values_all, block_start, key_block)
            .reshape(key_block, heads_dev, HD)
            .astype(jnp.float32)
        )
        new_max = jnp.maximum(run_max, jnp.max(jnp.where(mask_now, scores, -1e30), -1))
        weights = jnp.where(mask_now, jnp.exp(scores - new_max[..., None]), 0.0)
        run_decay = jnp.exp(run_max - new_max)
        run_total = run_total * run_decay + jnp.sum(weights, -1)
        run_accum = run_accum * run_decay[..., None] + jnp.einsum(
            "hqk,khd->hqd", weights, value_rows, precision=HIGHEST
        )
        return ((new_max, run_total, run_accum), None)

    start_carry = (
        jnp.full((heads_dev, tok_query), -1e30, jnp.float32),
        jnp.zeros((heads_dev, tok_query), jnp.float32),
        jnp.zeros((heads_dev, tok_query, HD), jnp.float32),
    )
    (run_max, run_total, run_accum), unused_out = lax.scan(
        forward_step, start_carry, jnp.arange(block_count, dtype=jnp.int32)
    )
    log_total = run_max + jnp.log(run_total)
    attended = run_accum / run_total[..., None]
    attn_rows = attended.transpose(1, 0, 2).reshape(tok_query, heads_dev * HD).astype(jnp.bfloat16)
    outputs_all = slot_gather(attn_rows)

    def attention_term(row_start, row_count):
        return jnp.dot(
            rows_of(outputs_all, row_start, row_count),
            attend_out,
            preferred_element_type=jnp.float32,
        )

    mixed_one = inputs_f + col_partials(attention_term, tok_rest)
    gained = mixed_one * second_gain
    squares_two, logit_part = feature_sums(
        (jnp.sum(mixed_one * mixed_one, 1), jnp.dot(gained, router_weight, precision=HIGHEST))
    )
    scale_two = lax.rsqrt(squares_two / feat_full + EPSILON)[:, None]
    router_probs = jax.nn.softmax(logit_part * scale_two, -1)
    routes_rest = lax.dynamic_slice_in_dim(routes, col_index * tok_rest, tok_rest, 0)
    route_hot = routes_rest[:, :, None] == jnp.arange(experts, dtype=jnp.int32)[None, None, :]
    gate_vals = jnp.sum(jnp.where(route_hot, router_probs[:, None, :], 0.0), -1)
    count_total, prob_total = token_stats(
        (jnp.sum(route_hot.astype(jnp.float32), (0, 1)), jnp.sum(router_probs, 0))
    )
    balance_loss = experts * jnp.sum(count_total / (2.0 * tokens_all) * prob_total / tokens_all)
    unit_two = mixed_one * scale_two
    normed_two = (unit_two * second_gain).astype(jnp.bfloat16)
    normed_two_all = token_gather(normed_two)
    flat_routes = routes.reshape(-1)
    flat_hot = (flat_routes[:, None] == jnp.arange(experts, dtype=jnp.int32)[None, :]).astype(
        jnp.int32
    )
    earlier = jnp.cumsum(flat_hot, 0) - flat_hot
    slot_of = flat_routes * capacity + jnp.sum(earlier * flat_hot, 1)
    slot_pairs = slot_of.reshape(tok_block, 2)
    slot_source = (
        jnp.full((experts * capacity,), 2 * tok_block, jnp.int32)
        .at[slot_of]
        .set(jnp.arange(2 * tok_block, dtype=jnp.int32))
    )
    padded_two = jnp.concatenate([normed_two_all, jnp.zeros((1, feat_dev), jnp.bfloat16)], 0)
    expert_rows = padded_two[slot_source // 2]
    shared_both = jnp.concatenate([shared_gate, shared_up], 1)

    def shared_term(row_start, row_count):
        return jnp.dot(
            rows_of(normed_two_all, row_start, row_count),
            shared_both,
            preferred_element_type=jnp.float32,
        )

    shared_pre = row_partials(shared_term, tok_query)
    shared_g = shared_pre[:, :shared_dev]
    shared_u = shared_pre[:, shared_dev:]
    shared_hidden = (jax.nn.silu(shared_g) * shared_u).astype(jnp.bfloat16)
    expert_both = jnp.concatenate([expert_gate, expert_up], 2)

    def expert_term(row_start, row_count):
        group_count = row_count // capacity
        picked = rows_of(expert_rows, row_start, row_count).reshape(group_count, capacity, feat_dev)
        return jnp.einsum(
            "ecd,edf->ecf", picked, expert_both, preferred_element_type=jnp.float32
        ).reshape(row_count, 2 * hidden_dev)

    expert_pre = row_partials(expert_term, slots_dev)
    expert_g = expert_pre[:, :hidden_dev]
    expert_u = expert_pre[:, hidden_dev:]
    expert_hidden = (jax.nn.silu(expert_g) * expert_u).astype(jnp.bfloat16)
    shared_all, expert_all = slot_gather((shared_hidden, expert_hidden))
    expert_out = jnp.einsum(
        "ecf,efd->ecd",
        expert_all.reshape(experts, capacity, hidden_dev),
        expert_down,
        preferred_element_type=jnp.float32,
    ).reshape(experts * capacity, feat_dev)

    def output_term(row_start, row_count):
        shared_part = jnp.dot(
            rows_of(shared_all, row_start, row_count),
            shared_down,
            preferred_element_type=jnp.float32,
        )
        pair_slots = rows_of(slot_pairs, row_start, row_count)
        return jnp.concatenate(
            [shared_part, expert_out[pair_slots[:, 0]], expert_out[pair_slots[:, 1]]], 1
        )

    branch_sums = col_partials(output_term, tok_rest)
    shared_result = branch_sums[:, :feat_dev]
    expert_pick = branch_sums[:, feat_dev:].reshape(tok_rest, 2, feat_dev)
    expert_result = jnp.sum(gate_vals[:, :, None] * expert_pick, 1)
    layer_out = (mixed_one + shared_result + expert_result).astype(jnp.bfloat16)
    cot_f = cotangent.astype(jnp.float32)
    gate_grad = feature_sums(jnp.sum(expert_pick * cot_f[:, None, :], -1))
    expert_cot = (
        (gate_vals[:, :, None] * cot_f[:, None, :])
        .astype(jnp.bfloat16)
        .reshape(tok_rest, 2 * feat_dev)
    )
    cot_all = token_gather(jnp.concatenate([cotangent, expert_cot], 1))
    shared_cot = cot_all[:, :feat_dev]
    pair_cot = jnp.concatenate(
        [
            cot_all[:, feat_dev:].reshape(2 * tok_block, feat_dev),
            jnp.zeros((1, feat_dev), jnp.bfloat16),
        ],
        0,
    )
    slot_cot = pair_cot[slot_source]
    shared_down_grad = jnp.einsum(
        "tf,td->fd", shared_all, shared_cot, preferred_element_type=jnp.float32
    )

    def shared_back(row_start, row_count):
        return jnp.einsum(
            "td,fd->tf",
            rows_of(shared_cot, row_start, row_count),
            shared_down,
            preferred_element_type=jnp.float32,
        )

    shared_pgrad = gate_up_grad(shared_g, shared_u, row_partials(shared_back, tok_query))
    expert_down_grad = jnp.einsum(
        "ecf,ecd->efd",
        expert_all.reshape(experts, capacity, hidden_dev),
        slot_cot.reshape(experts, capacity, feat_dev),
        preferred_element_type=jnp.float32,
    )

    def expert_back(row_start, row_count):
        group_count = row_count // capacity
        picked = rows_of(slot_cot, row_start, row_count).reshape(group_count, capacity, feat_dev)
        return jnp.einsum(
            "ecd,efd->ecf", picked, expert_down, preferred_element_type=jnp.float32
        ).reshape(row_count, hidden_dev)

    expert_pgrad = gate_up_grad(expert_g, expert_u, row_partials(expert_back, slots_dev))
    shared_pall, expert_pall = slot_gather((shared_pgrad, expert_pgrad))
    expert_pall_view = expert_pall.reshape(experts, capacity, 2 * hidden_dev)
    expert_both_grad = jnp.einsum(
        "ecd,ecf->edf",
        expert_rows.reshape(experts, capacity, feat_dev),
        expert_pall_view,
        preferred_element_type=jnp.float32,
    )
    expert_input_grad = jnp.einsum(
        "ecf,edf->ecd", expert_pall_view, expert_both, preferred_element_type=jnp.float32
    ).reshape(experts * capacity, feat_dev)
    shared_both_grad = jnp.einsum(
        "td,tf->df", normed_two_all, shared_pall, preferred_element_type=jnp.float32
    )

    def normed_back(row_start, row_count):
        pair_slots = rows_of(slot_pairs, row_start, row_count)
        shared_part = jnp.einsum(
            "tf,df->td",
            rows_of(shared_pall, row_start, row_count),
            shared_both,
            preferred_element_type=jnp.float32,
        )
        return (
            shared_part + expert_input_grad[pair_slots[:, 0]] + expert_input_grad[pair_slots[:, 1]]
        )

    normed_grad = col_partials(normed_back, tok_rest)
    prob_grad = jnp.sum(
        jnp.where(route_hot, gate_grad[:, :, None], 0.0), 1
    ) + experts * count_total / (2.0 * tokens_all * tokens_all)
    logit_grad = router_probs * (prob_grad - jnp.sum(router_probs * prob_grad, -1, keepdims=True))
    router_grad = jnp.einsum("td,te->de", unit_two * second_gain, logit_grad, precision=HIGHEST)
    two_grad = normed_grad + jnp.einsum("te,de->td", logit_grad, router_weight, precision=HIGHEST)
    gained_two = two_grad * second_gain
    second_gain_grad = jnp.sum(two_grad * unit_two, 0)
    inner_two = feature_sums(jnp.sum(gained_two * unit_two, 1))[:, None] / feat_full
    mixed_grad = cot_f + scale_two * (gained_two - unit_two * inner_two)
    mix_all = token_gather(mixed_grad.astype(jnp.bfloat16))
    attend_out_grad = jnp.einsum(
        "tc,td->cd", outputs_all, mix_all, preferred_element_type=jnp.float32
    )

    def output_back(row_start, row_count):
        return jnp.einsum(
            "td,cd->tc",
            rows_of(mix_all, row_start, row_count),
            attend_out,
            preferred_element_type=jnp.float32,
        )

    attn_grad = (
        row_partials(output_back, tok_query).astype(jnp.bfloat16).reshape(tok_query, heads_dev, HD)
    )
    attn_grad_f = attn_grad.astype(jnp.float32)
    row_delta = jnp.sum(attn_grad_f.transpose(1, 0, 2) * attended, -1)
    queries_f = queries.astype(jnp.float32)

    def backward_step(query_grad, block_index):
        block_start = group_base + block_index * key_block
        scores, mask_now, key_rows = block_scores(block_start)
        value_rows = rows_of(values_all, block_start, key_block).reshape(key_block, heads_dev, HD)
        weights = jnp.where(mask_now, jnp.exp(scores - log_total[..., None]), 0.0)
        prob_dot = jnp.einsum(
            "qhd,khd->hqk", attn_grad, value_rows, preferred_element_type=jnp.float32
        )
        score_grad = weights * (prob_dot - row_delta[..., None])
        query_grad = (
            query_grad
            + jnp.einsum(
                "hqk,khd->qhd", score_grad, key_rows.astype(jnp.float32), precision=HIGHEST
            )
            * score_scale
        )
        key_grad = (
            jnp.einsum("hqk,qhd->khd", score_grad, queries_f, precision=HIGHEST) * score_scale
        )
        value_grad = jnp.einsum("hqk,qhd->khd", weights, attn_grad_f, precision=HIGHEST)
        return (
            query_grad,
            jnp.concatenate(
                [
                    key_grad.reshape(key_block, heads_dev * HD),
                    value_grad.reshape(key_block, heads_dev * HD),
                ],
                1,
            ),
        )

    query_grad, kv_terms = lax.scan(
        backward_step,
        jnp.zeros((tok_query, heads_dev, HD), jnp.float32),
        jnp.arange(block_count, dtype=jnp.int32),
    )
    kv_group = kv_terms.reshape(group_len, 2 * heads_dev * HD)
    kv_full = lax.dynamic_update_slice_in_dim(
        jnp.zeros((tok_block, 2 * heads_dev * HD), jnp.float32), kv_group, group_base, 0
    )

    def kv_term(row_start, row_count):
        return rows_of(kv_full, row_start, row_count)

    kv_grad = row_partials(kv_term, tok_query)
    key_grad_raw = rotate(
        kv_grad[:, : heads_dev * HD].reshape(tok_query, heads_dev, HD), -query_angles
    )
    value_grad_raw = kv_grad[:, heads_dev * HD :].reshape(tok_query, heads_dev, HD)
    query_grad_raw = rotate(query_grad, -query_angles)
    qkv_grad = (
        jnp.stack([query_grad_raw, key_grad_raw, value_grad_raw], 2)
        .reshape(tok_query, head_cols)
        .astype(jnp.bfloat16)
    )
    qkv_all = slot_gather(qkv_grad)
    attend_in_grad = jnp.einsum(
        "td,tc->dc", normed_all, qkv_all, preferred_element_type=jnp.float32
    )

    def input_back(row_start, row_count):
        return jnp.einsum(
            "tc,dc->td",
            rows_of(qkv_all, row_start, row_count),
            attend_in,
            preferred_element_type=jnp.float32,
        )

    one_grad = col_partials(input_back, tok_rest)
    unit_one = inputs_f * scale_one
    gained_one = one_grad * first_gain
    first_gain_grad = jnp.sum(one_grad * unit_one, 0)
    inner_one = feature_sums(jnp.sum(gained_one * unit_one, 1))[:, None] / feat_full
    input_grad = (mixed_grad + scale_one * (gained_one - unit_one * inner_one)).astype(jnp.bfloat16)
    first_gain_grad, second_gain_grad, router_grad = token_stats(
        (first_gain_grad, second_gain_grad, router_grad)
    )
    summed = (
        lax.psum(attend_in_grad.astype(jnp.bfloat16), "dp").astype(jnp.float32),
        lax.psum(attend_out_grad.astype(jnp.bfloat16), "dp").astype(jnp.float32),
        lax.psum(shared_both_grad.astype(jnp.bfloat16), "dp").astype(jnp.float32),
        lax.psum(shared_down_grad.astype(jnp.bfloat16), "dp").astype(jnp.float32),
        lax.psum(expert_both_grad.astype(jnp.bfloat16), "dp").astype(jnp.float32),
        lax.psum(expert_down_grad.astype(jnp.bfloat16), "dp").astype(jnp.float32),
    )
    shared_both_sum = summed[2]
    expert_both_sum = summed[4]
    return (
        layer_out,
        input_grad,
        first_gain_grad,
        summed[0],
        summed[1],
        second_gain_grad,
        router_grad,
        shared_both_sum[:, :shared_dev],
        shared_both_sum[:, shared_dev:],
        summed[3],
        expert_both_sum[:, :, :hidden_dev],
        expert_both_sum[:, :, hidden_dev:],
        summed[5],
        balance_loss,
    )


def solution(mesh):
    in_specs = (
        P(("dp", "col"), "row"),
        P(("dp", "col"), "row"),
        P("dp", None),
        P("dp", None),
        P("row"),
        P("row", "col"),
        P("col", "row"),
        P("row"),
        P("row", None),
        P("row", "col"),
        P("row", "col"),
        P("col", "row"),
        P(None, "row", "col"),
        P(None, "row", "col"),
        P(None, "col", "row"),
    )
    out_specs = (
        P(("dp", "col"), "row"),
        P(("dp", "col"), "row"),
        P("row"),
        P("row", "col"),
        P("col", "row"),
        P("row"),
        P("row", None),
        P("row", "col"),
        P("row", "col"),
        P("col", "row"),
        P(None, "row", "col"),
        P(None, "row", "col"),
        P(None, "col", "row"),
        P(),
    )
    return jax.shard_map(body, mesh=mesh, in_specs=in_specs, out_specs=out_specs, check_vma=False)
```

profile of v0, /device:TPU:0, one launch (start us, length us, event | category | flops | bytes accessed | tf_op | source)
XLA Modules:
  0.0 1355.7 jit_solution(13509464850733719613)
XLA Ops:
  15.8 20.2 %all_gather.36 = bf16[1024,384]{1,0:T(8,128)(2,1)S(1)} all-gather(bf16[256,384]{1,0:T(8,128)(2,1)S(1)} %fusion.48), channel_id=1, replica_groups=mesh['dp'=4,'row'=2,'col'=4] {'col'}, dimensions={0}, use_global_device_ids=true | all-gather | bytes 983040 | tf_op jit(solution)/shard_map/all_gather | solution.py:22
  41.1 32.5 %reduce-scatter.12.cloned.1.call-done = f32[512,576]{0,1:T(8,128)} async-done(((f32[1024,576]{0,1:T(8,128)}), f32[512,576]{0,1:T(8,128)}) %reduce-scatter.12.cloned.1.call-update) | async-done | bytes 1179664 | tf_op jit(solution)/shard_map/reduce_scatter | solution.py:34
  90.2 19.0 %while.28 = (s32[]{:T(128)}, f32[3,512]{1,0:T(4,128)S(1)}, f32[3,512]{1,0:T(4,128)S(1)}, f32[3,512,64]{1,2,0:T(8,128)S(1)}, s32[2]{0:T(128)S(1)}, /*index=5*/s32...) while((s32[]{:T(128)}, f32[3,512]{1,0:T(4,128)S(1)}, ...), condition=%wide.region_11.12_spmd.clone, body=%wide.region_8.11_spmd.clone.sunk | while | flops 714391552 | bytes 25357612 | solution.py:212
  117.9 23.2 %reduce-scatter.14.cloned.1.call-done = bf16[256,384]{1,0:T(8,128)(2,1)} async-done(((bf16[1024,384]{1,0:T(8,128)(2,1)}), bf16[256,384]{1,0:T(8,128)(2,1)}) %reduce-scatter.14.cloned.1.call-update) | async-done | bytes 196624 | tf_op jit(solution)/shard_map/reduce_scatter | solution.py:43
  143.5 8.3 all-reduce.3
  154.6 48.7 %all-gather.11.cloned.1.call-done = bf16[1024,1152]{1,0:T(8,128)(2,1)} async-done(((bf16[256,1152]{1,0:T(8,128)(2,1)}), bf16[1024,1152]{1,0:T(8,128)(2,1)}) %all-gather.11.cloned.1.call-update) | async-done | bytes 2359312 | tf_op jit(solution)/shard_map/all_gather | solution.py:22
  206.9 17.9 %all_gather.40 = bf16[1024,384]{1,0:T(8,128)(2,1)S(1)} all-gather(bf16[256,384]{1,0:T(8,128)(2,1)S(1)} %multiply_convert_fusion.7), channel_id=1, replica_groups=mesh['dp'=4,'row'=2,'col'=4] {'col'}, dimensions={0}, use_global_device_ids=true | all-gather | bytes 983040 | tf_op jit(solution)/shard_map/all_gather | solution.py:22
  240.5 8.1 scatter_custom_fusion
  251.6 13.1 gather_fusion.3
  264.6 8.8 fusion.104
  285.8 13.0 gather_fusion
  298.8 14.6 %fusion.102 = f32[16,192,1024]{2,1,0:T(8,128)} fusion(bf16[16,192,384]{2,1,0:T(8,128)(2,1)} %bitcast.211, bf16[16,384,1024]{2,1,0:T(8,128)(2,1)} %constant_dynamic-update-slice_fusion.3), kind=kOutput, calls=%fused_computation.260 | convolution fusion | flops 2415919104 | bytes 27525120 | tf_op jit(solution)/shard_map/ecd,edf->ecf/dot_general | solution.py:276
  317.2 56.7 %reduce-scatter.24.cloned.1.call-done = f32[1536,512]{1,0:T(8,128)} async-done(((f32[3072,512]{1,0:T(8,128)}), f32[1536,512]{1,0:T(8,128)}) %reduce-scatter.24.cloned.1.call-update) | async-done | bytes 3145744 | tf_op jit(solution)/shard_map/reduce_scatter | solution.py:34
  373.9 147.5 %reduce-scatter.18.cloned.1.call-done = f32[1536,1024]{1,0:T(8,128)} async-done(((f32[3072,1024]{1,0:T(8,128)}), f32[1536,1024]{1,0:T(8,128)}) %reduce-scatter.18.cloned.1.call-update) | async-done | bytes 6291472 | tf_op jit(solution)/shard_map/reduce_scatter | solution.py:34
  534.4 10.4 all-gather.7.cloned.1.call-done
  547.6 43.7 %all-gather.9.cloned.1.call-done = bf16[3072,512]{1,0:T(8,128)(2,1)} async-done(((bf16[1536,512]{1,0:T(8,128)(2,1)}), bf16[3072,512]{1,0:T(8,128)(2,1)}) %all-gather.9.cloned.1.call-update) | async-done | bytes 3145744 | tf_op jit(solution)/shard_map/all_gather | solution.py:28
  610.9 62.7 %all-gather.15.cloned.1.call-done = bf16[3072,1024]{1,0:T(8,128)(2,1)} async-done(((bf16[1536,1024]{1,0:T(8,128)(2,1)}), bf16[3072,1024]{1,0:T(8,128)(2,1)}) %all-gather.15.cloned.1.call-update) | async-done | bytes 6291472 | tf_op jit(solution)/shard_map/all_gather | solution.py:28
  673.6 12.7 fusion.105
  700.1 8.2 all-gather.13.cloned.1.call-done
  712.7 46.1 %reduce-scatter.20.cloned.1.call-done = bf16[256,1152]{1,0:T(8,128)(2,1)} async-done(((bf16[1024,1152]{1,0:T(8,128)(2,1)}), bf16[256,1152]{1,0:T(8,128)(2,1)}) %reduce-scatter.20.cloned.1.call-update) | async-done | bytes 589840 | tf_op jit(solution)/shard_map/reduce_scatter | solution.py:43
  764.4 9.9 psum.122
  774.4 30.6 %psum.123 = f32[16]{0:T(128)S(1)} all-reduce(f32[16]{0:T(128)S(1)} %get-tuple-element.320), channel_id=1, replica_groups=mesh['dp'=4,'row'=2,'col'=4] {'dp','col'}, use_global_device_ids=true, to_apply=%region_34.35 | all-reduce | flops 16 | bytes 128 | tf_op jit(solution)/shard_map/psum | solution.py:52
  814.7 17.4 %all_gather.46 = bf16[1024,384]{1,0:T(8,128)(2,1)S(1)} all-gather(bf16[256,384]{1,0:T(8,128)(2,1)S(1)} %fusion.94), channel_id=1, replica_groups=mesh['dp'=4,'row'=2,'col'=4] {'col'}, dimensions={0}, use_global_device_ids=true | all-gather | bytes 983040 | tf_op jit(solution)/shard_map/all_gather | solution.py:22
  834.6 16.0 %reduce-scatter.28.cloned.1.call-done = f32[512,192]{0,1:T(8,128)} async-done(((f32[1024,192]{0,1:T(8,128)}), f32[512,192]{0,1:T(8,128)}) %reduce-scatter.28.cloned.1.call-update) | async-done | bytes 393232 | tf_op jit(solution)/shard_map/reduce_scatter | solution.py:34
  852.6 36.3 %while.29 = (s32[]{:T(128)}, f32[512,3,64]{0,2,1:T(8,128)S(1)}, f32[2,512,384]{2,1,0:T(8,128)}, s32[2]{0:T(128)S(1)}, s32[]{:T(128)}, /*index=5*/bf16[1024,192]{...) while((s32[]{:T(128)}, f32[512,3,64]{0,2,1:T(8,128)S(1)}, ...), condition=%wide.region_41.42_spmd.clone, body=%wide.region_40.41_spmd.clone.sunk | while | flops 2021728768 | bytes 44283788 | solution.py:442
  889.0 26.2 %reduce-scatter.30.cloned.1.call-done = f32[512,384]{1,0:T(8,128)} async-done(((f32[1024,384]{1,0:T(8,128)}), f32[512,384]{1,0:T(8,128)}) %reduce-scatter.30.cloned.1.call-update) | async-done | bytes 786448 | tf_op jit(solution)/shard_map/reduce_scatter | solution.py:34
  924.1 17.8 %all-gather.17.cloned.1.call-done = bf16[1024,576]{0,1:T(8,128)(2,1)} async-done(((bf16[512,576]{0,1:T(8,128)(2,1)}), bf16[1024,576]{0,1:T(8,128)(2,1)}) %all-gather.17.cloned.1.call-update) | async-done | bytes 1179664 | tf_op jit(solution)/shard_map/all_gather | solution.py:28
  945.1 7.9 convolution_convert_fusion.1
  953.0 11.1 convolution_convert_fusion
  972.2 63.0 %all-reduce.2 = (f32[384]{0:T(512)}, f32[384]{0:T(512)}, f32[384,16]{0,1:T(8,128)}, f32[16]{0:T(128)S(1)}) all-reduce(f32[384]{0:T(512)S(1)} %get-tuple-element.316, f32[384]{0:T(512)S(1)} %copy-done.78, f32[384,16]{0,1:T(8,128)S(1)} %fusion.57, f32[16]{0:T(128)S(1)} %copy-done.77), channel_id=1, replica_groups=mesh['dp'=4,'row'=2,'col'=4] {'dp','col'}, use_global_device_ids=true, to_apply=%region_47.48 | all-reduce | flops 6928 | bytes 55424 | tf_op jit(solution)/shard_map/psum | solution.py:52
  1043.5 279.4 %all-reduce.7.cloned.1.call-done = (bf16[384,576]{0,1:T(8,128)(2,1)}, bf16[192,384]{1,0:T(8,128)(2,1)}, bf16[384,1024]{1,0:T(8,128)(2,1)}, bf16[512,384]{1,0:T(8...) async-done(((bf16[384,576]{0,1:T(8,128)(2,1)}, bf16[192,384]{1,0:T(8,128)(2,1)}, bf16[384,1024]{1,0:T(8,128)(2,1)}, bf16[512,384]{1,0:T(8,128)(2,1)}, ...) | async-done | bytes 20643856 | tf_op jit(solution)/shard_map/psum | solution.py:489
  1323.0 14.1 %fusion.97 = (f32[16,384,512]{2,1,0:T(8,128)}, f32[16,384,512]{2,1,0:T(8,128)}) fusion(bf16[16,384,1024]{2,1,0:T(8,128)(2,1)} %get-tuple-element.400), kind=kLoop, calls=%fused_computation.255 | loop fusion | bytes 50331648 | tf_op jit(solution)/shard_map/slice | solution.py:510
  (410 shorter events, 245.1 us)
Async XLA Ops:
  7.2 66.4 %reduce-scatter.12.cloned.1.call-start = ((), (), s32[]{:S(2)}) async-start(), calls=%async_computation.11 | async-start | bytes 3538944 | tf_op jit(solution)/shard_map/reduce_scatter | solution.py:34
  39.1 101.9 %reduce-scatter.14.cloned.1.call-start = ((), (), s32[]{:S(2)}) async-start(), calls=%async_computation.12 | async-start | bytes 983040 | tf_op jit(solution)/shard_map/reduce_scatter | solution.py:43
  117.7 85.6 %all-gather.11.cloned.1.call-start = ((), (), s32[]{:S(2)}) async-start(), calls=%async_computation.18 | async-start | bytes 2949120 | tf_op jit(solution)/shard_map/all_gather | solution.py:22
  117.8 88.8 %copy-start.22 = (f32[256,384]{1,0:T(8,128)}, f32[256,384]{1,0:T(8,128)S(1)}, u32[]{:S(2)}) copy-start(f32[256,384]{1,0:T(8,128)S(1)} %convert_element_type.193) | copy-start | bytes 1179652
  154.6 158.9 %reduce-scatter.22.cloned.1.call-start = ((), (), s32[]{:S(2)}) async-start(), calls=%async_computation.19 | async-start | bytes 3145728 | tf_op jit(solution)/shard_map/reduce_scatter | solution.py:34
  206.6 106.9 %reduce-scatter.16.cloned.1.call-start = ((), (), s32[]{:S(2)}) async-start(), calls=%async_computation.13 | async-start | bytes 6291456 | tf_op jit(solution)/shard_map/reduce_scatter | solution.py:34
  229.1 144.8 %reduce-scatter.24.cloned.1.call-start = ((), (), s32[]{:S(2)}) async-start(), calls=%async_computation.21 | async-start | bytes 9437184 | tf_op jit(solution)/shard_map/reduce_scatter | solution.py:34
  273.5 247.9 %reduce-scatter.18.cloned.1.call-start = ((), (), s32[]{:S(2)}) async-start(), calls=%async_computation.15 | async-start | bytes 18874368 | tf_op jit(solution)/shard_map/reduce_scatter | solution.py:34
  313.4 231.4 %all-gather.7.cloned.1.call-start = ((), (), s32[]{:S(2)}) async-start(), calls=%async_computation.14 | async-start | bytes 1572864 | tf_op jit(solution)/shard_map/all_gather | solution.py:28
  317.1 274.2 %all-gather.9.cloned.1.call-start = ((), (), s32[]{:S(2)}) async-start(), calls=%async_computation.16 | async-start | bytes 4718592 | tf_op jit(solution)/shard_map/all_gather | solution.py:28
  527.3 146.4 %all-gather.15.cloned.1.call-start = ((), (), s32[]{:S(2)}) async-start(), calls=%async_computation.22 | async-start | bytes 9437184 | tf_op jit(solution)/shard_map/all_gather | solution.py:28
  530.8 177.5 %all-gather.13.cloned.1.call-start = ((), (), s32[]{:S(2)}) async-start(), calls=%async_computation.20 | async-start | bytes 3145728 | tf_op jit(solution)/shard_map/all_gather | solution.py:28
  533.1 225.7 %reduce-scatter.20.cloned.1.call-start = ((), (), s32[]{:S(2)}) async-start(), calls=%async_computation.17 | async-start | bytes 2949120 | tf_op jit(solution)/shard_map/reduce_scatter | solution.py:43
  610.8 195.5 %reduce-scatter.26.cloned.1.call-start = ((), (), s32[]{:S(2)}) async-start(), calls=%async_computation.23 | async-start | bytes 983040 | tf_op jit(solution)/shard_map/reduce_scatter | solution.py:43
  712.5 93.1 %copy-start.45 = (f32[256,16]{0,1:T(8,128)S(1)}, f32[256,16]{0,1:T(8,128)}, u32[]{:S(2)}) copy-start(f32[256,16]{0,1:T(8,128)} %copy-done.44) | copy-start | bytes 49156
  712.5 93.1 %copy-start.52 = (f32[256]{0:T(256)S(1)}, f32[256]{0:T(256)}, u32[]{:S(2)}) copy-start(f32[256]{0:T(256)} %copy-done.51) | copy-start | bytes 3076
  712.5 93.1 %copy-start.71 = (f32[256]{0:T(256)S(1)}, f32[256]{0:T(256)}, u32[]{:S(2)}) copy-start(f32[256]{0:T(256)} %copy-done.70) | copy-start | bytes 3076
  712.5 93.1 %copy-start.76 = (f32[256]{0:T(256)S(1)}, f32[256]{0:T(256)}, u32[]{:S(2)}) copy-start(f32[256]{0:T(256)} %copy-done.75) | copy-start | bytes 3076
  712.6 93.8 %copy-start.11 = (bf16[256,384]{1,0:T(8,128)(2,1)S(1)}, bf16[256,384]{1,0:T(8,128)(2,1)}, u32[]{:S(2)}) copy-start(bf16[256,384]{1,0:T(8,128)(2,1)} %param.19) | copy-start | bytes 589828
  712.6 93.8 %copy-start.17 = (bf16[256,384]{1,0:T(8,128)(2,1)S(1)}, bf16[256,384]{1,0:T(8,128)(2,1)}, u32[]{:S(2)}) copy-start(bf16[256,384]{1,0:T(8,128)(2,1)} %reduce-scatter.14.cloned.1.call-done) | copy-start | bytes 589828
  712.6 93.8 %copy-start.55 = (f32[256,16]{0,1:T(8,128)S(1)}, f32[256,16]{0,1:T(8,128)}, u32[]{:S(2)}) copy-start(f32[256,16]{0,1:T(8,128)} %copy-done.54) | copy-start | bytes 49156
  712.6 93.8 %copy-start.61 = (f32[384]{0:T(512)S(1)}, f32[384]{0:T(512)}, u32[]{:S(2)}) copy-start(f32[384]{0:T(512)} %param.26) | copy-start | bytes 4612
  712.6 93.8 %copy-start.64 = (f32[384,16]{0,1:T(8,128)S(1)}, f32[384,16]{0,1:T(8,128)}, u32[]{:S(2)}) copy-start(f32[384,16]{0,1:T(8,128)} %param.27) | copy-start | bytes 73732
  712.6 101.1 %copy-start.28 = (bf16[256,384]{1,0:T(8,128)(2,1)S(1)}, bf16[256,384]{1,0:T(8,128)(2,1)}, u32[]{:S(2)}) copy-start(bf16[256,384]{1,0:T(8,128)(2,1)} %param.20) | copy-start | bytes 589828
  712.7 138.0 %reduce-scatter.28.cloned.1.call-start = ((), (), s32[]{:S(2)}) async-start(), calls=%async_computation.24 | async-start | bytes 1179648 | tf_op jit(solution)/shard_map/reduce_scatter | solution.py:34
  834.5 80.7 %reduce-scatter.30.cloned.1.call-start = ((), (), s32[]{:S(2)}) async-start(), calls=%async_computation.25 | async-start | bytes 2359296 | tf_op jit(solution)/shard_map/reduce_scatter | solution.py:34
  888.9 53.0 %all-gather.17.cloned.1.call-start = ((), (), s32[]{:S(2)}) async-start(), calls=%async_computation.26 | async-start | bytes 1769472 | tf_op jit(solution)/shard_map/all_gather | solution.py:28
  919.0 52.0 %reduce-scatter.32.cloned.1.call-start = ((), (), s32[]{:S(2)}) async-start(), calls=%async_computation.27 | async-start | bytes 983040 | tf_op jit(solution)/shard_map/reduce_scatter | solution.py:43
  945.0 377.9 %all-reduce.7.cloned.1.call-start = ((), (), s32[]{:S(2)}) async-start(), calls=%async_computation.28 | async-start | bytes 41287680 | tf_op jit(solution)/shard_map/psum | solution.py:489
  969.4 71.9 %copy-start.29 = (bf16[256,384]{1,0:T(8,128)(2,1)S(1)}, bf16[256,384]{1,0:T(8,128)(2,1)}, u32[]{:S(2)}) copy-start(bf16[256,384]{1,0:T(8,128)(2,1)} %param.20) | copy-start | bytes 589828
  969.5 71.9 %copy-start.33 = (f32[256,384]{1,0:T(8,128)S(1)}, f32[256,384]{1,0:T(8,128)}, u32[]{:S(2)}) copy-start(f32[256,384]{1,0:T(8,128)} %get-tuple-element.313) | copy-start | bytes 1179652
  969.5 71.9 %copy-start.74 = (f32[256]{0:T(256)S(1)}, f32[256]{0:T(256)}, u32[]{:S(2)}) copy-start(f32[256]{0:T(256)} %copy-done.73) | copy-start | bytes 3076
  (77 other events, 1265.6 us)
Sparse Core Ops, SparseCore 0:
  39.3 34.2 reduce-scatter.11
  117.8 23.1 reduce-scatter.13
  154.7 48.5 all-gather.10
  206.8 30.6 reduce-scatter.21
  239.6 54.3 reduce-scatter.15
  296.7 77.1 reduce-scatter.23
  376.8 144.5 reduce-scatter.17
  523.5 21.2 all-gather.6
  546.4 44.8 all-gather.8
  593.3 80.3 all-gather.14
  675.2 33.0 all-gather.12
  711.1 47.6 reduce-scatter.19
  761.7 22.6 reduce-scatter.25
  834.6 15.9 reduce-scatter.27
  889.0 26.1 reduce-scatter.29
  919.1 22.7 all-gather.16
  945.1 23.1 reduce-scatter.31
  972.5 350.4 all-reduce.6
where the time goes:
time: 1360 us
  waiting for transfers between devices  819 us (60%)
  blocking collectives  203 us (15%)
  matrix products  130 us (10%)
  local copies, waits for them, and re-layouts  120 us (9%)
  other arithmetic  60.4 us (4%)
  between operations  17.8 us (1%)
    psum x1, waiting for transfers between devices, body(): lax.psum(attend_in_grad.astype(jnp.bfloat16), 'dp').astype(jnp.float32)  279 us
    reduce_scatter x7, waiting for transfers between devices, row_partials(): lax.psum_scatter(term_fn(jnp.int32(0), lax.axis_size('row') * row_count),...  279 us
    all_gather x5, waiting for transfers between devices, slot_gather(): lax.all_gather(for_sending(values), 'row', axis=0, tiled=True)  143 us
    psum x2, blocking collectives, token_stats(): return lax.psum(values, ('dp', 'col'))  93.6 us
    reduce_scatter x4, waiting for transfers between devices, col_partials(): lax.psum_scatter(term_fn(jnp.int32(0), lax.axis_size('col') * row_count)....  69.3 us
    all_gather x3, blocking collectives, token_gather(): return lax.all_gather(values, 'col', axis=0, tiled=True)  55.5 us
    all_gather x1, waiting for transfers between devices, token_gather(): return lax.all_gather(values, 'col', axis=0, tiled=True)  48.7 us
    psum x5, blocking collectives, feature_sums(): return lax.psum(values, 'row')  34 us
  transfers between devices with their start and end apart: 18, of which 14 were waited for; matrix products, arithmetic and copies ran while one was open for 15% of the time, Pallas kernels for 0%

commit v1 on v0

--- a/solution.py
+++ b/solution.py
@@ -1,6 +1,10 @@
+import functools
+
 import jax
 import jax.numpy as jnp
 from jax import lax
+from jax.experimental import pallas as pl
+from jax.experimental.pallas import tpu as pltpu
 from jax.sharding import PartitionSpec as P
 
 HD = 64
@@ -513,6 +517,654 @@
     )
 
 
+F32 = jnp.float32
+BF16 = jnp.bfloat16
+MASKED = -1e30
+
+
+def swap(value, axis, step=1):
+    size = lax.axis_size(axis)
+    return lax.ppermute(value, axis, [(i, i ^ step) for i in range(size)])
+
+
+def shifted(value, axis, step):
+    size = lax.axis_size(axis)
+    return lax.ppermute(value, axis, [(i, (i + step) % size) for i in range(size)])
+
+
+def in_order(parts, axis):
+    size, me = len(parts), lax.axis_index(axis)
+    whole = jnp.zeros((size,) + parts[0].shape, parts[0].dtype)
+    for step, part in enumerate(parts):
+        whole = lax.dynamic_update_index_in_dim(whole, part, (me - step) % size, 0)
+    return whole
+
+
+def col_parts(value):
+    return [value] + [shifted(value, "col", s) for s in range(1, lax.axis_size("col"))]
+
+
+def col_rows(value):
+    whole = in_order(col_parts(value), "col")
+    return whole.reshape((-1,) + value.shape[1:])
+
+
+def col_sum_rows(whole):
+    size, me = lax.axis_size("col"), lax.axis_index("col")
+    blocks = whole.reshape((size, whole.shape[0] // size) + whole.shape[1:])
+    total = lax.dynamic_index_in_dim(blocks, me, 0, False).astype(F32)
+    for step in range(1, size):
+        block = lax.dynamic_index_in_dim(blocks, (me + step) % size, 0, False)
+        total = total + shifted(block, "col", step).astype(F32)
+    return total
+
+
+def sum_by_swaps(value, axes):
+    for axis in axes:
+        step = 1
+        while step < lax.axis_size(axis):
+            value = value + swap(value, axis, step)
+            step *= 2
+    return value
+
+
+def pair_halves(whole):
+    core = lax.axis_index("dp") % 2
+    halves = whole.reshape((2, whole.shape[0] // 2) + whole.shape[1:])
+    mine = lax.dynamic_index_in_dim(halves, core, 0, False)
+    other = lax.dynamic_index_in_dim(halves, 1 - core, 0, False)
+    half = (mine.astype(F32) + swap(other, "dp", 1).astype(F32)).astype(BF16)
+    step = 2
+    while step < lax.axis_size("dp"):
+        half = (half.astype(F32) + swap(half, "dp", step).astype(F32)).astype(BF16)
+        step *= 2
+    return half, swap(half, "dp", 1)
+
+
+def dp_total(whole):
+    core = lax.axis_index("dp") % 2
+    half, rest = pair_halves(whole)
+    first = jnp.where(core == 0, half, rest)
+    second = jnp.where(core == 0, rest, half)
+    return jnp.concatenate([first, second], 0).astype(F32)
+
+
+def matmul(left, right, left_dim, right_dim):
+    return lax.dot_general(
+        left, right, (((left_dim,), (right_dim,)), ((), ())), preferred_element_type=F32
+    )
+
+
+def whole_block(shape):
+    return pl.BlockSpec(shape, lambda *unused: (0,) * len(shape))
+
+
+def visible_to(start_rows, row_base, row_count, key_count, prompt_len):
+    row_ids = row_base + lax.broadcasted_iota(jnp.int32, (row_count, key_count), 0)
+    key_ids = lax.broadcasted_iota(jnp.int32, (row_count, key_count), 1)
+    own_segment = (key_ids < prompt_len) | (key_ids >= start_rows)
+    return (key_ids <= row_ids) & own_segment
+
+
+def attend_kernel(
+    heads, block, prompt_len, scale,
+    left_ref, right_ref, weight_left_ref, weight_right_ref, out_weight_ref, cos_ref, sin_ref, start_ref,
+    qkv_ref, attended_ref, log_ref, partial_ref,
+):
+    raw = jnp.dot(left_ref[...], weight_left_ref[...], preferred_element_type=F32)
+    raw = raw + jnp.dot(right_ref[...], weight_right_ref[...], preferred_element_type=F32)
+    cosine, sine = cos_ref[...], sin_ref[...]
+    half = HD // 2
+    tokens = raw.shape[0]
+    partial = jnp.zeros(partial_ref.shape, F32)
+    for head in range(heads):
+        base = head * 3 * HD
+        for kind in range(3):
+            piece = raw[:, base + kind * HD : base + (kind + 1) * HD]
+            if kind < 2:
+                one, two = piece[:, :half], piece[:, half:]
+                piece = jnp.concatenate(
+                    [one * cosine - two * sine, one * sine + two * cosine], 1
+                )
+            qkv_ref[3 * head + kind] = piece.astype(BF16)
+        for low in range(0, tokens, block):
+            rows = pl.ds(low, block)
+            keys = low + block
+            scores = matmul(qkv_ref[3 * head, rows], qkv_ref[3 * head + 1, :keys], 1, 1) * scale
+            seen = visible_to(start_ref[rows], low, block, keys, prompt_len)
+            scores = jnp.where(seen, scores, MASKED)
+            top = jnp.max(scores, 1, keepdims=True)
+            weights = jnp.exp(scores - top)
+            total = jnp.sum(weights, 1, keepdims=True)
+            result = matmul(weights.astype(BF16), qkv_ref[3 * head + 2, :keys], 1, 0) / total
+            attended_ref[head, rows] = result
+            log_ref[head, rows] = top + jnp.log(total)
+        partial = partial + jnp.dot(
+            attended_ref[head].astype(BF16),
+            out_weight_ref[head * HD : (head + 1) * HD],
+            preferred_element_type=F32,
+        )
+    partial_ref[...] = partial.astype(BF16)
+
+
+def attend(left, right, weight_left, weight_right, out_weight, cosine, sine, start, block):
+    tokens, features = left.shape
+    heads = weight_left.shape[1] // (3 * HD)
+    pairs = sum(block * (low + block) for low in range(0, tokens, block)) * heads
+    return pl.pallas_call(
+        functools.partial(attend_kernel, heads, block, tokens // 2, HD ** (-0.5)),
+        out_shape=(
+            jax.ShapeDtypeStruct((3 * heads, tokens, HD), BF16),
+            jax.ShapeDtypeStruct((heads, tokens, HD), F32),
+            jax.ShapeDtypeStruct((heads, tokens, 1), F32),
+            jax.ShapeDtypeStruct((tokens, features), BF16),
+        ),
+        cost_estimate=pl.CostEstimate(
+            flops=4 * pairs * HD + 4 * tokens * features * 3 * HD * heads,
+            transcendentals=pairs,
+            bytes_accessed=8 * tokens * features,
+        ),
+        name="attend",
+    )(left, right, weight_left, weight_right, out_weight, cosine, sine, start)
+
+
+def attend_back_kernel(
+    heads, block, prompt_len, scale,
+    own_ref, peer_ref, qkv_ref, attended_ref, log_ref, cos_ref, sin_ref, start_ref, normed_ref, weight_ref,
+    one_ref, grad_ref, key_acc, value_acc, query_acc,
+):
+    cosine, sine = cos_ref[...], sin_ref[...]
+    half = HD // 2
+    tokens = own_ref.shape[0]
+    upper = (own_ref[...].astype(F32) + peer_ref[...].astype(F32)).astype(BF16)
+    pieces = []
+    for head in range(heads):
+        head_grad = upper[:, head * HD : (head + 1) * HD]
+        delta = jnp.sum(head_grad.astype(F32) * attended_ref[head], 1, keepdims=True)
+        key_acc[...] = jnp.zeros_like(key_acc)
+        value_acc[...] = jnp.zeros_like(value_acc)
+        for low in range(0, tokens, block):
+            rows = pl.ds(low, block)
+            keys = low + block
+            query = qkv_ref[3 * head, rows]
+            key = qkv_ref[3 * head + 1, :keys]
+            scores = matmul(query, key, 1, 1) * scale
+            seen = visible_to(start_ref[rows], low, block, keys, prompt_len)
+            weights = jnp.where(seen, jnp.exp(scores - log_ref[head, rows]), 0.0)
+            grad_rows = head_grad[low : low + block]
+            prob_dot = matmul(grad_rows, qkv_ref[3 * head + 2, :keys], 1, 1)
+            score_grad = (weights * (prob_dot - delta[low : low + block]) * scale).astype(BF16)
+            query_acc[rows] = matmul(score_grad, key, 1, 0)
+            key_acc[:keys] += matmul(score_grad, query, 0, 0)
+            value_acc[:keys] += matmul(weights.astype(BF16), grad_rows, 0, 0)
+        for piece in (query_acc[...], key_acc[...]):
+            one, two = piece[:, :half], piece[:, half:]
+            pieces += [one * cosine + two * sine, two * cosine - one * sine]
+        pieces.append(value_acc[...])
+    qkv_grad = jnp.concatenate(pieces, 1).astype(BF16)
+    one_ref[...] = matmul(qkv_grad, weight_ref[...], 1, 1)
+    grad_ref[...] = matmul(normed_ref[...], qkv_grad, 0, 0).astype(BF16)
+
+
+def attend_back(own, peer, qkv, attended, log_total, cosine, sine, start, normed, weight, block):
+    heads, tokens, unused = attended.shape
+    pairs = sum(block * (low + block) for low in range(0, tokens, block)) * heads
+    return pl.pallas_call(
+        functools.partial(attend_back_kernel, heads, block, tokens // 2, HD ** (-0.5)),
+        out_shape=(
+            jax.ShapeDtypeStruct(normed.shape, F32),
+            jax.ShapeDtypeStruct(weight.shape, BF16),
+        ),
+        scratch_shapes=[pltpu.VMEM((tokens, HD), F32)] * 3,
+        cost_estimate=pl.CostEstimate(
+            flops=10 * pairs * HD, transcendentals=pairs, bytes_accessed=16 * tokens * 3 * heads * HD
+        ),
+        name="attend_back",
+    )(own, peer, qkv, attended, log_total, cosine, sine, start, normed, weight)
+
+
+def picks(rank_ref, capacity):
+    rank = rank_ref[0]
+    return lax.broadcasted_iota(jnp.int32, (capacity, rank.shape[1]), 0) == rank
+
+
+def ones_where(mask):
+    return jnp.where(mask, 1.0, 0.0).astype(BF16)
+
+
+def back_hidden_kernel(rank_ref, cot_ref, down_ref, grad_ref, rows_ref):
+    chosen = ones_where(picks(rank_ref, rows_ref.shape[1]))
+    rows = jnp.dot(chosen, cot_ref[...], preferred_element_type=F32).astype(BF16)
+    rows_ref[0] = rows
+    grad_ref[0] = matmul(rows, down_ref[0], 1, 1).astype(BF16)
+
+
+def back_hidden(rank, cot_rows, down, first, count, capacity):
+    tokens, features = cot_rows.shape
+    hidden = down.shape[1]
+    return pl.pallas_call(
+        back_hidden_kernel,
+        grid=(count,),
+        in_specs=[
+            pl.BlockSpec((1, 1, tokens), lambda i: (first + i, 0, 0)),
+            whole_block((tokens, features)),
+            pl.BlockSpec((1, hidden, features), lambda i: (first + i, 0, 0)),
+        ],
+        out_specs=(
+            pl.BlockSpec((1, capacity, hidden), lambda i: (i, 0, 0)),
+            pl.BlockSpec((1, capacity, features), lambda i: (i, 0, 0)),
+        ),
+        out_shape=(
+            jax.ShapeDtypeStruct((count, capacity, hidden), BF16),
+            jax.ShapeDtypeStruct((count, capacity, features), BF16),
+        ),
+        cost_estimate=pl.CostEstimate(
+            flops=2 * count * capacity * features * (tokens + hidden),
+            transcendentals=0,
+            bytes_accessed=2 * count * (hidden * features + capacity * (hidden + features)),
+        ),
+        name="back_hidden",
+    )(rank, cot_rows, down)
+
+
+def open_experts_kernel(rank_ref, token_ref, gate_ref, up_ref, pre_ref, rows_ref):
+    hidden = gate_ref.shape[2]
+    chosen = ones_where(picks(rank_ref, rows_ref.shape[1]))
+    rows = jnp.dot(chosen, token_ref[...], preferred_element_type=F32).astype(BF16)
+    rows_ref[0] = rows
+    pre_ref[0, :, :hidden] = jnp.dot(rows, gate_ref[0], preferred_element_type=F32).astype(BF16)
+    pre_ref[0, :, hidden:] = jnp.dot(rows, up_ref[0], preferred_element_type=F32).astype(BF16)
+
+
+def open_experts(rank, token_rows, gate, up, first, count, capacity):
+    tokens, features = token_rows.shape
+    hidden = gate.shape[2]
+    return pl.pallas_call(
+        open_experts_kernel,
+        grid=(count,),
+        in_specs=[
+            pl.BlockSpec((1, 1, tokens), lambda i: (first + i, 0, 0)),
+            whole_block((tokens, features)),
+            pl.BlockSpec((1, features, hidden), lambda i: (first + i, 0, 0)),
+            pl.BlockSpec((1, features, hidden), lambda i: (first + i, 0, 0)),
+        ],
+        out_specs=(
+            pl.BlockSpec((1, capacity, 2 * hidden), lambda i: (i, 0, 0)),
+            pl.BlockSpec((1, capacity, features), lambda i: (i, 0, 0)),
+        ),
+        out_shape=(
+            jax.ShapeDtypeStruct((count, capacity, 2 * hidden), BF16),
+            jax.ShapeDtypeStruct((count, capacity, features), BF16),
+        ),
+        cost_estimate=pl.CostEstimate(
+            flops=2 * count * capacity * features * (tokens + 2 * hidden),
+            transcendentals=0,
+            bytes_accessed=2 * count * (2 * hidden * features + capacity * (2 * hidden + features)),
+        ),
+        name="open_experts",
+    )(rank, token_rows, gate, up)
+
+
+def gated(pre_gate, pre_up, hidden_grad):
+    sigma = 1.0 / (1.0 + jnp.exp(-pre_gate))
+    silu = pre_gate * sigma
+    grad_gate = hidden_grad * pre_up * sigma * (1.0 + pre_gate * (1.0 - sigma))
+    return silu * pre_up, grad_gate, hidden_grad * silu
+
+
+def experts_kernel(
+    rank_ref, prob_ref, pre_own_ref, pre_peer_ref, back_own_ref, back_peer_ref, rows_ref, cot_ref,
+    gate_ref, up_ref, down_ref, out_in_ref, dx_in_ref,
+    both_grad_ref, down_grad_ref, share_ref, out_ref, dx_ref,
+):
+    capacity, hidden = back_own_ref.shape[1:]
+
+    @pl.when(pl.program_id(0) == 0)
+    def start():
+        out_ref[...] = out_in_ref[...]
+        dx_ref[...] = dx_in_ref[...]
+
+    mask = picks(rank_ref, capacity)
+    chosen = ones_where(mask)
+    gate_val = jnp.sum(jnp.where(mask, prob_ref[0], 0.0), 1, keepdims=True)
+    pre = pre_own_ref[0].astype(F32) + pre_peer_ref[0].astype(F32)
+    raw_back = back_own_ref[0].astype(F32) + back_peer_ref[0].astype(F32)
+    result, grad_gate, grad_up = gated(pre[:, :hidden], pre[:, hidden:], gate_val * raw_back)
+    result = result.astype(BF16).astype(F32)
+    share = jnp.sum(result * raw_back, 1, keepdims=True)
+    share_ref[0] = jnp.sum(jnp.where(mask, share, 0.0), 0, keepdims=True)
+    scaled = (gate_val * result).astype(BF16)
+    grad_gate = grad_gate.astype(BF16)
+    grad_up = grad_up.astype(BF16)
+    rows = rows_ref[0]
+    out_rows = jnp.dot(scaled, down_ref[0], preferred_element_type=F32).astype(BF16)
+    out_ref[...] += matmul(chosen, out_rows, 0, 0)
+    dx_rows = (matmul(grad_gate, gate_ref[0], 1, 1) + matmul(grad_up, up_ref[0], 1, 1)).astype(BF16)
+    dx_ref[...] += matmul(chosen, dx_rows, 0, 0)
+    both_grad_ref[0, :, :hidden] = matmul(rows, grad_gate, 0, 0).astype(BF16)
+    both_grad_ref[0, :, hidden:] = matmul(rows, grad_up, 0, 0).astype(BF16)
+    down_grad_ref[0] = matmul(scaled, cot_ref[0], 0, 0).astype(BF16)
+
+
+def run_experts(
+    rank, probs, pre_own, pre_peer, back_own, back_peer, rows, cot_rows, gate, up, down, out_sum, dx_sum, first
+):
+    count, capacity, hidden = back_own.shape
+    tokens, features = out_sum.shape
+
+    def at(shape, base):
+        return pl.BlockSpec((1,) + shape, lambda i: (base + i, 0, 0))
+
+    return pl.pallas_call(
+        experts_kernel,
+        grid=(count,),
+        in_specs=[
+            at((1, tokens), first),
+            at((1, tokens), first),
+            at((capacity, 2 * hidden), 0),
+            at((capacity, 2 * hidden), 0),
+            at((capacity, hidden), 0),
+            at((capacity, hidden), 0),
+            at((capacity, features), 0),
+            at((capacity, features), 0),
+            at((features, hidden), first),
+            at((features, hidden), first),
+            at((hidden, features), first),
+            whole_block((tokens, features)),
+            whole_block((tokens, features)),
+        ],
+        out_specs=(
+            at((features, 2 * hidden), 0),
+            at((hidden, features), 0),
+            at((1, tokens), 0),
+            whole_block((tokens, features)),
+            whole_block((tokens, features)),
+        ),
+        out_shape=(
+            jax.ShapeDtypeStruct((count, features, 2 * hidden), BF16),
+            jax.ShapeDtypeStruct((count, hidden, features), BF16),
+            jax.ShapeDtypeStruct((count, 1, tokens), F32),
+            jax.ShapeDtypeStruct((tokens, features), F32),
+            jax.ShapeDtypeStruct((tokens, features), F32),
+        ),
+        cost_estimate=pl.CostEstimate(
+            flops=2 * count * capacity * features * (2 * tokens + 6 * hidden),
+            transcendentals=count * capacity * hidden,
+            bytes_accessed=2 * count * (6 * hidden * features + 6 * capacity * hidden),
+        ),
+        name="run_experts",
+    )(
+        rank, probs, pre_own, pre_peer, back_own, back_peer, rows, cot_rows, gate, up, down, out_sum, dx_sum
+    )
+
+
+def spread_kernel(core_ref, both_half_ref, both_rest_ref, down_half_ref, down_rest_ref, *refs):
+    gate_ref, up_ref, down_ref = refs[-3:]
+    hidden = gate_ref.shape[2]
+    own = pl.program_id(0) < pl.num_programs(0) // 2
+
+    @pl.when(own)
+    def first():
+        both = both_half_ref[0].astype(F32)
+        gate_ref[0] = both[:, :hidden]
+        up_ref[0] = both[:, hidden:]
+        down_ref[0] = down_half_ref[0].astype(F32)
+
+    @pl.when(jnp.logical_not(own))
+    def second():
+        both = both_rest_ref[0].astype(F32)
+        gate_ref[0] = both[:, :hidden]
+        up_ref[0] = both[:, hidden:]
+        down_ref[0] = down_rest_ref[0].astype(F32)
+
+
+def spread(core, both_half, both_rest, down_half, down_rest, earlier, first, experts):
+    half = both_half.shape[0]
+    features, hidden = both_half.shape[1], both_half.shape[2] // 2
+
+    def own_index(i, core):
+        return (jnp.minimum(i, half - 1), 0, 0)
+
+    def rest_index(i, core):
+        return (jnp.maximum(i - half, 0), 0, 0)
+
+    def out_index(i, core):
+        place = jnp.where(i < half, core[0] * half + i, (1 - core[0]) * half + i - half)
+        return (first + place, 0, 0)
+
+    shapes = ((features, hidden), (features, hidden), (hidden, features))
+    return pl.pallas_call(
+        spread_kernel,
+        grid_spec=pltpu.PrefetchScalarGridSpec(
+            num_scalar_prefetch=1,
+            grid=(2 * half,),
+            in_specs=[
+                pl.BlockSpec((1, features, 2 * hidden), own_index),
+                pl.BlockSpec((1, features, 2 * hidden), rest_index),
+                pl.BlockSpec((1, hidden, features), own_index),
+                pl.BlockSpec((1, hidden, features), rest_index),
+            ]
+            + [pl.BlockSpec(memory_space=pl.ANY)] * len(earlier),
+            out_specs=tuple(pl.BlockSpec((1,) + shape, out_index) for shape in shapes),
+        ),
+        out_shape=tuple(jax.ShapeDtypeStruct((experts,) + shape, F32) for shape in shapes),
+        input_output_aliases={5 + i: i for i in range(len(earlier))},
+        cost_estimate=pl.CostEstimate(
+            flops=0, transcendentals=0, bytes_accessed=36 * half * features * hidden
+        ),
+        name="spread",
+    )(core, both_half, both_rest, down_half, down_rest, *earlier)
+
+
+def paired_body(
+    inputs,
+    cotangent,
+    routes,
+    cont_lengths,
+    first_gain,
+    attend_in,
+    attend_out,
+    second_gain,
+    router_weight,
+    shared_gate,
+    shared_up,
+    shared_down,
+    expert_gate,
+    expert_up,
+    expert_down,
+):
+    col_size = lax.axis_size("col")
+    data_size = lax.axis_size("dp")
+    col_index = lax.axis_index("col")
+    tok_rest, feat_dev = inputs.shape
+    feat_full = feat_dev * 2
+    tok_block = tok_rest * col_size
+    experts = expert_gate.shape[0]
+    shared_dev = shared_gate.shape[1]
+    capacity = tok_block * 3 // experts
+    tokens_all = float(data_size * tok_block)
+    prompt_len = tok_block // 2
+    block = 256
+    chunk = 4
+    core = (lax.axis_index("dp") % 2).reshape(1)
+
+    own_parts = col_parts(inputs)
+    peer_parts = [swap(part, "row") for part in own_parts]
+    own_all = in_order(own_parts, "col").reshape(tok_block, feat_dev).astype(F32)
+    peer_all = in_order(peer_parts, "col").reshape(tok_block, feat_dev).astype(F32)
+    peer_weight = swap(attend_in, "row")
+    peer_gain = swap(first_gain, "row")
+    cot_all = col_rows(cotangent)
+
+    squares_one = jnp.sum(own_all * own_all, 1) + jnp.sum(peer_all * peer_all, 1)
+    scale_all = lax.rsqrt(squares_one / feat_full + EPSILON)[:, None]
+    unit_all = own_all * scale_all
+    normed_own = (unit_all * first_gain).astype(BF16)
+    normed_peer = (peer_all * scale_all * peer_gain).astype(BF16)
+
+    offsets = jnp.arange(tok_block, dtype=jnp.int32)
+    after = offsets - prompt_len
+    ends = jnp.cumsum(cont_lengths[0])
+    begin = jnp.max(jnp.where(ends[None, :] <= after[:, None], ends[None, :], 0), 1)
+    start = jnp.where(after < 0, 0, prompt_len + begin)
+    position = jnp.where(after < 0, offsets, prompt_len + after - begin)
+    angles = angle_table(position)
+    cosine, sine = jnp.cos(angles), jnp.sin(angles)
+    start = start[:, None]
+
+    expert_ids = jnp.arange(experts, dtype=jnp.int32)
+    named = (routes[:, 0][None, :] == expert_ids[:, None]) | (
+        routes[:, 1][None, :] == expert_ids[:, None]
+    )
+    before = (offsets[:, None] < offsets[None, :]).astype(BF16)
+    rank = jnp.dot(named.astype(BF16), before, preferred_element_type=F32).astype(jnp.int32)
+    rank = jnp.where(named, rank, -1)[:, None, :]
+    count_own = jnp.sum(named.astype(F32), 1)
+
+    back_own, cot_rows, back_peer = [], [], []
+    for first in range(0, experts, chunk):
+        back, rows = back_hidden(rank, cot_all, expert_down, first, chunk, capacity)
+        back_own.append(back)
+        cot_rows.append(rows)
+        back_peer.append(swap(back, "row"))
+    shared_back_own = matmul(cot_all, shared_down, 1, 1).astype(BF16)
+    shared_back_peer = swap(shared_back_own, "row")
+
+    qkv, attended, log_total, out_partial = attend(
+        normed_own, normed_peer, attend_in, peer_weight, attend_out, cosine, sine, start, block
+    )
+    inputs_f = inputs.astype(F32)
+    mixed_one = inputs_f + col_sum_rows(out_partial)
+    gained = mixed_one * second_gain
+    partial_stats = jnp.concatenate(
+        [
+            jnp.sum(mixed_one * mixed_one, 1, keepdims=True),
+            jnp.dot(gained, router_weight, precision=HIGHEST),
+        ],
+        1,
+    )
+    stats = partial_stats + swap(partial_stats, "row")
+    scale_two = lax.rsqrt(stats[:, :1] / feat_full + EPSILON)
+    router_probs = jax.nn.softmax(stats[:, 1:] * scale_two, -1)
+    unit_two = mixed_one * scale_two
+    normed_two = (unit_two * second_gain).astype(BF16)
+    normed_all = col_rows(normed_two)
+    probs_all = col_rows(router_probs)
+    probs_rows = probs_all.T[:, None, :]
+    count_total, prob_total = sum_by_swaps(jnp.stack([count_own, jnp.sum(probs_all, 0)]), ("dp",))
+    balance_loss = experts * jnp.sum(count_total / (2.0 * tokens_all) * prob_total / tokens_all)
+
+    shared_pre_own = jnp.concatenate(
+        [matmul(normed_all, shared_gate, 1, 0), matmul(normed_all, shared_up, 1, 0)], 1
+    ).astype(BF16)
+    shared_pre_peer = swap(shared_pre_own, "row")
+    pre_own, token_rows, pre_peer = [], [], []
+    for first in range(0, experts, chunk):
+        pre, rows = open_experts(rank, normed_all, expert_gate, expert_up, first, chunk, capacity)
+        pre_own.append(pre)
+        token_rows.append(rows)
+        pre_peer.append(swap(pre, "row"))
+
+    shared_pre = shared_pre_own.astype(F32) + shared_pre_peer.astype(F32)
+    shared_back = shared_back_own.astype(F32) + shared_back_peer.astype(F32)
+    shared_hidden, shared_gate_pgrad, shared_up_pgrad = (
+        value.astype(BF16)
+        for value in gated(shared_pre[:, :shared_dev], shared_pre[:, shared_dev:], shared_back)
+    )
+    out_sum = matmul(shared_hidden, shared_down, 1, 0)
+    dx_sum = matmul(shared_gate_pgrad, shared_gate, 1, 1) + matmul(shared_up_pgrad, shared_up, 1, 1)
+    shared_gate_grad = dp_total(matmul(normed_all, shared_gate_pgrad, 0, 0).astype(BF16))
+    shared_up_grad = dp_total(matmul(normed_all, shared_up_pgrad, 0, 0).astype(BF16))
+    shared_down_grad = dp_total(matmul(shared_hidden, cot_all, 0, 0).astype(BF16))
+
+    shares, expert_grads = [], ()
+    for index, first in enumerate(range(0, experts, chunk)):
+        both_grad, down_grad, share, out_sum, dx_sum = run_experts(
+            rank, probs_rows, pre_own[index], pre_peer[index], back_own[index], back_peer[index],
+            token_rows[index], cot_rows[index], expert_gate, expert_up, expert_down, out_sum, dx_sum, first,
+        )
+        shares.append(share[:, 0])
+        both_half, both_rest = pair_halves(both_grad)
+        down_half, down_rest = pair_halves(down_grad)
+        expert_grads = spread(
+            core, both_half, both_rest, down_half, down_rest, expert_grads, first, experts
+        )
+
+    layer_out = (mixed_one + col_sum_rows(out_sum.astype(BF16))).astype(BF16)
+    cot_f = cotangent.astype(F32)
+    gate_grad = col_sum_rows(jnp.concatenate(shares, 0).T)
+    prob_grad = gate_grad + experts * count_total / (2.0 * tokens_all * tokens_all)
+    logit_grad = router_probs * (prob_grad - jnp.sum(router_probs * prob_grad, -1, keepdims=True))
+    router_grad = jnp.einsum("td,te->ed", unit_two * second_gain, logit_grad, precision=HIGHEST)
+
+    normed_grad = col_sum_rows(dx_sum.astype(BF16))
+    two_grad = normed_grad + jnp.einsum("te,de->td", logit_grad, router_weight, precision=HIGHEST)
+    gained_two = two_grad * second_gain
+    second_gain_grad = jnp.sum(two_grad * unit_two, 0)
+    inner_two = jnp.sum(gained_two * unit_two, 1, keepdims=True)
+    inner_two = (inner_two + swap(inner_two, "row")) / feat_full
+    mixed_grad = cot_f + scale_two * (gained_two - unit_two * inner_two)
+    mix_all = col_rows(mixed_grad.astype(BF16))
+    attn_own = matmul(mix_all, attend_out, 1, 1).astype(BF16)
+    attn_peer = swap(attn_own, "row")
+    heads = attended.shape[0]
+    attn_rows = attended.astype(BF16)
+    attend_out_grad = jnp.concatenate(
+        [matmul(attn_rows[head], mix_all, 0, 0) for head in range(heads)], 0
+    ).astype(BF16)
+    attend_out_grad = dp_total(attend_out_grad)
+    one_partial, attend_in_grad = attend_back(
+        attn_own, attn_peer, qkv, attended, log_total, cosine, sine, start, normed_own, attend_in, block
+    )
+    attend_in_grad = dp_total(attend_in_grad)
+    first_gain_grad = jnp.sum(one_partial * unit_all, 0)
+    one_grad = col_sum_rows(one_partial.astype(BF16))
+    own_rows = col_index * tok_rest
+    unit_one = rows_of(unit_all, own_rows, tok_rest)
+    scale_one = rows_of(scale_all, own_rows, tok_rest)
+    gained_one = one_grad * first_gain
+    inner_one = jnp.sum(gained_one * unit_one, 1, keepdims=True)
+    inner_one = (inner_one + swap(inner_one, "row")) / feat_full
+    input_grad = (mixed_grad + scale_one * (gained_one - unit_one * inner_one)).astype(BF16)
+    early = sum_by_swaps(jnp.concatenate([second_gain_grad[None], router_grad], 0), ("dp", "col"))
+    first_gain_grad = sum_by_swaps(first_gain_grad, ("dp", "col"))
+    return (
+        layer_out,
+        input_grad,
+        first_gain_grad,
+        attend_in_grad,
+        attend_out_grad,
+        early[0],
+        early[1:].T,
+        shared_gate_grad,
+        shared_up_grad,
+        shared_down_grad,
+        expert_grads[0],
+        expert_grads[1],
+        expert_grads[2],
+        balance_loss,
+    )
+
+
+def power_of_two(number):
+    return number & (number - 1) == 0
+
+
+def chosen_body(*shards):
+    inputs, cont_lengths = shards[0], shards[3]
+    tok_block = inputs.shape[0] * lax.axis_size("col")
+    paired = (
+        lax.axis_size("row") == 2
+        and lax.axis_size("dp") >= 2
+        and power_of_two(lax.axis_size("dp"))
+        and power_of_two(lax.axis_size("col"))
+        and cont_lengths.shape[0] == 1
+        and tok_block % 512 == 0
+        and tok_block <= 2048
+    )
+    return (paired_body if paired else body)(*shards)
+
+
 def solution(mesh):
     in_specs = (
         P(("dp", "col"), "row"),
@@ -547,4 +1199,4 @@
         P(None, "col", "row"),
         P(),
     )
-    return jax.shard_map(body, mesh=mesh, in_specs=in_specs, out_specs=out_specs, check_vma=False)
+    return jax.shard_map(chosen_body, mesh=mesh, in_specs=in_specs, out_specs=out_specs, check_vma=False)

time: 1360 us -> 837 us (0.62)
  waiting for transfers between devices: 819 us -> 457 us
  blocking collectives: 203 us -> 0 us
  Pallas kernels: 0 us -> 154 us
  matrix products: 130 us -> 15.1 us
  starting transfers between devices: 1.64 us -> 101 us
  local copies, waits for them, and re-layouts: 120 us -> 33.8 us
    ppermute x0 -> x99, waiting for transfers between devices: none -> 457 us  [the longest x69 383 us: swap(): return lax.ppermute(value, axis, [(i, i ^ step) for i in range(size)])]
    reduce_scatter x11 -> x0, waiting for transfers between devices: 348 us -> none  [the longest x7 279 us: row_partials(): lax.psum_scatter(term_fn(jnp.int32(0), lax.axis_size('row') * row_count),...]
    psum x1 -> x0, waiting for transfers between devices: 279 us -> none  [body(): lax.psum(attend_in_grad.astype(jnp.bfloat16), 'dp').astype(jnp.float32)]
    all_gather x6 -> x0, waiting for transfers between devices: 191 us -> none  [the longest x5 143 us: slot_gather(): lax.all_gather(for_sending(values), 'row', axis=0, tiled=True)]
    pallas_call x0 -> x18, Pallas kernels: none -> 154 us  [the longest x4 52.3 us: run_experts(): pl.pallas_call(experts_kernel, grid=(count,), in_specs=[at((1, tokens), f...]
    psum x7 -> x0, blocking collectives: 128 us -> none  [the longest x2 93.6 us: token_stats(): return lax.psum(values, ('dp', 'col'))]
    dot_general x35 -> x17, matrix products: 130 us -> 15.1 us  [the longest x13 12.5 us: matmul(): lax.dot_general(left, right, (((left_dim,), (right_dim,)), ((), ())), pre...]
    ppermute x0 -> x99, starting transfers between devices: none -> 101 us  [the longest x30 59.1 us: shifted(): lax.ppermute(value, axis, [(i, (i + step) % size) for i in range(size)])]
  transfers between devices with their start and end apart: 18 -> 99, of which waited for: 14 -> 43; matrix products, arithmetic and copies ran while one was open for 15% -> 13% of each run, Pallas kernels for 0% -> 16%
where the time goes in v1:
time: 837 us; the launch traced here: 832 us
  waiting for transfers between devices  457 us (55%)
  Pallas kernels  154 us (18%)
  starting transfers between devices  101 us (12%)
  other arithmetic  66.8 us (8%)
  local copies, waits for them, and re-layouts  33.8 us (4%)
  matrix products  15.1 us (2%)
    ppermute x69, waiting for transfers between devices, swap(): return lax.ppermute(value, axis, [(i, i ^ step) for i in range(size)])  383 us
    ppermute x30, waiting for transfers between devices, shifted(): lax.ppermute(value, axis, [(i, (i + step) % size) for i in range(size)])  74.6 us
    ppermute x30, starting transfers between devices, shifted(): lax.ppermute(value, axis, [(i, (i + step) % size) for i in range(size)])  59.1 us
    pallas_call x4, Pallas kernels, run_experts(): pl.pallas_call(experts_kernel, grid=(count,), in_specs=[at((1, tokens), f...  52.3 us
    ppermute x69, starting transfers between devices, swap(): return lax.ppermute(value, axis, [(i, i ^ step) for i in range(size)])  42.2 us
    pallas_call x4, Pallas kernels, spread(): pl.pallas_call(spread_kernel, grid_spec=pltpu.PrefetchScalarGridSpec(num_...  27.3 us
    pallas_call x4, Pallas kernels, open_experts(): pl.pallas_call(open_experts_kernel, grid=(count,), in_specs=[pl.BlockSpec...  22.9 us
    pallas_call x4, Pallas kernels, back_hidden(): pl.pallas_call(back_hidden_kernel, grid=(count,), in_specs=[pl.BlockSpec(...  19.4 us
  transfers between devices with their start and end apart: 99, of which 43 were waited for; matrix products, arithmetic and copies ran while one was open for 13% of the time, Pallas kernels for 16%

profile of v1, /device:TPU:0, one launch (start us, length us, event | category | flops | bytes accessed | tf_op | source)
XLA Modules:
  0.0 832.1 jit_solution(13794763972195551152)
XLA Ops:
  19.8 8.2 collective-permute-done.20
  35.1 11.8 %collective-permute-done.4 = bf16[256,384]{1,0:T(8,128)(2,1)S(1)} collective-permute-done((bf16[256,384]{1,0:T(8,128)(2,1)}, bf16[256,384]{1,0:T(8,128)(2,1)S(1)}, u32[]{:S(2)}, u32[]{:S(2)}) %collective-permute-start.4) | collective-permute-done | bytes 196640 | tf_op jit(solution)/shard_map/ppermute | solution.py:527
  61.8 14.7 %attend.1 = (bf16[9,1024,64]{2,1,0:T(8,128)(2,1)}, f32[3,1024,64]{2,1,0:T(8,128)}, f32[3,1024,1]{2,1,0:T(8,128)}, bf16[1024,384]{1,0:T(8,128)(2,1)}) custom-call(bf16[1024,384]{1,0:T(8,128)(2,1)} %get-tuple-element.174.left_ref.normed_ref, bf16[1024,384]{1,0:T(8,128)(2,1)} %get-tuple-element.173.right_ref, bf16[384,576]{1,0:T(8,128)(2,1)} %copy-done.26, ...), custom_call_target="tpu_custom_call" | custom-call | flops 1409286144 | bytes 3145728 | tf_op jit(solution)/shard_map/attend/pallas_call | solution.py:654
  77.7 12.8 %collective-permute-start.9 = (bf16[256,384]{1,0:T(8,128)(2,1)S(1)}, bf16[256,384]{1,0:T(8,128)(2,1)S(1)}, u32[]{:S(2)}, u32[]{:S(2)}) collective-permute-start(bf16[256,384]{1,0:T(8,128)(2,1)S(1)} %get-tuple-element.147), channel_id=1, source_target_pairs={{0,1},{1,2},{2,3},{3,0},{4,5},{5,6},{6,7},{7,4},{8,9},{9,10},{10,1... | collective-permute-start | bytes 589832 | tf_op jit(solution)/shard_map/ppermute | solution.py:532
  99.3 8.3 collective-permute-done.10
  187.4 5.7 open_experts.5
  193.1 5.8 open_experts.4
  212.5 59.3 %collective-permute-done.28.pre_peer_ref = bf16[4,192,1024]{2,1,0:T(8,128)(2,1)} collective-permute-done((bf16[4,192,1024]{2,1,0:T(8,128)(2,1)}, bf16[4,192,1024]{2,1,0:T(8,128)(2,1)}, u32[]{:S(2)}, u32[]{:S(2)}) %collective-permute-start.28) | collective-permute-done | bytes 1572896 | tf_op jit(solution)/shard_map/ppermute | solution.py:527
  272.3 12.7 %run_experts.4 = (bf16[4,384,1024]{2,1,0:T(8,128)(2,1)}, bf16[4,512,384]{2,1,0:T(8,128)(2,1)}, f32[4,1,1024]{2,1,0:T(1,128)}, f32[1024,384]{1,0:T(8,128)}, f32[1024,384]{1,0:T(8,128)}) custom-call(s32[16,1,1024]{2,1,0:T(1,128)} %broadcast_in_dim.143.rank_ref, f32[16,1,1024]{2,1,0:T(1,128)} %broadcast_in_dim.150.prob_ref, ...), custom_call_target="tpu_custom_call" | custom-call | flops 3019898880 | bytes 14155776 | tf_op jit(solution)/shard_map/run_experts/pallas_call | solution.py:858
  286.6 18.9 %collective-permute-done.26.pre_peer_ref = bf16[4,192,1024]{2,1,0:T(8,128)(2,1)} collective-permute-done((bf16[4,192,1024]{2,1,0:T(8,128)(2,1)}, bf16[4,192,1024]{2,1,0:T(8,128)(2,1)}, u32[]{:S(2)}, u32[]{:S(2)}) %collective-permute-start.26) | collective-permute-done | bytes 1572896 | tf_op jit(solution)/shard_map/ppermute | solution.py:527
  305.5 13.3 %run_experts.5 = (bf16[4,384,1024]{2,1,0:T(8,128)(2,1)}, bf16[4,512,384]{2,1,0:T(8,128)(2,1)}, f32[4,1,1024]{2,1,0:T(1,128)}, f32[1024,384]{1,0:T(8,128)}, f32[1024,384]{1,0:T(8,128)}) custom-call(s32[16,1,1024]{2,1,0:T(1,128)} %broadcast_in_dim.143.rank_ref, f32[16,1,1024]{2,1,0:T(1,128)} %broadcast_in_dim.150.prob_ref, ...), custom_call_target="tpu_custom_call" | custom-call | flops 3019898880 | bytes 14155776 | tf_op jit(solution)/shard_map/run_experts/pallas_call | solution.py:858
  329.3 55.9 %collective-permute-done.24.pre_peer_ref = bf16[4,192,1024]{2,1,0:T(8,128)(2,1)} collective-permute-done((bf16[4,192,1024]{2,1,0:T(8,128)(2,1)}, bf16[4,192,1024]{2,1,0:T(8,128)(2,1)}, u32[]{:S(2)}, u32[]{:S(2)}) %collective-permute-start.24) | collective-permute-done | bytes 1572896 | tf_op jit(solution)/shard_map/ppermute | solution.py:527
  385.3 13.1 %run_experts.6 = (bf16[4,384,1024]{2,1,0:T(8,128)(2,1)}, bf16[4,512,384]{2,1,0:T(8,128)(2,1)}, f32[4,1,1024]{2,1,0:T(1,128)}, f32[1024,384]{1,0:T(8,128)}, f32[1024,384]{1,0:T(8,128)}) custom-call(s32[16,1,1024]{2,1,0:T(1,128)} %broadcast_in_dim.143.rank_ref, f32[16,1,1024]{2,1,0:T(1,128)} %broadcast_in_dim.150.prob_ref, ...), custom_call_target="tpu_custom_call" | custom-call | flops 3019898880 | bytes 14155776 | tf_op jit(solution)/shard_map/run_experts/pallas_call | solution.py:858
  398.4 13.2 %run_experts.7 = (bf16[4,384,1024]{2,1,0:T(8,128)(2,1)}, bf16[4,512,384]{2,1,0:T(8,128)(2,1)}, f32[4,1,1024]{2,1,0:T(1,128)}, f32[1024,384]{1,0:T(8,128)}, f32[1024,384]{1,0:T(8,128)}) custom-call(s32[16,1,1024]{2,1,0:T(1,128)} %broadcast_in_dim.143.rank_ref, f32[16,1,1024]{2,1,0:T(1,128)} %broadcast_in_dim.150.prob_ref, ...), custom_call_target="tpu_custom_call" | custom-call | flops 3019898880 | bytes 14155776 | tf_op jit(solution)/shard_map/run_experts/pallas_call | solution.py:858
  437.0 10.5 %collective-permute-done.33 = bf16[256,384]{1,0:T(8,128)(2,1)S(1)} collective-permute-done((bf16[256,384]{1,0:T(8,128)(2,1)S(1)}, bf16[256,384]{1,0:T(8,128)(2,1)S(1)}, u32[]{:S(2)}, u32[]{:S(2)}) %collective-permute-start.33) | collective-permute-done | bytes 196640 | tf_op jit(solution)/shard_map/ppermute | solution.py:532
  448.1 6.0 collective-permute-done.36
  480.2 7.6 collective-permute-done.44
  489.2 7.9 collective-permute-done.45
  515.9 9.8 %collective-permute-done.47.peer_ref = bf16[1024,192]{1,0:T(8,128)(2,1)S(1)} collective-permute-done((bf16[1024,192]{1,0:T(8,128)(2,1)S(1)}, bf16[1024,192]{1,0:T(8,128)(2,1)S(1)}, u32[]{:S(2)}, u32[]{:S(2)}) %collective-permute-start.47) | collective-permute-done | bytes 393248 | tf_op jit(solution)/shard_map/ppermute | solution.py:527
  526.5 17.2 %attend_back.1 = (f32[1024,384]{1,0:T(8,128)}, bf16[384,576]{1,0:T(8,128)(2,1)}) custom-call(bf16[1024,192]{1,0:T(8,128)(2,1)} %copy-done.25, bf16[1024,192]{1,0:T(8,128)(2,1)} %copy-done.42, bf16[9,1024,64]{2,1,0:T(8,128)(2,1)} %get-tuple-element.97.qkv_ref, f32[3,1024,64]{2,1,0:T(8,128)} %get-tuple-element.98.attended_ref, ...), custom_call_target="tpu_custom_call" | custom-call | flops 1258291200 | bytes 9437184 | tf_op jit(solution)/shard_map/attend_back/pallas_call | solution.py:712
  557.8 5.9 collective-permute-start.50
  569.3 6.4 collective-permute-done.49
  593.7 14.4 %collective-permute-done.57 = bf16[192,576]{0,1:T(8,128)(2,1)S(1)} collective-permute-done((bf16[192,576]{0,1:T(8,128)(2,1)S(1)}, bf16[192,576]{0,1:T(8,128)(2,1)S(1)}, u32[]{:S(2)}, u32[]{:S(2)}) %collective-permute-start.57) | collective-permute-done | bytes 221216 | tf_op jit(solution)/shard_map/ppermute | solution.py:527
  613.0 79.4 %collective-permute-done.91 = bf16[2,512,384]{2,1,0:T(8,128)(2,1)S(1)} collective-permute-done((bf16[2,512,384]{2,1,0:T(8,128)(2,1)S(1)}, bf16[2,512,384]{2,1,0:T(8,128)(2,1)S(1)}, u32[]{:S(2)}, u32[]{:S(2)}) %collective-permute-start.91) | collective-permute-done | bytes 786464 | tf_op jit(solution)/shard_map/ppermute | solution.py:527
  702.1 24.0 %collective-permute-done.82 = bf16[2,384,1024]{2,1,0:T(8,128)(2,1)S(1)} collective-permute-done((bf16[2,384,1024]{2,1,0:T(8,128)(2,1)S(1)}, bf16[2,384,1024]{2,1,0:T(8,128)(2,1)S(1)}, u32[]{:S(2)}, u32[]{:S(2)}) %collective-permute-start.82) | collective-permute-done | bytes 1572896 | tf_op jit(solution)/shard_map/ppermute | solution.py:527
  728.1 31.7 %collective-permute-done.76 = bf16[2,384,1024]{2,1,0:T(8,128)(2,1)S(1)} collective-permute-done((bf16[2,384,1024]{2,1,0:T(8,128)(2,1)S(1)}, bf16[2,384,1024]{2,1,0:T(8,128)(2,1)S(1)}, u32[]{:S(2)}, u32[]{:S(2)}) %collective-permute-start.76) | collective-permute-done | bytes 1572896 | tf_op jit(solution)/shard_map/ppermute | solution.py:527
  761.5 15.1 %collective-permute-done.85 = bf16[2,512,384]{2,1,0:T(8,128)(2,1)S(1)} collective-permute-done((bf16[2,512,384]{2,1,0:T(8,128)(2,1)}, bf16[2,512,384]{2,1,0:T(8,128)(2,1)S(1)}, u32[]{:S(2)}, u32[]{:S(2)}) %collective-permute-start.85) | collective-permute-done | bytes 786464 | tf_op jit(solution)/shard_map/ppermute | solution.py:527
  776.7 16.4 %collective-permute-done.79 = bf16[2,512,384]{2,1,0:T(8,128)(2,1)S(1)} collective-permute-done((bf16[2,512,384]{2,1,0:T(8,128)(2,1)}, bf16[2,512,384]{2,1,0:T(8,128)(2,1)S(1)}, u32[]{:S(2)}, u32[]{:S(2)}) %collective-permute-start.79) | collective-permute-done | bytes 786464 | tf_op jit(solution)/shard_map/ppermute | solution.py:527
  803.5 6.8 spread.4
  810.3 6.8 spread.5
  817.1 6.8 spread.6
  824.0 6.9 spread.7
  (516 shorter events, 294.5 us)
Async XLA Ops:
  10.1 84.4 %collective-permute-start.21 = (bf16[256,384]{1,0:T(8,128)(2,1)}, bf16[256,384]{1,0:T(8,128)(2,1)S(1)}, u32[]{:S(2)}, u32[]{:S(2)}) collective-permute-start(bf16[256,384]{1,0:T(8,128)(2,1)} %param.16), channel_id=1, source_target_pairs={{0,2},{1,3},{2,0},{3,1},{4,6},{5,7},{6,4},{7,5},{8,10},{9,11},{10,... | collective-permute-start | bytes 589832 | tf_op jit(solution)/shard_map/ppermute | solution.py:532
  28.0 81.8 %collective-permute-start.22 = (bf16[256,384]{1,0:T(8,128)(2,1)S(1)}, bf16[256,384]{1,0:T(8,128)(2,1)}, u32[]{:S(2)}, u32[]{:S(2)}) collective-permute-start(bf16[256,384]{1,0:T(8,128)(2,1)S(1)} %copy-done.27), channel_id=1, source_target_pairs={{0,3},{1,0},{2,1},{3,2},{4,7},{5,4},{6,5},{7,6},{8,11},{9,8},{10,9... | collective-permute-start | bytes 589832 | tf_op jit(solution)/shard_map/ppermute | solution.py:532
  28.3 31.1 %collective-permute-start.7 = (f32[384]{0:T(512)S(1)}, f32[384]{0:T(512)S(1)}, u32[]{:S(2)}, u32[]{:S(2)}) collective-permute-start(f32[384]{0:T(512)S(1)} %copy-done.68), channel_id=1, source_target_pairs={{0,4},{4,0},{1,5},{5,1},{2,6},{6,2},{3,7},{7,3},{8,12},{12,8},{9,1... | collective-permute-start | bytes 4616 | tf_op jit(solution)/shard_map/ppermute | solution.py:527
  116.2 86.1 %collective-permute-start.31 = (bf16[1024,512]{0,1:T(8,128)(2,1)}, bf16[1024,512]{0,1:T(8,128)(2,1)}, u32[]{:S(2)}, u32[]{:S(2)}) collective-permute-start(bf16[1024,512]{0,1:T(8,128)(2,1)} %convolution_convert_fusion), channel_id=1, source_target_pairs={{0,4},{4,0},{1,5},{5,1},{2,6},{6,2},{3,7},{7,3},{8,12},{12,8},{9,1... | collective-permute-start | bytes 3145736 | tf_op jit(solution)/shard_map/ppermute | solution.py:527
  132.4 66.5 %collective-permute-start.30 = (bf16[1024,1024]{0,1:T(8,128)(2,1)}, bf16[1024,1024]{0,1:T(8,128)(2,1)}, u32[]{:S(2)}, u32[]{:S(2)}) collective-permute-start(bf16[1024,1024]{0,1:T(8,128)(2,1)} %pad_maximum_fusion), channel_id=1, source_target_pairs={{0,4},{4,0},{1,5},{5,1},{2,6},{6,2},{3,7},{7,3},{8,12},{12,8},{9,1... | collective-permute-start | bytes 6291464 | tf_op jit(solution)/shard_map/ppermute | solution.py:527
  160.8 51.1 %collective-permute-start.29 = (bf16[4,192,512]{2,1,0:T(8,128)(2,1)}, bf16[4,192,512]{2,1,0:T(8,128)(2,1)}, u32[]{:S(2)}, u32[]{:S(2)}) collective-permute-start(bf16[4,192,512]{2,1,0:T(8,128)(2,1)} %get-tuple-element.82.back_own_ref), channel_id=1, source_target_pairs={{0,4},{4,0},{1,5},{5,1},{2,6},{6,2},{3,7},{7,3},{8,12},{12,8},{9,1... | collective-permute-start | bytes 2359304 | tf_op jit(solution)/shard_map/ppermute | solution.py:527
  164.0 121.1 %collective-permute-start.27 = (bf16[4,192,512]{2,1,0:T(8,128)(2,1)}, bf16[4,192,512]{2,1,0:T(8,128)(2,1)}, u32[]{:S(2)}, u32[]{:S(2)}) collective-permute-start(bf16[4,192,512]{2,1,0:T(8,128)(2,1)} %get-tuple-element.78.back_own_ref), channel_id=1, source_target_pairs={{0,4},{4,0},{1,5},{5,1},{2,6},{6,2},{3,7},{7,3},{8,12},{12,8},{9,1... | collective-permute-start | bytes 2359304 | tf_op jit(solution)/shard_map/ppermute | solution.py:527
  172.2 157.2 %collective-permute-start.25 = (bf16[4,192,512]{2,1,0:T(8,128)(2,1)}, bf16[4,192,512]{2,1,0:T(8,128)(2,1)}, u32[]{:S(2)}, u32[]{:S(2)}) collective-permute-start(bf16[4,192,512]{2,1,0:T(8,128)(2,1)} %get-tuple-element.74.back_own_ref), channel_id=1, source_target_pairs={{0,4},{4,0},{1,5},{5,1},{2,6},{6,2},{3,7},{7,3},{8,12},{12,8},{9,1... | collective-permute-start | bytes 2359304 | tf_op jit(solution)/shard_map/ppermute | solution.py:527
  198.9 72.9 %collective-permute-start.28 = (bf16[4,192,1024]{2,1,0:T(8,128)(2,1)}, bf16[4,192,1024]{2,1,0:T(8,128)(2,1)}, u32[]{:S(2)}, u32[]{:S(2)}) collective-permute-start(bf16[4,192,1024]{2,1,0:T(8,128)(2,1)} %get-tuple-element.81.pre_own_ref), channel_id=1, source_target_pairs={{0,4},{4,0},{1,5},{5,1},{2,6},{6,2},{3,7},{7,3},{8,12},{12,8},{9,1... | collective-permute-start | bytes 4718600 | tf_op jit(solution)/shard_map/ppermute | solution.py:527
  202.4 103.1 %collective-permute-start.26 = (bf16[4,192,1024]{2,1,0:T(8,128)(2,1)}, bf16[4,192,1024]{2,1,0:T(8,128)(2,1)}, u32[]{:S(2)}, u32[]{:S(2)}) collective-permute-start(bf16[4,192,1024]{2,1,0:T(8,128)(2,1)} %get-tuple-element.77.pre_own_ref), channel_id=1, source_target_pairs={{0,4},{4,0},{1,5},{5,1},{2,6},{6,2},{3,7},{7,3},{8,12},{12,8},{9,1... | collective-permute-start | bytes 4718600 | tf_op jit(solution)/shard_map/ppermute | solution.py:527
  211.9 186.5 %collective-permute-start.23 = (bf16[4,192,512]{2,1,0:T(8,128)(2,1)}, bf16[4,192,512]{2,1,0:T(8,128)(2,1)}, u32[]{:S(2)}, u32[]{:S(2)}) collective-permute-start(bf16[4,192,512]{2,1,0:T(8,128)(2,1)} %get-tuple-element.70.back_own_ref), channel_id=1, source_target_pairs={{0,4},{4,0},{1,5},{5,1},{2,6},{6,2},{3,7},{7,3},{8,12},{12,8},{9,1... | collective-permute-start | bytes 2359304 | tf_op jit(solution)/shard_map/ppermute | solution.py:527
  271.8 126.6 %collective-permute-start.19 = (bf16[4,192,1024]{2,1,0:T(8,128)(2,1)}, bf16[4,192,1024]{2,1,0:T(8,128)(2,1)}, u32[]{:S(2)}, u32[]{:S(2)}) collective-permute-start(bf16[4,192,1024]{2,1,0:T(8,128)(2,1)} %get-tuple-element.69.pre_own_ref), channel_id=1, source_target_pairs={{0,4},{4,0},{1,5},{5,1},{2,6},{6,2},{3,7},{7,3},{8,12},{12,8},{9,1... | collective-permute-start | bytes 4718600 | tf_op jit(solution)/shard_map/ppermute | solution.py:527
  285.0 100.2 %collective-permute-start.24 = (bf16[4,192,1024]{2,1,0:T(8,128)(2,1)}, bf16[4,192,1024]{2,1,0:T(8,128)(2,1)}, u32[]{:S(2)}, u32[]{:S(2)}) collective-permute-start(bf16[4,192,1024]{2,1,0:T(8,128)(2,1)} %get-tuple-element.73.pre_own_ref), channel_id=1, source_target_pairs={{0,4},{4,0},{1,5},{5,1},{2,6},{6,2},{3,7},{7,3},{8,12},{12,8},{9,1... | collective-permute-start | bytes 4718600 | tf_op jit(solution)/shard_map/ppermute | solution.py:527
  448.0 99.1 %collective-permute-start.96 = (bf16[2,512,384]{2,1,0:T(8,128)(2,1)}, bf16[2,512,384]{2,1,0:T(8,128)(2,1)}, u32[]{:S(2)}, u32[]{:S(2)}) collective-permute-start(bf16[2,512,384]{2,1,0:T(8,128)(2,1)} %dynamic-slice_bitcast_fusion.4), channel_id=1, source_target_pairs={{0,8},{8,0},{16,24},{24,16},{1,9},{9,1},{17,25},{25,17},{2,10},{10... | collective-permute-start | bytes 2359304 | tf_op jit(solution)/shard_map/ppermute | solution.py:527
  454.1 128.8 %collective-permute-start.93 = (bf16[2,384,1024]{2,1,0:T(8,128)(2,1)}, bf16[2,384,1024]{2,1,0:T(8,128)(2,1)}, u32[]{:S(2)}, u32[]{:S(2)}) collective-permute-start(bf16[2,384,1024]{2,1,0:T(8,128)(2,1)} %dynamic-slice_bitcast_fusion), channel_id=1, source_target_pairs={{0,8},{8,0},{16,24},{24,16},{1,9},{9,1},{17,25},{25,17},{2,10},{10... | collective-permute-start | bytes 4718600 | tf_op jit(solution)/shard_map/ppermute | solution.py:527
  455.6 97.1 %collective-permute-start.90 = (bf16[2,512,384]{2,1,0:T(8,128)(2,1)}, bf16[2,512,384]{2,1,0:T(8,128)(2,1)}, u32[]{:S(2)}, u32[]{:S(2)}) collective-permute-start(bf16[2,512,384]{2,1,0:T(8,128)(2,1)} %dynamic-slice_bitcast_fusion.5), channel_id=1, source_target_pairs={{0,8},{8,0},{16,24},{24,16},{1,9},{9,1},{17,25},{25,17},{2,10},{10... | collective-permute-start | bytes 2359304 | tf_op jit(solution)/shard_map/ppermute | solution.py:527
  514.9 37.9 %collective-permute-start.84 = (bf16[2,512,384]{2,1,0:T(8,128)(2,1)}, bf16[2,512,384]{2,1,0:T(8,128)(2,1)}, u32[]{:S(2)}, u32[]{:S(2)}) collective-permute-start(bf16[2,512,384]{2,1,0:T(8,128)(2,1)} %dynamic-slice_bitcast_fusion.6), channel_id=1, source_target_pairs={{0,8},{8,0},{16,24},{24,16},{1,9},{9,1},{17,25},{25,17},{2,10},{10... | collective-permute-start | bytes 2359304 | tf_op jit(solution)/shard_map/ppermute | solution.py:527
  552.7 34.5 %collective-permute-start.87 = (bf16[2,384,1024]{2,1,0:T(8,128)(2,1)}, bf16[2,384,1024]{2,1,0:T(8,128)(2,1)}, u32[]{:S(2)}, u32[]{:S(2)}) collective-permute-start(bf16[2,384,1024]{2,1,0:T(8,128)(2,1)} %dynamic-slice_bitcast_fusion.1), channel_id=1, source_target_pairs={{0,8},{8,0},{16,24},{24,16},{1,9},{9,1},{17,25},{25,17},{2,10},{10... | collective-permute-start | bytes 4718600 | tf_op jit(solution)/shard_map/ppermute | solution.py:527
  555.0 35.2 %collective-permute-start.81 = (bf16[2,384,1024]{2,1,0:T(8,128)(2,1)}, bf16[2,384,1024]{2,1,0:T(8,128)(2,1)}, u32[]{:S(2)}, u32[]{:S(2)}) collective-permute-start(bf16[2,384,1024]{2,1,0:T(8,128)(2,1)} %dynamic-slice_bitcast_fusion.2), channel_id=1, source_target_pairs={{0,8},{8,0},{16,24},{24,16},{1,9},{9,1},{17,25},{25,17},{2,10},{10... | collective-permute-start | bytes 4718600 | tf_op jit(solution)/shard_map/ppermute | solution.py:527
  569.3 39.2 %collective-permute-start.75 = (bf16[2,384,1024]{2,1,0:T(8,128)(2,1)}, bf16[2,384,1024]{2,1,0:T(8,128)(2,1)}, u32[]{:S(2)}, u32[]{:S(2)}) collective-permute-start(bf16[2,384,1024]{2,1,0:T(8,128)(2,1)} %dynamic-slice_bitcast_fusion.3), channel_id=1, source_target_pairs={{0,8},{8,0},{16,24},{24,16},{1,9},{9,1},{17,25},{25,17},{2,10},{10... | collective-permute-start | bytes 4718600 | tf_op jit(solution)/shard_map/ppermute | solution.py:527
  581.3 31.0 %collective-permute-start.97 = (bf16[2,512,384]{2,1,0:T(8,128)(2,1)S(1)}, bf16[2,512,384]{2,1,0:T(8,128)(2,1)S(1)}, u32[]{:S(2)}, u32[]{:S(2)}) collective-permute-start(bf16[2,512,384]{2,1,0:T(8,128)(2,1)S(1)} %fusion.6), channel_id=1, source_target_pairs={{0,16},{8,24},{16,0},{24,8},{1,17},{9,25},{17,1},{25,9},{2,18},{10... | collective-permute-start | bytes 2359304 | tf_op jit(solution)/shard_map/ppermute | solution.py:527
  587.2 106.5 %collective-permute-start.94 = (bf16[2,384,1024]{2,1,0:T(8,128)(2,1)S(1)}, bf16[2,384,1024]{2,1,0:T(8,128)(2,1)S(1)}, u32[]{:S(2)}, u32[]{:S(2)}) collective-permute-start(bf16[2,384,1024]{2,1,0:T(8,128)(2,1)S(1)} %fusion.1), channel_id=1, source_target_pairs={{0,16},{8,24},{16,0},{24,8},{1,17},{9,25},{17,1},{25,9},{2,18},{10... | collective-permute-start | bytes 4718600 | tf_op jit(solution)/shard_map/ppermute | solution.py:527
  590.2 109.9 %collective-permute-start.88 = (bf16[2,384,1024]{2,1,0:T(8,128)(2,1)S(1)}, bf16[2,384,1024]{2,1,0:T(8,128)(2,1)S(1)}, u32[]{:S(2)}, u32[]{:S(2)}) collective-permute-start(bf16[2,384,1024]{2,1,0:T(8,128)(2,1)S(1)} %fusion.2), channel_id=1, source_target_pairs={{0,16},{8,24},{16,0},{24,8},{1,17},{9,25},{17,1},{25,9},{2,18},{10... | collective-permute-start | bytes 4718600 | tf_op jit(solution)/shard_map/ppermute | solution.py:527
  608.1 84.3 %collective-permute-start.91 = (bf16[2,512,384]{2,1,0:T(8,128)(2,1)S(1)}, bf16[2,512,384]{2,1,0:T(8,128)(2,1)S(1)}, u32[]{:S(2)}, u32[]{:S(2)}) collective-permute-start(bf16[2,512,384]{2,1,0:T(8,128)(2,1)S(1)} %fusion.7), channel_id=1, source_target_pairs={{0,16},{8,24},{16,0},{24,8},{1,17},{9,25},{17,1},{25,9},{2,18},{10... | collective-permute-start | bytes 2359304 | tf_op jit(solution)/shard_map/ppermute | solution.py:527
  608.5 117.6 %collective-permute-start.82 = (bf16[2,384,1024]{2,1,0:T(8,128)(2,1)S(1)}, bf16[2,384,1024]{2,1,0:T(8,128)(2,1)S(1)}, u32[]{:S(2)}, u32[]{:S(2)}) collective-permute-start(bf16[2,384,1024]{2,1,0:T(8,128)(2,1)S(1)} %fusion.3), channel_id=1, source_target_pairs={{0,16},{8,24},{16,0},{24,8},{1,17},{9,25},{17,1},{25,9},{2,18},{10... | collective-permute-start | bytes 4718600 | tf_op jit(solution)/shard_map/ppermute | solution.py:527
  612.4 147.4 %collective-permute-start.76 = (bf16[2,384,1024]{2,1,0:T(8,128)(2,1)S(1)}, bf16[2,384,1024]{2,1,0:T(8,128)(2,1)S(1)}, u32[]{:S(2)}, u32[]{:S(2)}) collective-permute-start(bf16[2,384,1024]{2,1,0:T(8,128)(2,1)S(1)} %fusion.4), channel_id=1, source_target_pairs={{0,16},{8,24},{16,0},{24,8},{1,17},{9,25},{17,1},{25,9},{2,18},{10... | collective-permute-start | bytes 4718600 | tf_op jit(solution)/shard_map/ppermute | solution.py:527
  698.1 78.5 %collective-permute-start.85 = (bf16[2,512,384]{2,1,0:T(8,128)(2,1)}, bf16[2,512,384]{2,1,0:T(8,128)(2,1)S(1)}, u32[]{:S(2)}, u32[]{:S(2)}) collective-permute-start(bf16[2,512,384]{2,1,0:T(8,128)(2,1)} %fusion.8), channel_id=1, source_target_pairs={{0,16},{8,24},{16,0},{24,8},{1,17},{9,25},{17,1},{25,9},{2,18},{10... | collective-permute-start | bytes 2359304 | tf_op jit(solution)/shard_map/ppermute | solution.py:527
  698.5 94.5 %collective-permute-start.79 = (bf16[2,512,384]{2,1,0:T(8,128)(2,1)}, bf16[2,512,384]{2,1,0:T(8,128)(2,1)S(1)}, u32[]{:S(2)}, u32[]{:S(2)}) collective-permute-start(bf16[2,512,384]{2,1,0:T(8,128)(2,1)} %fusion.9), channel_id=1, source_target_pairs={{0,16},{8,24},{16,0},{24,8},{1,17},{9,25},{17,1},{25,9},{2,18},{10... | collective-permute-start | bytes 2359304 | tf_op jit(solution)/shard_map/ppermute | solution.py:527
  700.2 92.9 %collective-permute-start.98 = (bf16[2,512,384]{2,1,0:T(8,128)(2,1)S(1)}, bf16[2,512,384]{2,1,0:T(8,128)(2,1)S(1)}, u32[]{:S(2)}, u32[]{:S(2)}) collective-permute-start(bf16[2,512,384]{2,1,0:T(8,128)(2,1)S(1)} %add_convert_fusion.4.down_half_ref), channel_id=1, source_target_pairs={{0,8},{8,0},{16,24},{24,16},{1,9},{9,1},{17,25},{25,17},{2,10},{10... | collective-permute-start | bytes 2359304 | tf_op jit(solution)/shard_map/ppermute | solution.py:527
  726.1 73.6 %collective-permute-start.95 = (bf16[2,384,1024]{2,1,0:T(8,128)(2,1)S(1)}, bf16[2,384,1024]{2,1,0:T(8,128)(2,1)S(1)}, u32[]{:S(2)}, u32[]{:S(2)}) collective-permute-start(bf16[2,384,1024]{2,1,0:T(8,128)(2,1)S(1)} %add_convert_fusion.both_half_ref), channel_id=1, source_target_pairs={{0,8},{8,0},{16,24},{24,16},{1,9},{9,1},{17,25},{25,17},{2,10},{10... | collective-permute-start | bytes 4718600 | tf_op jit(solution)/shard_map/ppermute | solution.py:527
  761.4 38.1 %collective-permute-start.92 = (bf16[2,512,384]{2,1,0:T(8,128)(2,1)S(1)}, bf16[2,512,384]{2,1,0:T(8,128)(2,1)S(1)}, u32[]{:S(2)}, u32[]{:S(2)}) collective-permute-start(bf16[2,512,384]{2,1,0:T(8,128)(2,1)S(1)} %add_convert_fusion.5.down_half_ref), channel_id=1, source_target_pairs={{0,8},{8,0},{16,24},{24,16},{1,9},{9,1},{17,25},{25,17},{2,10},{10... | collective-permute-start | bytes 2359304 | tf_op jit(solution)/shard_map/ppermute | solution.py:527
  776.7 33.6 %collective-permute-start.89 = (bf16[2,384,1024]{2,1,0:T(8,128)(2,1)}, bf16[2,384,1024]{2,1,0:T(8,128)(2,1)}, u32[]{:S(2)}, u32[]{:S(2)}) collective-permute-start(bf16[2,384,1024]{2,1,0:T(8,128)(2,1)} %add_convert_fusion.1.both_half_ref), channel_id=1, source_target_pairs={{0,8},{8,0},{16,24},{24,16},{1,9},{9,1},{17,25},{25,17},{2,10},{10... | collective-permute-start | bytes 4718600 | tf_op jit(solution)/shard_map/ppermute | solution.py:527
  (146 other events, 1972.0 us)

commit v2 on v1

--- a/solution.py
+++ b/solution.py
@@ -520,6 +520,7 @@
 F32 = jnp.float32
 BF16 = jnp.bfloat16
 MASKED = -1e30
+LIGHT = pl.CostEstimate(flops=1, transcendentals=0, bytes_accessed=1)
 
 
 def swap(value, axis, step=1):
@@ -568,22 +569,46 @@
     return value
 
 
-def pair_halves(whole):
+def held(value, *others):
+    return lax.optimization_barrier((value,) + others)[0]
+
+
+def high_low(value):
+    high = value.astype(BF16)
+    return high, (value - high.astype(F32)).astype(BF16)
+
+
+def with_rows(value, extra):
+    high, low = high_low(extra)
+    rows = jnp.concatenate([high, low], -2)
+    room = [(0, 0)] * (rows.ndim - 1) + [(0, value.shape[-1] - rows.shape[-1])]
+    return jnp.concatenate([value, jnp.pad(rows, room)], -2)
+
+
+def split_rows(value, count, extra, width):
+    tail = value[..., count:, :width].astype(F32)
+    return value[..., :count, :], tail[..., :extra, :] + tail[..., extra:, :]
+
+
+def pair_half(whole):
     core = lax.axis_index("dp") % 2
     halves = whole.reshape((2, whole.shape[0] // 2) + whole.shape[1:])
     mine = lax.dynamic_index_in_dim(halves, core, 0, False)
     other = lax.dynamic_index_in_dim(halves, 1 - core, 0, False)
-    half = (mine.astype(F32) + swap(other, "dp", 1).astype(F32)).astype(BF16)
+    return (mine.astype(F32) + swap(other, "dp", 1).astype(F32)).astype(BF16)
+
+
+def cross_sum(half):
     step = 2
     while step < lax.axis_size("dp"):
         half = (half.astype(F32) + swap(half, "dp", step).astype(F32)).astype(BF16)
         step *= 2
-    return half, swap(half, "dp", 1)
-
-
-def dp_total(whole):
+    return half
+
+
+def both_halves(half):
     core = lax.axis_index("dp") % 2
-    half, rest = pair_halves(whole)
+    rest = swap(half, "dp", 1)
     first = jnp.where(core == 0, half, rest)
     second = jnp.where(core == 0, rest, half)
     return jnp.concatenate([first, second], 0).astype(F32)
@@ -650,7 +675,6 @@
 def attend(left, right, weight_left, weight_right, out_weight, cosine, sine, start, block):
     tokens, features = left.shape
     heads = weight_left.shape[1] // (3 * HD)
-    pairs = sum(block * (low + block) for low in range(0, tokens, block)) * heads
     return pl.pallas_call(
         functools.partial(attend_kernel, heads, block, tokens // 2, HD ** (-0.5)),
         out_shape=(
@@ -659,11 +683,7 @@
             jax.ShapeDtypeStruct((heads, tokens, 1), F32),
             jax.ShapeDtypeStruct((tokens, features), BF16),
         ),
-        cost_estimate=pl.CostEstimate(
-            flops=4 * pairs * HD + 4 * tokens * features * 3 * HD * heads,
-            transcendentals=pairs,
-            bytes_accessed=8 * tokens * features,
-        ),
+        cost_estimate=LIGHT,
         name="attend",
     )(left, right, weight_left, weight_right, out_weight, cosine, sine, start)
 
@@ -708,7 +728,6 @@
 
 def attend_back(own, peer, qkv, attended, log_total, cosine, sine, start, normed, weight, block):
     heads, tokens, unused = attended.shape
-    pairs = sum(block * (low + block) for low in range(0, tokens, block)) * heads
     return pl.pallas_call(
         functools.partial(attend_back_kernel, heads, block, tokens // 2, HD ** (-0.5)),
         out_shape=(
@@ -716,9 +735,7 @@
             jax.ShapeDtypeStruct(weight.shape, BF16),
         ),
         scratch_shapes=[pltpu.VMEM((tokens, HD), F32)] * 3,
-        cost_estimate=pl.CostEstimate(
-            flops=10 * pairs * HD, transcendentals=pairs, bytes_accessed=16 * tokens * 3 * heads * HD
-        ),
+        cost_estimate=LIGHT,
         name="attend_back",
     )(own, peer, qkv, attended, log_total, cosine, sine, start, normed, weight)
 
@@ -758,11 +775,7 @@
             jax.ShapeDtypeStruct((count, capacity, hidden), BF16),
             jax.ShapeDtypeStruct((count, capacity, features), BF16),
         ),
-        cost_estimate=pl.CostEstimate(
-            flops=2 * count * capacity * features * (tokens + hidden),
-            transcendentals=0,
-            bytes_accessed=2 * count * (hidden * features + capacity * (hidden + features)),
-        ),
+        cost_estimate=LIGHT,
         name="back_hidden",
     )(rank, cot_rows, down)
 
@@ -796,11 +809,7 @@
             jax.ShapeDtypeStruct((count, capacity, 2 * hidden), BF16),
             jax.ShapeDtypeStruct((count, capacity, features), BF16),
         ),
-        cost_estimate=pl.CostEstimate(
-            flops=2 * count * capacity * features * (tokens + 2 * hidden),
-            transcendentals=0,
-            bytes_accessed=2 * count * (2 * hidden * features + capacity * (2 * hidden + features)),
-        ),
+        cost_estimate=LIGHT,
         name="open_experts",
     )(rank, token_rows, gate, up)
 
@@ -815,7 +824,7 @@
 def experts_kernel(
     rank_ref, prob_ref, pre_own_ref, pre_peer_ref, back_own_ref, back_peer_ref, rows_ref, cot_ref,
     gate_ref, up_ref, down_ref, out_in_ref, dx_in_ref,
-    both_grad_ref, down_grad_ref, share_ref, out_ref, dx_ref,
+    grad_ref, share_ref, out_ref, dx_ref,
 ):
     capacity, hidden = back_own_ref.shape[1:]
 
@@ -841,16 +850,17 @@
     out_ref[...] += matmul(chosen, out_rows, 0, 0)
     dx_rows = (matmul(grad_gate, gate_ref[0], 1, 1) + matmul(grad_up, up_ref[0], 1, 1)).astype(BF16)
     dx_ref[...] += matmul(chosen, dx_rows, 0, 0)
-    both_grad_ref[0, :, :hidden] = matmul(rows, grad_gate, 0, 0).astype(BF16)
-    both_grad_ref[0, :, hidden:] = matmul(rows, grad_up, 0, 0).astype(BF16)
-    down_grad_ref[0] = matmul(scaled, cot_ref[0], 0, 0).astype(BF16)
+    grad_ref[0, 0] = matmul(rows, grad_gate, 0, 0).astype(BF16)
+    grad_ref[0, 1] = matmul(rows, grad_up, 0, 0).astype(BF16)
+    grad_ref[0, 2] = matmul(cot_ref[0], scaled, 0, 0).astype(BF16)
 
 
 def run_experts(
     rank, probs, pre_own, pre_peer, back_own, back_peer, rows, cot_rows, gate, up, down, out_sum, dx_sum, first
 ):
-    count, capacity, hidden = back_own.shape
-    tokens, features = out_sum.shape
+    count, capacity, features = rows.shape
+    hidden = gate.shape[2]
+    tokens = out_sum.shape[0]
 
     def at(shape, base):
         return pl.BlockSpec((1,) + shape, lambda i: (base + i, 0, 0))
@@ -863,10 +873,10 @@
             at((1, tokens), first),
             at((capacity, 2 * hidden), 0),
             at((capacity, 2 * hidden), 0),
-            at((capacity, hidden), 0),
-            at((capacity, hidden), 0),
+            at((capacity, hidden), first),
+            at((capacity, hidden), first),
             at((capacity, features), 0),
-            at((capacity, features), 0),
+            at((capacity, features), first),
             at((features, hidden), first),
             at((features, hidden), first),
             at((hidden, features), first),
@@ -874,59 +884,46 @@
             whole_block((tokens, features)),
         ],
         out_specs=(
-            at((features, 2 * hidden), 0),
-            at((hidden, features), 0),
+            pl.BlockSpec((1, 3, features, hidden), lambda i: (i, 0, 0, 0)),
             at((1, tokens), 0),
             whole_block((tokens, features)),
             whole_block((tokens, features)),
         ),
         out_shape=(
-            jax.ShapeDtypeStruct((count, features, 2 * hidden), BF16),
-            jax.ShapeDtypeStruct((count, hidden, features), BF16),
+            jax.ShapeDtypeStruct((count, 3, features, hidden), BF16),
             jax.ShapeDtypeStruct((count, 1, tokens), F32),
             jax.ShapeDtypeStruct((tokens, features), F32),
             jax.ShapeDtypeStruct((tokens, features), F32),
         ),
-        cost_estimate=pl.CostEstimate(
-            flops=2 * count * capacity * features * (2 * tokens + 6 * hidden),
-            transcendentals=count * capacity * hidden,
-            bytes_accessed=2 * count * (6 * hidden * features + 6 * capacity * hidden),
-        ),
+        cost_estimate=LIGHT,
         name="run_experts",
     )(
         rank, probs, pre_own, pre_peer, back_own, back_peer, rows, cot_rows, gate, up, down, out_sum, dx_sum
     )
 
 
-def spread_kernel(core_ref, both_half_ref, both_rest_ref, down_half_ref, down_rest_ref, *refs):
-    gate_ref, up_ref, down_ref = refs[-3:]
-    hidden = gate_ref.shape[2]
+def spread_kernel(core_ref, half_ref, rest_ref, *refs):
+    gate_ref, up_ref, down_ref, flag_ref = refs[-4:]
+    flag_ref[...] = jnp.zeros_like(flag_ref)
+
+    def write(source_ref):
+        gate_ref[0] = source_ref[0, 0].astype(F32)
+        up_ref[0] = source_ref[0, 1].astype(F32)
+        down_ref[0] = source_ref[0, 2].astype(F32).T
+
     own = pl.program_id(0) < pl.num_programs(0) // 2
-
-    @pl.when(own)
-    def first():
-        both = both_half_ref[0].astype(F32)
-        gate_ref[0] = both[:, :hidden]
-        up_ref[0] = both[:, hidden:]
-        down_ref[0] = down_half_ref[0].astype(F32)
-
-    @pl.when(jnp.logical_not(own))
-    def second():
-        both = both_rest_ref[0].astype(F32)
-        gate_ref[0] = both[:, :hidden]
-        up_ref[0] = both[:, hidden:]
-        down_ref[0] = down_rest_ref[0].astype(F32)
-
-
-def spread(core, both_half, both_rest, down_half, down_rest, earlier, first, experts):
-    half = both_half.shape[0]
-    features, hidden = both_half.shape[1], both_half.shape[2] // 2
+    pl.when(own)(lambda: write(half_ref))
+    pl.when(jnp.logical_not(own))(lambda: write(rest_ref))
+
+
+def spread(core, half_grads, rest_grads, earlier, first, experts):
+    half, unused, features, hidden = half_grads.shape
 
     def own_index(i, core):
-        return (jnp.minimum(i, half - 1), 0, 0)
+        return (jnp.minimum(i, half - 1), 0, 0, 0)
 
     def rest_index(i, core):
-        return (jnp.maximum(i - half, 0), 0, 0)
+        return (jnp.maximum(i - half, 0), 0, 0, 0)
 
     def out_index(i, core):
         place = jnp.where(i < half, core[0] * half + i, (1 - core[0]) * half + i - half)
@@ -939,21 +936,19 @@
             num_scalar_prefetch=1,
             grid=(2 * half,),
             in_specs=[
-                pl.BlockSpec((1, features, 2 * hidden), own_index),
-                pl.BlockSpec((1, features, 2 * hidden), rest_index),
-                pl.BlockSpec((1, hidden, features), own_index),
-                pl.BlockSpec((1, hidden, features), rest_index),
+                pl.BlockSpec((1, 3, features, hidden), own_index),
+                pl.BlockSpec((1, 3, features, hidden), rest_index),
             ]
             + [pl.BlockSpec(memory_space=pl.ANY)] * len(earlier),
-            out_specs=tuple(pl.BlockSpec((1,) + shape, out_index) for shape in shapes),
+            out_specs=tuple(pl.BlockSpec((1,) + shape, out_index) for shape in shapes)
+            + (whole_block((8, 128)),),
         ),
-        out_shape=tuple(jax.ShapeDtypeStruct((experts,) + shape, F32) for shape in shapes),
-        input_output_aliases={5 + i: i for i in range(len(earlier))},
-        cost_estimate=pl.CostEstimate(
-            flops=0, transcendentals=0, bytes_accessed=36 * half * features * hidden
-        ),
+        out_shape=tuple(jax.ShapeDtypeStruct((experts,) + shape, F32) for shape in shapes)
+        + (jax.ShapeDtypeStruct((8, 128), F32),),
+        input_output_aliases={3 + i: i for i in range(len(earlier))},
+        cost_estimate=LIGHT,
         name="spread",
-    )(core, both_half, both_rest, down_half, down_rest, *earlier)
+    )(core, half_grads, rest_grads, *earlier)
 
 
 def paired_body(
@@ -988,13 +983,17 @@
     chunk = 4
     core = (lax.axis_index("dp") % 2).reshape(1)
 
+    gain_high, gain_low = high_low(first_gain)
+    gain_last = (first_gain - gain_high.astype(F32) - gain_low.astype(F32)).astype(BF16)
+    gain_rows = jnp.pad(jnp.stack([gain_high, gain_low, gain_last]), ((0, 5), (0, 0)))
+    peer_first = swap(jnp.concatenate([inputs, gain_rows], 0), "row")
+    peer_gain = jnp.sum(peer_first[tok_rest : tok_rest + 3].astype(F32)[::-1], 0)
+    peer_weight = swap(attend_in, "row")
     own_parts = col_parts(inputs)
-    peer_parts = [swap(part, "row") for part in own_parts]
+    peer_parts = [peer_first[:tok_rest]] + [swap(part, "row") for part in own_parts[1:]]
     own_all = in_order(own_parts, "col").reshape(tok_block, feat_dev).astype(F32)
     peer_all = in_order(peer_parts, "col").reshape(tok_block, feat_dev).astype(F32)
-    peer_weight = swap(attend_in, "row")
-    peer_gain = swap(first_gain, "row")
-    cot_all = col_rows(cotangent)
+    cot_all = col_rows(held(cotangent, *own_parts))
 
     squares_one = jnp.sum(own_all * own_all, 1) + jnp.sum(peer_all * peer_all, 1)
     scale_all = lax.rsqrt(squares_one / feat_full + EPSILON)[:, None]
@@ -1019,22 +1018,19 @@
     before = (offsets[:, None] < offsets[None, :]).astype(BF16)
     rank = jnp.dot(named.astype(BF16), before, preferred_element_type=F32).astype(jnp.int32)
     rank = jnp.where(named, rank, -1)[:, None, :]
-    count_own = jnp.sum(named.astype(F32), 1)
-
-    back_own, cot_rows, back_peer = [], [], []
-    for first in range(0, experts, chunk):
-        back, rows = back_hidden(rank, cot_all, expert_down, first, chunk, capacity)
-        back_own.append(back)
-        cot_rows.append(rows)
-        back_peer.append(swap(back, "row"))
+    count_total = sum_by_swaps(jnp.sum(named.astype(F32), 1), ("dp",))
+
+    qkv, attended, log_total, out_partial = attend(
+        normed_own, normed_peer, attend_in, peer_weight, attend_out, cosine, sine, start, block
+    )
+    cot_all = held(cot_all, out_partial)
+    back_own, cot_rows = back_hidden(rank, cot_all, expert_down, 0, experts, capacity)
+    back_peer = swap(back_own, "row")
     shared_back_own = matmul(cot_all, shared_down, 1, 1).astype(BF16)
     shared_back_peer = swap(shared_back_own, "row")
 
-    qkv, attended, log_total, out_partial = attend(
-        normed_own, normed_peer, attend_in, peer_weight, attend_out, cosine, sine, start, block
-    )
     inputs_f = inputs.astype(F32)
-    mixed_one = inputs_f + col_sum_rows(out_partial)
+    mixed_one = inputs_f + held(col_sum_rows(out_partial), back_own, shared_back_own)
     gained = mixed_one * second_gain
     partial_stats = jnp.concatenate(
         [
@@ -1048,22 +1044,43 @@
     router_probs = jax.nn.softmax(stats[:, 1:] * scale_two, -1)
     unit_two = mixed_one * scale_two
     normed_two = (unit_two * second_gain).astype(BF16)
-    normed_all = col_rows(normed_two)
-    probs_all = col_rows(router_probs)
-    probs_rows = probs_all.T[:, None, :]
-    count_total, prob_total = sum_by_swaps(jnp.stack([count_own, jnp.sum(probs_all, 0)]), ("dp",))
-    balance_loss = experts * jnp.sum(count_total / (2.0 * tokens_all) * prob_total / tokens_all)
-
+    sent = in_order(col_parts(with_rows(normed_two, router_probs.T)), "col")
+    normed_all, probs_all = split_rows(sent, tok_rest, experts, tok_rest)
+    normed_all = normed_all.reshape(tok_block, feat_dev)
+    probs_rows = probs_all.transpose(1, 0, 2).reshape(experts, 1, tok_block)
+
+    pre_own, token_rows, pre_peer = [], [], []
+    firsts = list(range(0, experts, chunk))
+    for first in firsts:
+        pre, rows = open_experts(rank, normed_all, expert_gate, expert_up, first, chunk, capacity)
+        pre_own.append(pre)
+        token_rows.append(rows)
     shared_pre_own = jnp.concatenate(
         [matmul(normed_all, shared_gate, 1, 0), matmul(normed_all, shared_up, 1, 0)], 1
     ).astype(BF16)
-    shared_pre_peer = swap(shared_pre_own, "row")
-    pre_own, token_rows, pre_peer = [], [], []
-    for first in range(0, experts, chunk):
-        pre, rows = open_experts(rank, normed_all, expert_gate, expert_up, first, chunk, capacity)
-        pre_own.append(pre)
-        token_rows.append(rows)
-        pre_peer.append(swap(pre, "row"))
+    order = pre_own[:-1] + [shared_pre_own] + pre_own[-1:]
+    arrived = []
+    for index, value in enumerate(order):
+        arrived.append(swap(held(value, *arrived[index - 2 : index - 1]) if index > 1 else value, "row"))
+    pre_peer = arrived[:-2] + arrived[-1:]
+    shared_pre_peer = arrived[-2]
+
+    out_sum = jnp.zeros((tok_block, feat_dev), F32)
+    dx_sum = jnp.zeros((tok_block, feat_dev), F32)
+    shares, halves, crossed = [], [], []
+    for index, first in enumerate(firsts):
+        pre = pre_peer[index]
+        if index:
+            pre = held(pre, halves[-1])
+        if index > 2:
+            pre = held(pre, crossed[index - 3])
+        grads, share, out_sum, dx_sum = run_experts(
+            rank, probs_rows, pre_own[index], pre, back_own, back_peer,
+            token_rows[index], cot_rows, expert_gate, expert_up, expert_down, out_sum, dx_sum, first,
+        )
+        shares.append(share[:, 0])
+        halves.append(pair_half(grads))
+        crossed.append(cross_sum(held(halves[-1], crossed[-1]) if index else halves[-1]))
 
     shared_pre = shared_pre_own.astype(F32) + shared_pre_peer.astype(F32)
     shared_back = shared_back_own.astype(F32) + shared_back_peer.astype(F32)
@@ -1071,52 +1088,64 @@
         value.astype(BF16)
         for value in gated(shared_pre[:, :shared_dev], shared_pre[:, shared_dev:], shared_back)
     )
-    out_sum = matmul(shared_hidden, shared_down, 1, 0)
-    dx_sum = matmul(shared_gate_pgrad, shared_gate, 1, 1) + matmul(shared_up_pgrad, shared_up, 1, 1)
-    shared_gate_grad = dp_total(matmul(normed_all, shared_gate_pgrad, 0, 0).astype(BF16))
-    shared_up_grad = dp_total(matmul(normed_all, shared_up_pgrad, 0, 0).astype(BF16))
-    shared_down_grad = dp_total(matmul(shared_hidden, cot_all, 0, 0).astype(BF16))
-
-    shares, expert_grads = [], ()
-    for index, first in enumerate(range(0, experts, chunk)):
-        both_grad, down_grad, share, out_sum, dx_sum = run_experts(
-            rank, probs_rows, pre_own[index], pre_peer[index], back_own[index], back_peer[index],
-            token_rows[index], cot_rows[index], expert_gate, expert_up, expert_down, out_sum, dx_sum, first,
-        )
-        shares.append(share[:, 0])
-        both_half, both_rest = pair_halves(both_grad)
-        down_half, down_rest = pair_halves(down_grad)
-        expert_grads = spread(
-            core, both_half, both_rest, down_half, down_rest, expert_grads, first, experts
-        )
-
-    layer_out = (mixed_one + col_sum_rows(out_sum.astype(BF16))).astype(BF16)
-    cot_f = cotangent.astype(F32)
-    gate_grad = col_sum_rows(jnp.concatenate(shares, 0).T)
-    prob_grad = gate_grad + experts * count_total / (2.0 * tokens_all * tokens_all)
+    out_sum = out_sum + matmul(shared_hidden, shared_down, 1, 0)
+    dx_sum = (
+        dx_sum + matmul(shared_gate_pgrad, shared_gate, 1, 1) + matmul(shared_up_pgrad, shared_up, 1, 1)
+    )
+    shared_half = pair_half(
+        jnp.stack(
+            [
+                matmul(normed_all, shared_gate_pgrad, 0, 0).astype(BF16),
+                matmul(normed_all, shared_up_pgrad, 0, 0).astype(BF16),
+                matmul(cot_all, shared_hidden, 0, 0).astype(BF16),
+            ],
+            1,
+        )
+    )
+
+    share_rows = jnp.concatenate(shares, 0).reshape(experts, col_size, tok_rest).transpose(1, 0, 2)
+    dx_blocks = with_rows(dx_sum.astype(BF16).reshape(col_size, tok_rest, feat_dev), share_rows)
+    dx_blocks = col_sum_rows(dx_blocks.reshape(-1, feat_dev))
+    normed_grad, gate_grad = split_rows(dx_blocks, tok_rest, experts, tok_rest)
+    normed_grad = held(normed_grad, crossed[1], shared_half)
+    prob_grad = gate_grad.T + experts * count_total / (2.0 * tokens_all * tokens_all)
     logit_grad = router_probs * (prob_grad - jnp.sum(router_probs * prob_grad, -1, keepdims=True))
     router_grad = jnp.einsum("td,te->ed", unit_two * second_gain, logit_grad, precision=HIGHEST)
-
-    normed_grad = col_sum_rows(dx_sum.astype(BF16))
     two_grad = normed_grad + jnp.einsum("te,de->td", logit_grad, router_weight, precision=HIGHEST)
     gained_two = two_grad * second_gain
     second_gain_grad = jnp.sum(two_grad * unit_two, 0)
     inner_two = jnp.sum(gained_two * unit_two, 1, keepdims=True)
     inner_two = (inner_two + swap(inner_two, "row")) / feat_full
+    cot_f = cotangent.astype(F32)
     mixed_grad = cot_f + scale_two * (gained_two - unit_two * inner_two)
     mix_all = col_rows(mixed_grad.astype(BF16))
     attn_own = matmul(mix_all, attend_out, 1, 1).astype(BF16)
     attn_peer = swap(attn_own, "row")
+
+    expert_grads = ()
+    flags = []
+    for index, first in enumerate(firsts):
+        rest = swap(crossed[index], "dp", 1)
+        *expert_grads, flag = spread(core, crossed[index], rest, expert_grads, first, experts)
+        flags.append(flag)
+
+    layer_out = (
+        mixed_one + col_sum_rows(held(out_sum.astype(BF16), mix_all))
+    ).astype(BF16)
+    attn_peer = held(attn_peer, crossed[2], flags[0])
+    one_partial, attend_in_grad = attend_back(
+        attn_own, attn_peer, qkv, attended, log_total, cosine, sine, start, normed_own, attend_in, block
+    )
+    one_partial = held(one_partial, layer_out)
     heads = attended.shape[0]
     attn_rows = attended.astype(BF16)
     attend_out_grad = jnp.concatenate(
         [matmul(attn_rows[head], mix_all, 0, 0) for head in range(heads)], 0
     ).astype(BF16)
-    attend_out_grad = dp_total(attend_out_grad)
-    one_partial, attend_in_grad = attend_back(
-        attn_own, attn_peer, qkv, attended, log_total, cosine, sine, start, normed_own, attend_in, block
-    )
-    attend_in_grad = dp_total(attend_in_grad)
+    width = attend_in_grad.shape[1]
+    attend_half = pair_half(
+        jnp.concatenate([attend_in_grad, attend_out_grad.reshape(-1, width)], 0)
+    )
     first_gain_grad = jnp.sum(one_partial * unit_all, 0)
     one_grad = col_sum_rows(one_partial.astype(BF16))
     own_rows = col_index * tok_rest
@@ -1126,19 +1155,29 @@
     inner_one = jnp.sum(gained_one * unit_one, 1, keepdims=True)
     inner_one = (inner_one + swap(inner_one, "row")) / feat_full
     input_grad = (mixed_grad + scale_one * (gained_one - unit_one * inner_one)).astype(BF16)
-    early = sum_by_swaps(jnp.concatenate([second_gain_grad[None], router_grad], 0), ("dp", "col"))
-    first_gain_grad = sum_by_swaps(first_gain_grad, ("dp", "col"))
+
+    prob_sums = jnp.pad(jnp.sum(router_probs, 0), (0, feat_dev - experts))
+    totals = sum_by_swaps(
+        jnp.concatenate(
+            [first_gain_grad[None], second_gain_grad[None], prob_sums[None], router_grad], 0
+        ),
+        ("dp", "col"),
+    )
+    prob_total = totals[2, :experts]
+    balance_loss = experts * jnp.sum(count_total / (2.0 * tokens_all) * prob_total / tokens_all)
+    shared_grads = both_halves(cross_sum(shared_half))
+    attend_grads = both_halves(cross_sum(held(attend_half, crossed[3])))
     return (
         layer_out,
         input_grad,
-        first_gain_grad,
-        attend_in_grad,
-        attend_out_grad,
-        early[0],
-        early[1:].T,
-        shared_gate_grad,
-        shared_up_grad,
-        shared_down_grad,
+        totals[0],
+        attend_grads[:feat_dev],
+        attend_grads[feat_dev:].reshape(attend_out_grad.shape),
+        totals[1],
+        totals[3:].T,
+        shared_grads[:, 0],
+        shared_grads[:, 1],
+        shared_grads[:, 2].T,
         expert_grads[0],
         expert_grads[1],
         expert_grads[2],

time: 837 us -> 630 us (0.75)
  waiting for transfers between devices: 457 us -> 230 us
  local copies, waits for them, and re-layouts: 33.8 us -> 56.5 us
  starting transfers between devices: 101 us -> 85.4 us
  other arithmetic: 66.8 us -> 78.4 us
    ppermute x69 -> x40, waiting for transfers between devices: 383 us -> 192 us  [swap(): return lax.ppermute(value, axis, [(i, i ^ step) for i in range(size)])]
    ppermute x30 -> x24, waiting for transfers between devices: 74.6 us -> 38.8 us  [shifted(): lax.ppermute(value, axis, [(i, (i + step) % size) for i in range(size)])]
    dynamic_update_slice x22 -> x19, local copies, waits for them, and re-layouts: 5.61 us -> 14.3 us  [in_order(): whole = lax.dynamic_update_index_in_dim(whole, part, (me - step) % size, 0)]
    ppermute x30 -> x24, starting transfers between devices: 59.1 us -> 51.1 us  [shifted(): lax.ppermute(value, axis, [(i, (i + step) % size) for i in range(size)])]
    ppermute x69 -> x40, starting transfers between devices: 42.2 us -> 34.4 us  [swap(): return lax.ppermute(value, axis, [(i, i ^ step) for i in range(size)])]
    pallas_call x4 -> x1, Pallas kernels: 19.4 us -> 14.9 us  [back_hidden(): pl.pallas_call(back_hidden_kernel, grid=(count,), in_specs=[pl.BlockSpec(...]
    convert_element_type x33 -> x23, other arithmetic: 36.8 us -> 38.1 us  [the longest x6 18.5 us: cross_sum(): half = (half.astype(F32) + swap(half, 'dp', step).astype(F32)).astype(BF16)]
  transfers between devices with their start and end apart: 99 -> 64, of which waited for: 43 -> 27; matrix products, arithmetic and copies ran while one was open for 13% -> 24% of each run, Pallas kernels for 16% -> 20%
where the time goes in v2:
time: 630 us; the launch traced here: 624 us
  waiting for transfers between devices  230 us (37%)
  Pallas kernels  149 us (24%)
  starting transfers between devices  85.4 us (14%)
  other arithmetic  78.4 us (12%)
  local copies, waits for them, and re-layouts  56.5 us (9%)
  matrix products  20.6 us (3%)
    ppermute x40, waiting for transfers between devices, swap(): return lax.ppermute(value, axis, [(i, i ^ step) for i in range(size)])  192 us
    ppermute x24, starting transfers between devices, shifted(): lax.ppermute(value, axis, [(i, (i + step) % size) for i in range(size)])  51.1 us
    pallas_call x4, Pallas kernels, run_experts(): pl.pallas_call(experts_kernel, grid=(count,), in_specs=[at((1, tokens), f...  50.8 us
    ppermute x24, waiting for transfers between devices, shifted(): lax.ppermute(value, axis, [(i, (i + step) % size) for i in range(size)])  38.8 us
    ppermute x40, starting transfers between devices, swap(): return lax.ppermute(value, axis, [(i, i ^ step) for i in range(size)])  34.4 us
    pallas_call x4, Pallas kernels, spread(): pl.pallas_call(spread_kernel, grid_spec=pltpu.PrefetchScalarGridSpec(num_...  28.4 us
    pallas_call x4, Pallas kernels, open_experts(): pl.pallas_call(open_experts_kernel, grid=(count,), in_specs=[pl.BlockSpec...  22.9 us
    convert_element_type x6, other arithmetic, cross_sum(): half = (half.astype(F32) + swap(half, 'dp', step).astype(F32)).astype(BF16)  18.5 us
  transfers between devices with their start and end apart: 64, of which 27 were waited for; matrix products, arithmetic and copies ran while one was open for 24% of the time, Pallas kernels for 20%

profile of v2, /device:TPU:0, one launch (start us, length us, event | category | flops | bytes accessed | tf_op | source)
XLA Modules:
  0.0 624.3 jit_solution(1583602695690861894)
XLA Ops:
  0.7 5.1 collective-permute-start.2
  36.4 5.0 collective-permute-done.5
  53.7 14.7 %attend.1 = (bf16[9,1024,64]{2,1,0:T(8,128)(2,1)}, f32[3,1024,64]{2,1,0:T(8,128)}, f32[3,1024,1]{2,1,0:T(8,128)}, bf16[1024,384]{1,0:T(8,128)(2,1)}) custom-call(bf16[1024,384]{1,0:T(8,128)(2,1)} %get-tuple-element.214.left_ref.normed_ref, bf16[1024,384]{1,0:T(8,128)(2,1)} %get-tuple-element.213.right_ref, bf16[384,576]{1,0:T(8,128)(2,1)} %copy-done.22, ...), custom_call_target="tpu_custom_call" | custom-call | flops 1 | bytes 1 | tf_op jit(solution)/shard_map/attend/pallas_call | solution.py:678
  74.7 14.9 %back_hidden.1 = (bf16[16,192,512]{2,1,0:T(8,128)(2,1)}, bf16[16,192,384]{2,1,0:T(8,128)(2,1)}) custom-call(s32[16,1,1024]{2,1,0:T(1,128)} %broadcast_in_dim.134.rank_ref, bf16[1024,384]{1,0:T(8,128)(2,1)} %bitcast.247, bf16[16,512,384]{2,1,0:T(8,128)(2,1)} %down_ref.9), custom_call_target="tpu_custom_call" | custom-call | flops 1 | bytes 1 | tf_op jit(solution)/shard_map/back_hidden/pallas_call | solution.py:762
  107.7 6.0 collective-permute-done.16
  116.2 9.5 %dynamic_update_slice.77 = bf16[4,288,384]{2,0,1:T(4,128)(2,1)} dynamic-update-slice(bf16[4,288,384]{2,0,1:T(4,128)(2,1)} %copy.77, bf16[1,288,384]{2,0,1:T(2,128)(2,1)} %copy.78, s32[]{:T(128)S(6)} %select_n.238, s32[]{:T(128)} %constant.275.clone.1, s32[]{:T(128)} %constant.275.clone.1) | dynamic-update-slice | bytes 442372 | tf_op jit(solution)/shard_map/jit(dynamic_update_index_in_dim)/dynamic_update_slice | solution.py:540
  128.1 5.7 open_experts.7
  135.2 5.7 open_experts.6
  148.9 52.1 %collective-permute-done.21.pre_peer_ref = bf16[4,192,1024]{2,1,0:T(8,128)(2,1)} collective-permute-done((bf16[4,192,1024]{2,1,0:T(8,128)(2,1)}, bf16[4,192,1024]{2,1,0:T(8,128)(2,1)}, u32[]{:S(2)}, u32[]{:S(2)}) %collective-permute-start.21) | collective-permute-done | bytes 1572896 | tf_op jit(solution)/shard_map/ppermute | solution.py:528
  201.6 33.2 %collective-permute-done.18.pre_peer_ref = bf16[4,192,1024]{2,1,0:T(8,128)(2,1)} collective-permute-done((bf16[4,192,1024]{2,1,0:T(8,128)(2,1)}, bf16[4,192,1024]{2,1,0:T(8,128)(2,1)}, u32[]{:S(2)}, u32[]{:S(2)}) %collective-permute-start.18) | collective-permute-done | bytes 1572896 | tf_op jit(solution)/shard_map/ppermute | solution.py:528
  236.1 12.9 %run_experts.4 = (bf16[4,3,384,512]{3,2,1,0:T(8,128)(2,1)}, f32[4,1,1024]{2,1,0:T(1,128)}, f32[1024,384]{1,0:T(8,128)}, f32[1024,384]{1,0:T(8,128)}) custom-call(s32[16,1,1024]{2,1,0:T(1,128)} %broadcast_in_dim.134.rank_ref, f32[16,1,1024]{2,1,0:T(1,128)} %reshape.219.prob_ref, bf16[4,192,1024]{2,1,0:T(8,128)(2,1)} %get-tuple-element.83.pre_own_ref, ...), custom_call_target="tpu_custom_call" | custom-call | flops 1 | bytes 1 | tf_op jit(solution)/shard_map/run_experts/pallas_call | solution.py:868
  253.0 5.8 open_experts.5
  260.3 19.4 %collective-permute-done.27 = bf16[1024,1024]{1,0:T(8,128)(2,1)} collective-permute-done((bf16[1024,1024]{1,0:T(8,128)(2,1)}, bf16[1024,1024]{1,0:T(8,128)(2,1)}, u32[]{:S(2)}, u32[]{:S(2)}) %collective-permute-start.27) | collective-permute-done | bytes 2097184 | tf_op jit(solution)/shard_map/ppermute | solution.py:528
  287.9 12.6 %run_experts.5 = (bf16[4,3,384,512]{3,2,1,0:T(8,128)(2,1)}, f32[4,1,1024]{2,1,0:T(1,128)}, f32[1024,384]{1,0:T(8,128)}, f32[1024,384]{1,0:T(8,128)}) custom-call(s32[16,1,1024]{2,1,0:T(1,128)} %broadcast_in_dim.134.rank_ref, f32[16,1,1024]{2,1,0:T(1,128)} %reshape.219.prob_ref, bf16[4,192,1024]{2,1,0:T(8,128)(2,1)} %get-tuple-element.86.pre_own_ref, ...), custom_call_target="tpu_custom_call" | custom-call | flops 1 | bytes 1 | tf_op jit(solution)/shard_map/run_experts/pallas_call | solution.py:868
  314.4 15.4 %collective-permute-done.19.pre_peer_ref = bf16[4,192,1024]{2,1,0:T(8,128)(2,1)} collective-permute-done((bf16[4,192,1024]{2,1,0:T(8,128)(2,1)}, bf16[4,192,1024]{2,1,0:T(8,128)(2,1)}, u32[]{:S(2)}, u32[]{:S(2)}) %collective-permute-start.19) | collective-permute-done | bytes 1572896 | tf_op jit(solution)/shard_map/ppermute | solution.py:528
  329.8 12.5 %run_experts.6 = (bf16[4,3,384,512]{3,2,1,0:T(8,128)(2,1)}, f32[4,1,1024]{2,1,0:T(1,128)}, f32[1024,384]{1,0:T(8,128)}, f32[1024,384]{1,0:T(8,128)}) custom-call(s32[16,1,1024]{2,1,0:T(1,128)} %broadcast_in_dim.134.rank_ref, f32[16,1,1024]{2,1,0:T(1,128)} %reshape.219.prob_ref, bf16[4,192,1024]{2,1,0:T(8,128)(2,1)} %get-tuple-element.84.pre_own_ref, ...), custom_call_target="tpu_custom_call" | custom-call | flops 1 | bytes 1 | tf_op jit(solution)/shard_map/run_experts/pallas_call | solution.py:868
  352.1 22.2 %collective-permute-done.35 = f32[16]{0:T(128)S(1)} collective-permute-done((f32[16]{0:T(128)S(1)}, f32[16]{0:T(128)S(1)}, u32[]{:S(2)}, u32[]{:S(2)}) %collective-permute-start.35) | collective-permute-done | bytes 96 | tf_op jit(solution)/shard_map/ppermute | solution.py:528
  377.8 5.7 open_experts.4
  385.7 4.6 add_convert_fusion.3.half_ref
  405.0 14.0 %collective-permute-done.20.pre_peer_ref = bf16[4,192,1024]{2,1,0:T(8,128)(2,1)} collective-permute-done((bf16[4,192,1024]{2,1,0:T(8,128)(2,1)}, bf16[4,192,1024]{2,1,0:T(8,128)(2,1)}, u32[]{:S(2)}, u32[]{:S(2)}) %collective-permute-start.20) | collective-permute-done | bytes 1572896 | tf_op jit(solution)/shard_map/ppermute | solution.py:528
  419.1 12.7 %run_experts.7 = (bf16[4,3,384,512]{3,2,1,0:T(8,128)(2,1)}, f32[4,1,1024]{2,1,0:T(1,128)}, f32[1024,384]{1,0:T(8,128)}, f32[1024,384]{1,0:T(8,128)}) custom-call(s32[16,1,1024]{2,1,0:T(1,128)} %broadcast_in_dim.134.rank_ref, f32[16,1,1024]{2,1,0:T(1,128)} %reshape.219.prob_ref, bf16[4,192,1024]{2,1,0:T(8,128)(2,1)} %get-tuple-element.85.pre_own_ref, ...), custom_call_target="tpu_custom_call" | custom-call | flops 1 | bytes 1 | tf_op jit(solution)/shard_map/run_experts/pallas_call | solution.py:868
  456.3 7.1 %spread.4 = (f32[16,384,512]{2,1,0:T(8,128)}, f32[16,384,512]{2,1,0:T(8,128)}, f32[16,512,384]{2,1,0:T(8,128)}, f32[8,128]{1,0:T(8,128)}) custom-call(s32[1]{0:T(128)} %bitcast.91.core_ref, bf16[2,3,384,512]{3,2,1,0:T(8,128)(2,1)} %add_convert_fusion.3.half_ref, bf16[2,3,384,512]{3,2,1,0:T(8,128)(2,1)} %collective-permute-done.63.rest_ref), custom_call_target="tpu_custom_call" | custom-call | flops 1 | bytes 1 | tf_op jit(solution)/shard_map/spread/pallas_call | solution.py:933
  468.6 4.7 collective-permute-start.37
  483.6 5.5 collective-permute-done.38
  489.1 10.4 %collective-permute-done.44 = bf16[2,3,384,512]{3,2,1,0:T(8,128)(2,1)} collective-permute-done((bf16[2,3,384,512]{3,2,1,0:T(8,128)(2,1)}, bf16[2,3,384,512]{3,2,1,0:T(8,128)(2,1)}, u32[]{:S(2)}, u32[]{:S(2)}) %collective-permute-start.44) | collective-permute-done | bytes 2359328 | tf_op jit(solution)/shard_map/ppermute | solution.py:528
  523.0 6.0 collective-permute-start.41
  529.9 4.8 collective-permute-done.41
  536.3 17.1 %attend_back.1 = (f32[1024,384]{1,0:T(8,128)}, bf16[384,576]{1,0:T(8,128)(2,1)}) custom-call(bf16[1024,192]{1,0:T(8,128)(2,1)} %copy-done.34, bf16[1024,192]{1,0:T(8,128)(2,1)} %copy-done.47, bf16[9,1024,64]{2,1,0:T(8,128)(2,1)} %get-tuple-element.117.qkv_ref, f32[3,1024,64]{2,1,0:T(8,128)} %get-tuple-element.118.attended_ref, ...), custom_call_target="tpu_custom_call" | custom-call | flops 1 | bytes 1 | tf_op jit(solution)/shard_map/attend_back/pallas_call | solution.py:731
  577.4 7.2 %spread.5 = (f32[16,384,512]{2,1,0:T(8,128)}, f32[16,384,512]{2,1,0:T(8,128)}, f32[16,512,384]{2,1,0:T(8,128)}, f32[8,128]{1,0:T(8,128)}) custom-call(s32[1]{0:T(128)} %bitcast.91.core_ref, bf16[2,3,384,512]{3,2,1,0:T(8,128)(2,1)} %copy-done.10, ...), custom_call_target="tpu_custom_call", output_to_operand_aliasing={{0}: (3, {}), {1}: (4, {}), {2}: (5, {})} | custom-call | flops 1 | bytes 1 | tf_op jit(solution)/shard_map/spread/pallas_call | solution.py:933
  594.5 5.2 collective-permute-done.46
  606.5 7.1 %spread.6 = (f32[16,384,512]{2,1,0:T(8,128)}, f32[16,384,512]{2,1,0:T(8,128)}, f32[16,512,384]{2,1,0:T(8,128)}, f32[8,128]{1,0:T(8,128)}) custom-call(s32[1]{0:T(128)} %bitcast.91.core_ref, bf16[2,3,384,512]{3,2,1,0:T(8,128)(2,1)} %add_convert_fusion.1.half_ref, ...), custom_call_target="tpu_custom_call", output_to_operand_aliasing={{0}: (3, {}), {1}: (4, {}), {2}: (5, {})} | custom-call | flops 1 | bytes 1 | tf_op jit(solution)/shard_map/spread/pallas_call | solution.py:933
  615.8 7.1 %spread.7 = (f32[16,384,512]{2,1,0:T(8,128)}, f32[16,384,512]{2,1,0:T(8,128)}, f32[16,512,384]{2,1,0:T(8,128)}, f32[8,128]{1,0:T(8,128)}) custom-call(s32[1]{0:T(128)} %bitcast.91.core_ref, bf16[2,3,384,512]{3,2,1,0:T(8,128)(2,1)} %add_convert_fusion.half_ref, ...), custom_call_target="tpu_custom_call", output_to_operand_aliasing={{0}: (3, {}), {1}: (4, {}), {2}: (5, {})} | custom-call | flops 1 | bytes 1 | tf_op jit(solution)/shard_map/spread/pallas_call | solution.py:933
  (467 shorter events, 248.2 us)
Async XLA Ops:
  0.7 18.4 %collective-permute-start.2 = (bf16[256,384]{1,0:T(8,128)(2,1)}, bf16[256,384]{1,0:T(8,128)(2,1)S(1)}, u32[]{:S(2)}, u32[]{:S(2)}) collective-permute-start(bf16[256,384]{1,0:T(8,128)(2,1)} %param.15), channel_id=1, source_target_pairs={{0,3},{1,0},{2,1},{3,2},{4,7},{5,4},{6,5},{7,6},{8,11},{9,8},{10,9... | collective-permute-start | bytes 589832 | tf_op jit(solution)/shard_map/ppermute | solution.py:533
  8.6 20.4 %collective-permute-start.3 = (bf16[264,384]{1,0:T(8,128)(2,1)S(1)}, bf16[264,384]{1,0:T(8,128)(2,1)S(1)}, u32[]{:S(2)}, u32[]{:S(2)}) collective-permute-start(bf16[264,384]{1,0:T(8,128)(2,1)S(1)} %pad_maximum_fusion.4), channel_id=1, source_target_pairs={{0,4},{4,0},{1,5},{5,1},{2,6},{6,2},{3,7},{7,3},{8,12},{12,8},{9,1... | collective-permute-start | bytes 608264 | tf_op jit(solution)/shard_map/ppermute | solution.py:528
  11.4 41.5 %collective-permute-start.7 = (bf16[384,576]{1,0:T(8,128)(2,1)S(1)}, bf16[384,576]{1,0:T(8,128)(2,1)S(1)}, u32[]{:S(2)}, u32[]{:S(2)}) collective-permute-start(bf16[384,576]{1,0:T(8,128)(2,1)S(1)} %copy.76.weight_left_ref.weight_ref), channel_id=1, source_target_pairs={{0,4},{4,0},{1,5},{5,1},{2,6},{6,2},{3,7},{7,3},{8,12},{12,8},{9,1... | collective-permute-start | bytes 1327112 | tf_op jit(solution)/shard_map/ppermute | solution.py:528
  22.7 26.8 %collective-permute-start.13 = (bf16[256,384]{1,0:T(8,128)(2,1)S(1)}, bf16[256,384]{1,0:T(8,128)(2,1)}, u32[]{:S(2)}, u32[]{:S(2)}) collective-permute-start(bf16[256,384]{1,0:T(8,128)(2,1)S(1)} %copy-done.42), channel_id=1, source_target_pairs={{0,3},{1,0},{2,1},{3,2},{4,7},{5,4},{6,5},{7,6},{8,11},{9,8},{10,9... | collective-permute-start | bytes 589832 | tf_op jit(solution)/shard_map/ppermute | solution.py:533
  23.1 25.5 %collective-permute-start.12 = (bf16[256,384]{1,0:T(8,128)(2,1)S(1)}, bf16[256,384]{1,0:T(8,128)(2,1)}, u32[]{:S(2)}, u32[]{:S(2)}) collective-permute-start(bf16[256,384]{1,0:T(8,128)(2,1)S(1)} %copy-done.42), channel_id=1, source_target_pairs={{0,2},{1,3},{2,0},{3,1},{4,6},{5,7},{6,4},{7,5},{8,10},{9,11},{10,... | collective-permute-start | bytes 589832 | tf_op jit(solution)/shard_map/ppermute | solution.py:533
  25.6 22.0 %collective-permute-start.11 = (bf16[256,384]{1,0:T(8,128)(2,1)S(1)}, bf16[256,384]{1,0:T(8,128)(2,1)}, u32[]{:S(2)}, u32[]{:S(2)}) collective-permute-start(bf16[256,384]{1,0:T(8,128)(2,1)S(1)} %copy-done.42), channel_id=1, source_target_pairs={{0,1},{1,2},{2,3},{3,0},{4,5},{5,6},{6,7},{7,4},{8,9},{9,10},{10,1... | collective-permute-start | bytes 589832 | tf_op jit(solution)/shard_map/ppermute | solution.py:533
  70.4 22.4 %collective-permute-start.8 = (bf16[256,384]{1,0:T(8,128)(2,1)}, bf16[256,384]{1,0:T(8,128)(2,1)}, u32[]{:S(2)}, u32[]{:S(2)}) collective-permute-start(bf16[256,384]{1,0:T(8,128)(2,1)} %get-tuple-element.200), channel_id=1, source_target_pairs={{0,1},{1,2},{2,3},{3,0},{4,5},{5,6},{6,7},{7,4},{8,9},{9,10},{10,1... | collective-permute-start | bytes 589832 | tf_op jit(solution)/shard_map/ppermute | solution.py:533
  70.4 22.4 %collective-permute-start.10 = (bf16[256,384]{1,0:T(8,128)(2,1)}, bf16[256,384]{1,0:T(8,128)(2,1)}, u32[]{:S(2)}, u32[]{:S(2)}) collective-permute-start(bf16[256,384]{1,0:T(8,128)(2,1)} %get-tuple-element.201), channel_id=1, source_target_pairs={{0,3},{1,0},{2,1},{3,2},{4,7},{5,4},{6,5},{7,6},{8,11},{9,8},{10,9... | collective-permute-start | bytes 589832 | tf_op jit(solution)/shard_map/ppermute | solution.py:533
  74.7 18.1 %collective-permute-start.9 = (bf16[256,384]{1,0:T(8,128)(2,1)}, bf16[256,384]{1,0:T(8,128)(2,1)}, u32[]{:S(2)}, u32[]{:S(2)}) collective-permute-start(bf16[256,384]{1,0:T(8,128)(2,1)} %get-tuple-element.202), channel_id=1, source_target_pairs={{0,2},{1,3},{2,0},{3,1},{4,6},{5,7},{6,4},{7,5},{8,10},{9,11},{10,... | collective-permute-start | bytes 589832 | tf_op jit(solution)/shard_map/ppermute | solution.py:533
  96.3 138.5 %collective-permute-start.22 = (bf16[16,192,512]{2,1,0:T(8,128)(2,1)S(1)}, bf16[16,192,512]{2,1,0:T(8,128)(2,1)}, u32[]{:S(2)}, u32[]{:S(2)}) collective-permute-start(bf16[16,192,512]{2,1,0:T(8,128)(2,1)S(1)} %copy-done.2), channel_id=1, source_target_pairs={{0,4},{4,0},{1,5},{5,1},{2,6},{6,2},{3,7},{7,3},{8,12},{12,8},{9,1... | collective-permute-start | bytes 9437192 | tf_op jit(solution)/shard_map/ppermute | solution.py:528
  133.7 67.3 %collective-permute-start.21 = (bf16[4,192,1024]{2,1,0:T(8,128)(2,1)}, bf16[4,192,1024]{2,1,0:T(8,128)(2,1)}, u32[]{:S(2)}, u32[]{:S(2)}) collective-permute-start(bf16[4,192,1024]{2,1,0:T(8,128)(2,1)} %get-tuple-element.86.pre_own_ref), channel_id=1, source_target_pairs={{0,4},{4,0},{1,5},{5,1},{2,6},{6,2},{3,7},{7,3},{8,12},{12,8},{9,1... | collective-permute-start | bytes 4718600 | tf_op jit(solution)/shard_map/ppermute | solution.py:528
  140.9 93.9 %collective-permute-start.18 = (bf16[4,192,1024]{2,1,0:T(8,128)(2,1)}, bf16[4,192,1024]{2,1,0:T(8,128)(2,1)}, u32[]{:S(2)}, u32[]{:S(2)}) collective-permute-start(bf16[4,192,1024]{2,1,0:T(8,128)(2,1)} %get-tuple-element.83.pre_own_ref), channel_id=1, source_target_pairs={{0,4},{4,0},{1,5},{5,1},{2,6},{6,2},{3,7},{7,3},{8,12},{12,8},{9,1... | collective-permute-start | bytes 4718600 | tf_op jit(solution)/shard_map/ppermute | solution.py:528
  201.1 78.6 %collective-permute-start.27 = (bf16[1024,1024]{1,0:T(8,128)(2,1)}, bf16[1024,1024]{1,0:T(8,128)(2,1)}, u32[]{:S(2)}, u32[]{:S(2)}) collective-permute-start(bf16[1024,1024]{1,0:T(8,128)(2,1)} %pad_maximum_fusion), channel_id=1, source_target_pairs={{0,4},{4,0},{1,5},{5,1},{2,6},{6,2},{3,7},{7,3},{8,12},{12,8},{9,1... | collective-permute-start | bytes 6291464 | tf_op jit(solution)/shard_map/ppermute | solution.py:528
  252.5 31.6 %collective-permute-start.23 = (bf16[2,3,384,512]{3,2,1,0:T(8,128)(2,1)}, bf16[2,3,384,512]{3,2,1,0:T(8,128)(2,1)}, u32[]{:S(2)}, u32[]{:S(2)}) collective-permute-start(bf16[2,3,384,512]{3,2,1,0:T(8,128)(2,1)} %dynamic-slice_bitcast_fusion.3), channel_id=1, source_target_pairs={{0,8},{8,0},{16,24},{24,16},{1,9},{9,1},{17,25},{25,17},{2,10},{10... | collective-permute-start | bytes 7077896 | tf_op jit(solution)/shard_map/ppermute | solution.py:528
  252.5 50.2 %collective-permute-start.28 = (bf16[1024,512]{1,0:T(8,128)(2,1)S(1)}, bf16[1024,512]{1,0:T(8,128)(2,1)}, u32[]{:S(2)}, u32[]{:S(2)}) collective-permute-start(bf16[1024,512]{1,0:T(8,128)(2,1)S(1)} %copy-done.27), channel_id=1, source_target_pairs={{0,4},{4,0},{1,5},{5,1},{2,6},{6,2},{3,7},{7,3},{8,12},{12,8},{9,1... | collective-permute-start | bytes 3145736 | tf_op jit(solution)/shard_map/ppermute | solution.py:528
  258.8 70.9 %collective-permute-start.19 = (bf16[4,192,1024]{2,1,0:T(8,128)(2,1)}, bf16[4,192,1024]{2,1,0:T(8,128)(2,1)}, u32[]{:S(2)}, u32[]{:S(2)}) collective-permute-start(bf16[4,192,1024]{2,1,0:T(8,128)(2,1)} %get-tuple-element.84.pre_own_ref), channel_id=1, source_target_pairs={{0,4},{4,0},{1,5},{5,1},{2,6},{6,2},{3,7},{7,3},{8,12},{12,8},{9,1... | collective-permute-start | bytes 4718600 | tf_op jit(solution)/shard_map/ppermute | solution.py:528
  308.4 77.3 %collective-permute-start.26 = (bf16[2,3,384,512]{3,2,1,0:T(8,128)(2,1)}, bf16[2,3,384,512]{3,2,1,0:T(8,128)(2,1)}, u32[]{:S(2)}, u32[]{:S(2)}) collective-permute-start(bf16[2,3,384,512]{3,2,1,0:T(8,128)(2,1)} %fusion.3), channel_id=1, source_target_pairs={{0,16},{8,24},{16,0},{24,8},{1,17},{9,25},{17,1},{25,9},{2,18},{10... | collective-permute-start | bytes 7077896 | tf_op jit(solution)/shard_map/ppermute | solution.py:528
  313.0 71.1 %collective-permute-start.58 = (bf16[192,3,512]{2,0,1:T(8,128)(2,1)S(1)}, bf16[192,3,512]{2,0,1:T(8,128)(2,1)}, u32[]{:S(2)}, u32[]{:S(2)}) collective-permute-start(bf16[192,3,512]{2,0,1:T(8,128)(2,1)S(1)} %fusion.8), channel_id=1, source_target_pairs={{0,16},{8,24},{16,0},{24,8},{1,17},{9,25},{17,1},{25,9},{2,18},{10... | collective-permute-start | bytes 1769480 | tf_op jit(solution)/shard_map/ppermute | solution.py:528
  345.7 54.8 %collective-permute-start.25 = (bf16[2,3,384,512]{3,2,1,0:T(8,128)(2,1)}, bf16[2,3,384,512]{3,2,1,0:T(8,128)(2,1)}, u32[]{:S(2)}, u32[]{:S(2)}) collective-permute-start(bf16[2,3,384,512]{3,2,1,0:T(8,128)(2,1)} %dynamic-slice_bitcast_fusion.1), channel_id=1, source_target_pairs={{0,8},{8,0},{16,24},{24,16},{1,9},{9,1},{17,25},{25,17},{2,10},{10... | collective-permute-start | bytes 7077896 | tf_op jit(solution)/shard_map/ppermute | solution.py:528
  350.5 23.7 %collective-permute-start.35 = (f32[16]{0:T(128)S(1)}, f32[16]{0:T(128)S(1)}, u32[]{:S(2)}, u32[]{:S(2)}) collective-permute-start(f32[16]{0:T(128)S(1)} %add.429), channel_id=1, source_target_pairs={{0,16},{8,24},{16,0},{24,8},{1,17},{9,25},{17,1},{25,9},{2,18},{10... | collective-permute-start | bytes 200 | tf_op jit(solution)/shard_map/ppermute | solution.py:528
  383.5 35.5 %collective-permute-start.20 = (bf16[4,192,1024]{2,1,0:T(8,128)(2,1)}, bf16[4,192,1024]{2,1,0:T(8,128)(2,1)}, u32[]{:S(2)}, u32[]{:S(2)}) collective-permute-start(bf16[4,192,1024]{2,1,0:T(8,128)(2,1)} %get-tuple-element.85.pre_own_ref), channel_id=1, source_target_pairs={{0,4},{4,0},{1,5},{5,1},{2,6},{6,2},{3,7},{7,3},{8,12},{12,8},{9,1... | collective-permute-start | bytes 4718600 | tf_op jit(solution)/shard_map/ppermute | solution.py:528
  390.3 53.7 %collective-permute-start.32 = (bf16[2,3,384,512]{3,2,1,0:T(8,128)(2,1)S(1)}, bf16[2,3,384,512]{3,2,1,0:T(8,128)(2,1)}, u32[]{:S(2)}, u32[]{:S(2)}) collective-permute-start(bf16[2,3,384,512]{3,2,1,0:T(8,128)(2,1)S(1)} %fusion.2), channel_id=1, source_target_pairs={{0,16},{8,24},{16,0},{24,8},{1,17},{9,25},{17,1},{25,9},{2,18},{10... | collective-permute-start | bytes 7077896 | tf_op jit(solution)/shard_map/ppermute | solution.py:528
  400.3 56.1 %collective-permute-start.63 = (bf16[2,3,384,512]{3,2,1,0:T(8,128)(2,1)}, bf16[2,3,384,512]{3,2,1,0:T(8,128)(2,1)}, u32[]{:S(2)}, u32[]{:S(2)}) collective-permute-start(bf16[2,3,384,512]{3,2,1,0:T(8,128)(2,1)} %add_convert_fusion.3.half_ref), channel_id=1, source_target_pairs={{0,8},{8,0},{16,24},{24,16},{1,9},{9,1},{17,25},{25,17},{2,10},{10... | collective-permute-start | bytes 7077896 | tf_op jit(solution)/shard_map/ppermute | solution.py:528
  446.4 53.1 %collective-permute-start.44 = (bf16[2,3,384,512]{3,2,1,0:T(8,128)(2,1)}, bf16[2,3,384,512]{3,2,1,0:T(8,128)(2,1)}, u32[]{:S(2)}, u32[]{:S(2)}) collective-permute-start(bf16[2,3,384,512]{3,2,1,0:T(8,128)(2,1)} %fusion.1), channel_id=1, source_target_pairs={{0,16},{8,24},{16,0},{24,8},{1,17},{9,25},{17,1},{25,9},{2,18},{10... | collective-permute-start | bytes 7077896 | tf_op jit(solution)/shard_map/ppermute | solution.py:528
  449.8 126.9 %collective-permute-start.62 = (bf16[2,3,384,512]{3,2,1,0:T(8,128)(2,1)S(1)}, bf16[2,3,384,512]{3,2,1,0:T(8,128)(2,1)}, u32[]{:S(2)}, u32[]{:S(2)}) collective-permute-start(bf16[2,3,384,512]{3,2,1,0:T(8,128)(2,1)S(1)} %add_convert_fusion.2.half_ref), channel_id=1, source_target_pairs={{0,8},{8,0},{16,24},{24,16},{1,9},{9,1},{17,25},{25,17},{2,10},{10... | collective-permute-start | bytes 7077896 | tf_op jit(solution)/shard_map/ppermute | solution.py:528
  452.7 51.4 %collective-permute-start.54 = (bf16[2,3,384,512]{3,2,1,0:T(8,128)(2,1)}, bf16[2,3,384,512]{3,2,1,0:T(8,128)(2,1)}, u32[]{:S(2)}, u32[]{:S(2)}) collective-permute-start(bf16[2,3,384,512]{3,2,1,0:T(8,128)(2,1)} %dynamic-slice_bitcast_fusion), channel_id=1, source_target_pairs={{0,8},{8,0},{16,24},{24,16},{1,9},{9,1},{17,25},{25,17},{2,10},{10... | collective-permute-start | bytes 7077896 | tf_op jit(solution)/shard_map/ppermute | solution.py:528
  481.1 29.1 %collective-permute-start.39 = (bf16[256,384]{1,0:T(8,128)(2,1)S(1)}, bf16[256,384]{1,0:T(8,128)(2,1)S(1)}, u32[]{:S(2)}, u32[]{:S(2)}) collective-permute-start(bf16[256,384]{1,0:T(8,128)(2,1)S(1)} %get-tuple-element.173), channel_id=1, source_target_pairs={{0,3},{1,0},{2,1},{3,2},{4,7},{5,4},{6,5},{7,6},{8,11},{9,8},{10,9... | collective-permute-start | bytes 589832 | tf_op jit(solution)/shard_map/ppermute | solution.py:533
  508.7 52.2 %collective-permute-start.55 = (bf16[2,3,384,512]{3,2,1,0:T(8,128)(2,1)}, bf16[2,3,384,512]{3,2,1,0:T(8,128)(2,1)}, u32[]{:S(2)}, u32[]{:S(2)}) collective-permute-start(bf16[2,3,384,512]{3,2,1,0:T(8,128)(2,1)} %fusion), channel_id=1, source_target_pairs={{0,16},{8,24},{16,0},{24,8},{1,17},{9,25},{17,1},{25,9},{2,18},{10... | collective-permute-start | bytes 7077896 | tf_op jit(solution)/shard_map/ppermute | solution.py:528
  510.7 24.8 %collective-permute-start.43 = (bf16[1024,192]{1,0:T(8,128)(2,1)S(1)}, bf16[1024,192]{1,0:T(8,128)(2,1)S(1)}, u32[]{:S(2)}, u32[]{:S(2)}) collective-permute-start(bf16[1024,192]{1,0:T(8,128)(2,1)S(1)} %convolution_convert_fusion.3.own_ref), channel_id=1, source_target_pairs={{0,4},{4,0},{1,5},{5,1},{2,6},{6,2},{3,7},{7,3},{8,12},{12,8},{9,1... | collective-permute-start | bytes 1179656 | tf_op jit(solution)/shard_map/ppermute | solution.py:528
  557.7 48.8 %collective-permute-start.61 = (bf16[2,3,384,512]{3,2,1,0:T(8,128)(2,1)}, bf16[2,3,384,512]{3,2,1,0:T(8,128)(2,1)}, u32[]{:S(2)}, u32[]{:S(2)}) collective-permute-start(bf16[2,3,384,512]{3,2,1,0:T(8,128)(2,1)} %add_convert_fusion.1.half_ref), channel_id=1, source_target_pairs={{0,8},{8,0},{16,24},{24,16},{1,9},{9,1},{17,25},{25,17},{2,10},{10... | collective-permute-start | bytes 7077896 | tf_op jit(solution)/shard_map/ppermute | solution.py:528
  565.4 50.4 %collective-permute-start.60 = (bf16[2,3,384,512]{3,2,1,0:T(8,128)(2,1)}, bf16[2,3,384,512]{3,2,1,0:T(8,128)(2,1)}, u32[]{:S(2)}, u32[]{:S(2)}) collective-permute-start(bf16[2,3,384,512]{3,2,1,0:T(8,128)(2,1)} %add_convert_fusion.half_ref), channel_id=1, source_target_pairs={{0,8},{8,0},{16,24},{24,16},{1,9},{9,1},{17,25},{25,17},{2,10},{10... | collective-permute-start | bytes 7077896 | tf_op jit(solution)/shard_map/ppermute | solution.py:528
  569.8 19.4 %collective-permute-start.53 = (bf16[256,576]{0,1:T(8,128)(2,1)}, bf16[256,576]{0,1:T(8,128)(2,1)}, u32[]{:S(2)}, u32[]{:S(2)}) collective-permute-start(bf16[256,576]{0,1:T(8,128)(2,1)} %bitcast.273), channel_id=1, source_target_pairs={{0,8},{8,0},{16,24},{24,16},{1,9},{9,1},{17,25},{25,17},{2,10},{10... | collective-permute-start | bytes 884744 | tf_op jit(solution)/shard_map/ppermute | solution.py:528
  (129 other events, 1703.3 us)

commit v3 on v2

--- a/solution.py
+++ b/solution.py
@@ -569,6 +569,10 @@
     return value
 
 
+def stage(*values):
+    return lax.optimization_barrier(values)
+
+
 def held(value, *others):
     return lax.optimization_barrier((value,) + others)[0]
 
@@ -588,6 +592,44 @@
 def split_rows(value, count, extra, width):
     tail = value[..., count:, :width].astype(F32)
     return value[..., :count, :], tail[..., :extra, :] + tail[..., extra:, :]
+
+
+def add_kernel(one_ref, two_ref, *sum_refs):
+    total = (one_ref[...].astype(F32) + two_ref[...].astype(F32)).astype(BF16)
+    for index, sum_ref in enumerate(sum_refs):
+        pl.when(pl.program_id(0) == index)(lambda sum_ref=sum_ref: sum_ref.__setitem__(Ellipsis, total))
+
+
+def added(one, two):
+    steps = one.shape[0]
+    shape = (1,) + one.shape[1:]
+    spec = pl.BlockSpec(shape, lambda i: (i,) + (0,) * (one.ndim - 1))
+    return pl.pallas_call(
+        add_kernel,
+        grid=(steps,),
+        in_specs=[spec, spec],
+        out_specs=[whole_block(shape)] * steps,
+        out_shape=[jax.ShapeDtypeStruct(shape, BF16)] * steps,
+        cost_estimate=LIGHT,
+        name="added",
+    )(one, two)
+
+
+def join_kernel(one_ref, two_ref, pair_ref):
+    pl.when(pl.program_id(0) == 0)(lambda: pair_ref.__setitem__(Ellipsis, one_ref[...]))
+    pl.when(pl.program_id(0) == 1)(lambda: pair_ref.__setitem__(Ellipsis, two_ref[...]))
+
+
+def joined(one, two):
+    return pl.pallas_call(
+        join_kernel,
+        grid=(2,),
+        in_specs=[whole_block(one.shape)] * 2,
+        out_specs=pl.BlockSpec(one.shape, lambda i: (i,) + (0,) * (one.ndim - 1)),
+        out_shape=jax.ShapeDtypeStruct((2,) + one.shape[1:], BF16),
+        cost_estimate=LIGHT,
+        name="joined",
+    )(one, two)
 
 
 def pair_half(whole):
@@ -596,6 +638,17 @@
     mine = lax.dynamic_index_in_dim(halves, core, 0, False)
     other = lax.dynamic_index_in_dim(halves, 1 - core, 0, False)
     return (mine.astype(F32) + swap(other, "dp", 1).astype(F32)).astype(BF16)
+
+
+def sent_back(blocks):
+    return [blocks[0]] + [shifted(blocks[step], "col", -step) for step in range(1, len(blocks))]
+
+
+def summed_up(blocks):
+    total = blocks[0].astype(F32)
+    for block in blocks[1:]:
+        total = total + block.astype(F32)
+    return total
 
 
 def cross_sum(half):
@@ -749,69 +802,37 @@
     return jnp.where(mask, 1.0, 0.0).astype(BF16)
 
 
-def back_hidden_kernel(rank_ref, cot_ref, down_ref, grad_ref, rows_ref):
-    chosen = ones_where(picks(rank_ref, rows_ref.shape[1]))
-    rows = jnp.dot(chosen, cot_ref[...], preferred_element_type=F32).astype(BF16)
-    rows_ref[0] = rows
-    grad_ref[0] = matmul(rows, down_ref[0], 1, 1).astype(BF16)
-
-
-def back_hidden(rank, cot_rows, down, first, count, capacity):
-    tokens, features = cot_rows.shape
-    hidden = down.shape[1]
+def pack_kernel(place_ref, gate_ref, up_ref, down_ref, out_ref):
+    out_ref[0, 0] = gate_ref[0]
+    out_ref[0, 1] = up_ref[0]
+    out_ref[0, 2] = down_ref[0].astype(F32).T.astype(BF16)
+
+
+def pack(place, gate, up, down, first, count, parts):
+    features, hidden = gate.shape[1], gate.shape[2] // parts
+
+    def row_place(i, place):
+        return (0, place[i], 0) if parts > 1 else (first + place[i], 0, 0)
+
+    def lane_place(i, place):
+        return (0, 0, place[i]) if parts > 1 else (first + place[i], 0, 0)
+
     return pl.pallas_call(
-        back_hidden_kernel,
-        grid=(count,),
-        in_specs=[
-            pl.BlockSpec((1, 1, tokens), lambda i: (first + i, 0, 0)),
-            whole_block((tokens, features)),
-            pl.BlockSpec((1, hidden, features), lambda i: (first + i, 0, 0)),
-        ],
-        out_specs=(
-            pl.BlockSpec((1, capacity, hidden), lambda i: (i, 0, 0)),
-            pl.BlockSpec((1, capacity, features), lambda i: (i, 0, 0)),
+        pack_kernel,
+        grid_spec=pltpu.PrefetchScalarGridSpec(
+            num_scalar_prefetch=1,
+            grid=(count,),
+            in_specs=[
+                pl.BlockSpec((1, features, hidden), lane_place),
+                pl.BlockSpec((1, features, hidden), lane_place),
+                pl.BlockSpec((1, hidden, features), row_place),
+            ],
+            out_specs=pl.BlockSpec((1, 3, features, hidden), lambda i, place: (i, 0, 0, 0)),
         ),
-        out_shape=(
-            jax.ShapeDtypeStruct((count, capacity, hidden), BF16),
-            jax.ShapeDtypeStruct((count, capacity, features), BF16),
-        ),
+        out_shape=jax.ShapeDtypeStruct((count, 3, features, hidden), BF16),
         cost_estimate=LIGHT,
-        name="back_hidden",
-    )(rank, cot_rows, down)
-
-
-def open_experts_kernel(rank_ref, token_ref, gate_ref, up_ref, pre_ref, rows_ref):
-    hidden = gate_ref.shape[2]
-    chosen = ones_where(picks(rank_ref, rows_ref.shape[1]))
-    rows = jnp.dot(chosen, token_ref[...], preferred_element_type=F32).astype(BF16)
-    rows_ref[0] = rows
-    pre_ref[0, :, :hidden] = jnp.dot(rows, gate_ref[0], preferred_element_type=F32).astype(BF16)
-    pre_ref[0, :, hidden:] = jnp.dot(rows, up_ref[0], preferred_element_type=F32).astype(BF16)
-
-
-def open_experts(rank, token_rows, gate, up, first, count, capacity):
-    tokens, features = token_rows.shape
-    hidden = gate.shape[2]
-    return pl.pallas_call(
-        open_experts_kernel,
-        grid=(count,),
-        in_specs=[
-            pl.BlockSpec((1, 1, tokens), lambda i: (first + i, 0, 0)),
-            whole_block((tokens, features)),
-            pl.BlockSpec((1, features, hidden), lambda i: (first + i, 0, 0)),
-            pl.BlockSpec((1, features, hidden), lambda i: (first + i, 0, 0)),
-        ],
-        out_specs=(
-            pl.BlockSpec((1, capacity, 2 * hidden), lambda i: (i, 0, 0)),
-            pl.BlockSpec((1, capacity, features), lambda i: (i, 0, 0)),
-        ),
-        out_shape=(
-            jax.ShapeDtypeStruct((count, capacity, 2 * hidden), BF16),
-            jax.ShapeDtypeStruct((count, capacity, features), BF16),
-        ),
-        cost_estimate=LIGHT,
-        name="open_experts",
-    )(rank, token_rows, gate, up)
+        name="pack",
+    )(place, gate, up, down)
 
 
 def gated(pre_gate, pre_up, hidden_grad):
@@ -821,84 +842,172 @@
     return silu * pre_up, grad_gate, hidden_grad * silu
 
 
+def shared_kernel(
+    place_ref, token_ref, token_peer_ref, cot_ref, cot_peer_ref, gate_ref, up_ref, down_ref, near_ref, far_ref,
+    own_grad_ref, other_grad_ref, out_ref, dx_ref, peer_ref,
+):
+    step = pl.program_id(0)
+
+    @pl.when(step == 0)
+    def start():
+        peer_ref[...] = near_ref[0]
+        out_ref[...] = jnp.zeros_like(out_ref)
+        dx_ref[...] = jnp.zeros_like(dx_ref)
+
+    @pl.when(step > 0)
+    def turn():
+        peer_ref[...] = far_ref[0]
+
+    rows, rows_peer = token_ref[...], token_peer_ref[...]
+    gate, up, down = gate_ref[0], up_ref[0], down_ref[0]
+    pre_gate = matmul(rows, gate, 1, 0) + matmul(rows_peer, peer_ref[0], 1, 0)
+    pre_up = matmul(rows, up, 1, 0) + matmul(rows_peer, peer_ref[1], 1, 0)
+    back = matmul(cot_ref[...], down, 1, 1) + matmul(cot_peer_ref[...], peer_ref[2], 1, 0)
+    result, grad_gate, grad_up = gated(pre_gate, pre_up, back)
+    result, grad_gate, grad_up = result.astype(BF16), grad_gate.astype(BF16), grad_up.astype(BF16)
+    out_ref[...] += matmul(result, down, 1, 0)
+    dx_ref[...] += matmul(grad_gate, gate, 1, 1) + matmul(grad_up, up, 1, 1)
+    grads = (
+        matmul(rows, grad_gate, 0, 0).astype(BF16),
+        matmul(rows, grad_up, 0, 0).astype(BF16),
+        matmul(cot_ref[...], result, 0, 0).astype(BF16),
+    )
+
+    def write(target_ref):
+        for kind in range(3):
+            target_ref[0, kind] = grads[kind]
+
+    pl.when(step == 0)(lambda: write(own_grad_ref))
+    pl.when(step > 0)(lambda: write(other_grad_ref))
+
+
+def run_shared(place, tokens_own, tokens_peer, cot_own, cot_peer, gate, up, down, near, far):
+    tokens, features = tokens_own.shape
+    hidden = gate.shape[2] // 2
+    grads = jax.ShapeDtypeStruct((1, 3, features, hidden), BF16)
+    sums = jax.ShapeDtypeStruct((tokens, features), F32)
+    return pl.pallas_call(
+        shared_kernel,
+        grid_spec=pltpu.PrefetchScalarGridSpec(
+            num_scalar_prefetch=1,
+            grid=(2,),
+            in_specs=[whole_block((tokens, features))] * 4
+            + [
+                pl.BlockSpec((1, features, hidden), lambda i, place: (0, 0, place[i])),
+                pl.BlockSpec((1, features, hidden), lambda i, place: (0, 0, place[i])),
+                pl.BlockSpec((1, hidden, features), lambda i, place: (0, place[i], 0)),
+            ]
+            + [whole_block((1, 3, features, hidden))] * 2,
+            out_specs=(whole_block(grads.shape),) * 2 + (whole_block(sums.shape),) * 2,
+            scratch_shapes=[pltpu.VMEM((3, features, hidden), BF16)],
+        ),
+        out_shape=(grads, grads, sums, sums),
+        cost_estimate=LIGHT,
+        name="run_shared",
+    )(place, tokens_own, tokens_peer, cot_own, cot_peer, gate, up, down, near, far)
+
+
 def experts_kernel(
-    rank_ref, prob_ref, pre_own_ref, pre_peer_ref, back_own_ref, back_peer_ref, rows_ref, cot_ref,
-    gate_ref, up_ref, down_ref, out_in_ref, dx_in_ref,
-    grad_ref, share_ref, out_ref, dx_ref,
+    capacity,
+    place_ref, rank_ref, prob_ref, token_ref, token_peer_ref, cot_ref, cot_peer_ref,
+    gate_ref, up_ref, down_ref, near_ref, far_ref, out_in_ref, dx_in_ref,
+    own_grad_ref, other_grad_ref, share_ref, out_ref, dx_ref, peer_ref,
 ):
-    capacity, hidden = back_own_ref.shape[1:]
-
-    @pl.when(pl.program_id(0) == 0)
+    step = pl.program_id(0)
+
+    @pl.when(step == 0)
     def start():
         out_ref[...] = out_in_ref[...]
         dx_ref[...] = dx_in_ref[...]
 
+    @pl.when(step < 2)
+    def first_pair():
+        peer_ref[...] = near_ref[0]
+
+    @pl.when(step >= 2)
+    def second_pair():
+        peer_ref[...] = far_ref[0]
+
     mask = picks(rank_ref, capacity)
     chosen = ones_where(mask)
     gate_val = jnp.sum(jnp.where(mask, prob_ref[0], 0.0), 1, keepdims=True)
-    pre = pre_own_ref[0].astype(F32) + pre_peer_ref[0].astype(F32)
-    raw_back = back_own_ref[0].astype(F32) + back_peer_ref[0].astype(F32)
-    result, grad_gate, grad_up = gated(pre[:, :hidden], pre[:, hidden:], gate_val * raw_back)
+    rows, rows_peer, cot_rows, cot_rows_peer = (
+        jnp.dot(chosen, ref[...], preferred_element_type=F32).astype(BF16)
+        for ref in (token_ref, token_peer_ref, cot_ref, cot_peer_ref)
+    )
+    gate, up, down = gate_ref[0], up_ref[0], down_ref[0]
+    pre_gate = matmul(rows, gate, 1, 0) + matmul(rows_peer, peer_ref[0], 1, 0)
+    pre_up = matmul(rows, up, 1, 0) + matmul(rows_peer, peer_ref[1], 1, 0)
+    raw_back = matmul(cot_rows, down, 1, 1) + matmul(cot_rows_peer, peer_ref[2], 1, 0)
+    result, grad_gate, grad_up = gated(pre_gate, pre_up, gate_val * raw_back)
     result = result.astype(BF16).astype(F32)
     share = jnp.sum(result * raw_back, 1, keepdims=True)
     share_ref[0] = jnp.sum(jnp.where(mask, share, 0.0), 0, keepdims=True)
     scaled = (gate_val * result).astype(BF16)
     grad_gate = grad_gate.astype(BF16)
     grad_up = grad_up.astype(BF16)
-    rows = rows_ref[0]
-    out_rows = jnp.dot(scaled, down_ref[0], preferred_element_type=F32).astype(BF16)
+    out_rows = matmul(scaled, down, 1, 0).astype(BF16)
     out_ref[...] += matmul(chosen, out_rows, 0, 0)
-    dx_rows = (matmul(grad_gate, gate_ref[0], 1, 1) + matmul(grad_up, up_ref[0], 1, 1)).astype(BF16)
+    dx_rows = (matmul(grad_gate, gate, 1, 1) + matmul(grad_up, up, 1, 1)).astype(BF16)
     dx_ref[...] += matmul(chosen, dx_rows, 0, 0)
-    grad_ref[0, 0] = matmul(rows, grad_gate, 0, 0).astype(BF16)
-    grad_ref[0, 1] = matmul(rows, grad_up, 0, 0).astype(BF16)
-    grad_ref[0, 2] = matmul(cot_ref[0], scaled, 0, 0).astype(BF16)
+    grads = (
+        matmul(rows, grad_gate, 0, 0).astype(BF16),
+        matmul(rows, grad_up, 0, 0).astype(BF16),
+        matmul(cot_rows, scaled, 0, 0).astype(BF16),
+    )
+
+    def write(target_ref):
+        for kind in range(3):
+            target_ref[0, kind] = grads[kind]
+
+    pl.when(step < 2)(lambda: write(own_grad_ref))
+    pl.when(step >= 2)(lambda: write(other_grad_ref))
 
 
 def run_experts(
-    rank, probs, pre_own, pre_peer, back_own, back_peer, rows, cot_rows, gate, up, down, out_sum, dx_sum, first
+    place, rank, probs, tokens_own, tokens_peer, cot_own, cot_peer, gate, up, down, near, far,
+    out_sum, dx_sum, first, capacity,
 ):
-    count, capacity, features = rows.shape
+    tokens, features = out_sum.shape
     hidden = gate.shape[2]
-    tokens = out_sum.shape[0]
 
     def at(shape, base):
-        return pl.BlockSpec((1,) + shape, lambda i: (base + i, 0, 0))
-
+        return pl.BlockSpec((1,) + shape, lambda i, place: (base + place[i], 0, 0))
+
+    block = (1, 3, features, hidden)
+    grads = jax.ShapeDtypeStruct((2, 3, features, hidden), BF16)
+    sums = jax.ShapeDtypeStruct((tokens, features), F32)
     return pl.pallas_call(
-        experts_kernel,
-        grid=(count,),
-        in_specs=[
-            at((1, tokens), first),
-            at((1, tokens), first),
-            at((capacity, 2 * hidden), 0),
-            at((capacity, 2 * hidden), 0),
-            at((capacity, hidden), first),
-            at((capacity, hidden), first),
-            at((capacity, features), 0),
-            at((capacity, features), first),
-            at((features, hidden), first),
-            at((features, hidden), first),
-            at((hidden, features), first),
-            whole_block((tokens, features)),
-            whole_block((tokens, features)),
-        ],
-        out_specs=(
-            pl.BlockSpec((1, 3, features, hidden), lambda i: (i, 0, 0, 0)),
-            at((1, tokens), 0),
-            whole_block((tokens, features)),
-            whole_block((tokens, features)),
+        functools.partial(experts_kernel, capacity),
+        grid_spec=pltpu.PrefetchScalarGridSpec(
+            num_scalar_prefetch=1,
+            grid=(4,),
+            in_specs=[at((1, tokens), first)] * 2
+            + [whole_block((tokens, features))] * 4
+            + [
+                at((features, hidden), first),
+                at((features, hidden), first),
+                at((hidden, features), first),
+                pl.BlockSpec(block, lambda i, place: (jnp.minimum(i, 1), 0, 0, 0)),
+                pl.BlockSpec(block, lambda i, place: (jnp.maximum(i, 2) - 2, 0, 0, 0)),
+                whole_block((tokens, features)),
+                whole_block((tokens, features)),
+            ],
+            out_specs=(
+                pl.BlockSpec(block, lambda i, place: (place[jnp.minimum(i, 1)] // 2, 0, 0, 0)),
+                pl.BlockSpec(block, lambda i, place: (place[jnp.maximum(i, 2)] // 2, 0, 0, 0)),
+                at((1, tokens), 0),
+                whole_block(sums.shape),
+                whole_block(sums.shape),
+            ),
+            scratch_shapes=[pltpu.VMEM((3, features, hidden), BF16)],
         ),
-        out_shape=(
-            jax.ShapeDtypeStruct((count, 3, features, hidden), BF16),
-            jax.ShapeDtypeStruct((count, 1, tokens), F32),
-            jax.ShapeDtypeStruct((tokens, features), F32),
-            jax.ShapeDtypeStruct((tokens, features), F32),
-        ),
+        out_shape=(grads, grads, jax.ShapeDtypeStruct((4, 1, tokens), F32), sums, sums),
         cost_estimate=LIGHT,
         name="run_experts",
     )(
-        rank, probs, pre_own, pre_peer, back_own, back_peer, rows, cot_rows, gate, up, down, out_sum, dx_sum
+        place, rank, probs, tokens_own, tokens_peer, cot_own, cot_peer, gate, up, down, near, far,
+        out_sum, dx_sum,
     )
 
 
@@ -917,6 +1026,7 @@
 
 
 def spread(core, half_grads, rest_grads, earlier, first, experts):
+    aliased = min(len(earlier), 3)
     half, unused, features, hidden = half_grads.shape
 
     def own_index(i, core):
@@ -926,7 +1036,7 @@
         return (jnp.maximum(i - half, 0), 0, 0, 0)
 
     def out_index(i, core):
-        place = jnp.where(i < half, core[0] * half + i, (1 - core[0]) * half + i - half)
+        place = jnp.where(i < half, 2 * i + core[0], 2 * (i - half) + 1 - core[0])
         return (first + place, 0, 0)
 
     shapes = ((features, hidden), (features, hidden), (hidden, features))
@@ -945,7 +1055,7 @@
         ),
         out_shape=tuple(jax.ShapeDtypeStruct((experts,) + shape, F32) for shape in shapes)
         + (jax.ShapeDtypeStruct((8, 128), F32),),
-        input_output_aliases={3 + i: i for i in range(len(earlier))},
+        input_output_aliases={3 + i: i for i in range(aliased)},
         cost_estimate=LIGHT,
         name="spread",
     )(core, half_grads, rest_grads, *earlier)
@@ -981,19 +1091,31 @@
     prompt_len = tok_block // 2
     block = 256
     chunk = 4
-    core = (lax.axis_index("dp") % 2).reshape(1)
-
+    shards = lax.axis_index("dp")
+    core = (shards % 2).reshape(1)
+    place = jnp.stack([shards, shards ^ 2, shards ^ 1, shards ^ 3])
+    sides = jnp.stack([shards % 2, 1 - shards % 2])
+    firsts = list(range(0, experts, 4))
+    by_quarters = 2
+
+    own_parts = col_parts(inputs)
     gain_high, gain_low = high_low(first_gain)
     gain_last = (first_gain - gain_high.astype(F32) - gain_low.astype(F32)).astype(BF16)
     gain_rows = jnp.pad(jnp.stack([gain_high, gain_low, gain_last]), ((0, 5), (0, 0)))
     peer_first = swap(jnp.concatenate([inputs, gain_rows], 0), "row")
     peer_gain = jnp.sum(peer_first[tok_rest : tok_rest + 3].astype(F32)[::-1], 0)
     peer_weight = swap(attend_in, "row")
-    own_parts = col_parts(inputs)
     peer_parts = [peer_first[:tok_rest]] + [swap(part, "row") for part in own_parts[1:]]
     own_all = in_order(own_parts, "col").reshape(tok_block, feat_dev).astype(F32)
     peer_all = in_order(peer_parts, "col").reshape(tok_block, feat_dev).astype(F32)
-    cot_all = col_rows(held(cotangent, *own_parts))
+
+    shared_gate, shared_up, shared_down = shared_gate[None], shared_up[None], shared_down[None]
+
+    def pack_experts(place, index):
+        return pack(place, expert_gate, expert_up, expert_down, firsts[index], 1, 1)
+
+    late_place = held(place, peer_parts[1])
+    packed = [pack_experts(late_place, 0), pack_experts(late_place, 1)]
 
     squares_one = jnp.sum(own_all * own_all, 1) + jnp.sum(peer_all * peer_all, 1)
     scale_all = lax.rsqrt(squares_one / feat_full + EPSILON)[:, None]
@@ -1017,20 +1139,40 @@
     )
     before = (offsets[:, None] < offsets[None, :]).astype(BF16)
     rank = jnp.dot(named.astype(BF16), before, preferred_element_type=F32).astype(jnp.int32)
-    rank = jnp.where(named, rank, -1)[:, None, :]
+    rank = jnp.where(named, rank, -1).reshape(experts, col_size, tok_rest)
+    rank = jnp.concatenate(
+        [
+            lax.dynamic_index_in_dim(rank, (col_index - step) % col_size, 1, False)
+            for step in range(col_size)
+        ],
+        1,
+    )[:, None, :]
     count_total = sum_by_swaps(jnp.sum(named.astype(F32), 1), ("dp",))
 
+    packed, place, sides, normed_own, normed_peer, peer_weight, cot_sent, count_total = stage(
+        packed, place, sides, normed_own, normed_peer, peer_weight, cotangent, count_total
+    )
+    weights = [swap(packed[0], "row")]
+    cot_parts = col_parts(cot_sent)
     qkv, attended, log_total, out_partial = attend(
         normed_own, normed_peer, attend_in, peer_weight, attend_out, cosine, sine, start, block
     )
-    cot_all = held(cot_all, out_partial)
-    back_own, cot_rows = back_hidden(rank, cot_all, expert_down, 0, experts, capacity)
-    back_peer = swap(back_own, "row")
-    shared_back_own = matmul(cot_all, shared_down, 1, 1).astype(BF16)
-    shared_back_peer = swap(shared_back_own, "row")
-
+    late_place = held(place, out_partial)
+    packed += [pack_experts(late_place, 2), pack_experts(late_place, 3)]
+    weights, cot_parts, out_partial, packed, place = stage(weights, cot_parts, out_partial, packed, place)
+
+    weights.append(swap(packed[1], "row"))
+    across = swap(weights[0], "dp", 2)
+    cot_own = jnp.concatenate(cot_parts, 0)
     inputs_f = inputs.astype(F32)
-    mixed_one = inputs_f + held(col_sum_rows(out_partial), back_own, shared_back_own)
+    mixed_one = inputs_f + col_sum_rows(out_partial)
+    late_place, late_sides = held((place[1:], sides), cot_own)
+    packed.append(pack_experts(late_place, 3))
+    shared_packed = pack(late_sides, shared_gate, shared_up, shared_down, 0, 1, 2)
+    weights, across, cot_own, mixed_one, shared_packed, packed = stage(
+        weights, across, cot_own, mixed_one, shared_packed, packed
+    )
+
     gained = mixed_one * second_gain
     partial_stats = jnp.concatenate(
         [
@@ -1044,110 +1186,193 @@
     router_probs = jax.nn.softmax(stats[:, 1:] * scale_two, -1)
     unit_two = mixed_one * scale_two
     normed_two = (unit_two * second_gain).astype(BF16)
-    sent = in_order(col_parts(with_rows(normed_two, router_probs.T)), "col")
-    normed_all, probs_all = split_rows(sent, tok_rest, experts, tok_rest)
-    normed_all = normed_all.reshape(tok_block, feat_dev)
-    probs_rows = probs_all.transpose(1, 0, 2).reshape(experts, 1, tok_block)
-
-    pre_own, token_rows, pre_peer = [], [], []
-    firsts = list(range(0, experts, chunk))
-    for first in firsts:
-        pre, rows = open_experts(rank, normed_all, expert_gate, expert_up, first, chunk, capacity)
-        pre_own.append(pre)
-        token_rows.append(rows)
-    shared_pre_own = jnp.concatenate(
-        [matmul(normed_all, shared_gate, 1, 0), matmul(normed_all, shared_up, 1, 0)], 1
-    ).astype(BF16)
-    order = pre_own[:-1] + [shared_pre_own] + pre_own[-1:]
-    arrived = []
-    for index, value in enumerate(order):
-        arrived.append(swap(held(value, *arrived[index - 2 : index - 1]) if index > 1 else value, "row"))
-    pre_peer = arrived[:-2] + arrived[-1:]
-    shared_pre_peer = arrived[-2]
-
-    out_sum = jnp.zeros((tok_block, feat_dev), F32)
-    dx_sum = jnp.zeros((tok_block, feat_dev), F32)
-    shares, halves, crossed = [], [], []
-    for index, first in enumerate(firsts):
-        pre = pre_peer[index]
-        if index:
-            pre = held(pre, halves[-1])
-        if index > 2:
-            pre = held(pre, crossed[index - 3])
-        grads, share, out_sum, dx_sum = run_experts(
-            rank, probs_rows, pre_own[index], pre, back_own, back_peer,
-            token_rows[index], cot_rows, expert_gate, expert_up, expert_down, out_sum, dx_sum, first,
+    normed_sent = with_rows(normed_two, router_probs.T)
+    normed_sent, cot_own, shared_packed, weights, across = stage(
+        normed_sent, cot_own, shared_packed, weights, across
+    )
+
+    sent_parts = col_parts(normed_sent)
+    cot_peer = swap(cot_own, "row")
+    shared_near = swap(shared_packed, "row")
+    near = [joined(weights[0], across)]
+    sent_parts, cot_peer, shared_near, near, weights, packed = stage(
+        sent_parts, cot_peer, shared_near, near, weights, packed
+    )
+
+    opened = [split_rows(part, tok_rest, experts, tok_rest) for part in sent_parts]
+    tokens_own = jnp.concatenate([part[0] for part in opened], 0)
+    probs = jnp.concatenate([part[1] for part in opened], 1)[:, None, :]
+    tokens_peer = swap(tokens_own, "row")
+    shared_far = swap(shared_near, "dp", 1)
+    far = [swap(near[0], "dp", 1)]
+    across = swap(weights[1], "dp", 2)
+    tokens_own, tokens_peer, probs, shared_far, far, packed, weights = stage(
+        tokens_own, tokens_peer, probs, shared_far, far, packed, weights
+    )
+
+    ready, landed, totalled, arrived = [], [], [], []
+    expert_grads, finished = [], {}
+
+    def launch(count):
+        flights = [(name, half, swap(half, "dp", 2)) for name, half in ready[:count]]
+        returns = [(name, total, swap(total, "dp", 1)) for name, total in totalled]
+        del ready[:count], totalled[:]
+        return flights, returns
+
+    def follow(*values):
+        for name, mine, theirs in landed:
+            totalled.append((name, added(held(mine, *values) if values else mine, theirs)[0]))
+        for name, total, rest in arrived:
+            if isinstance(name, int):
+                turn = held(core, *values) if values else core
+                expert_grads[:] = spread(turn, total, rest, tuple(expert_grads), name, experts)
+            else:
+                finished[name] = (total, rest)
+        del landed[:], arrived[:]
+
+    def land(launched, *values):
+        flights, returns = launched
+        got = stage(flights_of(flights), flights_of(returns), flights_of(ready), flights_of(totalled),
+                    expert_grads[3:], values)
+        landed[:] = [(old[0],) + new for old, new in zip(flights, got[0])]
+        arrived[:] = [(old[0],) + new for old, new in zip(returns, got[1])]
+        ready[:] = [(old[0],) + new for old, new in zip(ready, got[2])]
+        totalled[:] = [(old[0],) + new for old, new in zip(totalled, got[3])]
+        expert_grads[3:] = got[4]
+        return got[5]
+
+    def flights_of(items):
+        return [item[1:] for item in items]
+
+    def pair_up(name, mine, theirs, *values):
+        for index, half in enumerate(added(held(mine, *values) if values else mine, theirs)):
+            ready.append((name + 2 * index if isinstance(name, int) else name, half))
+
+    weights.append(swap(packed[2], "row"))
+    shared_mine, shared_other, out_sum, dx_sum = run_shared(
+        sides, tokens_own, tokens_peer, cot_own, cot_peer,
+        shared_gate, shared_up, shared_down, shared_near, shared_far,
+    )
+    weights, across, packed, out_sum, dx_sum, shared_mine, shared_other = stage(
+        weights, across, packed, out_sum, dx_sum, shared_mine, shared_other
+    )
+    near.append(joined(weights[1], across))
+    shares = []
+
+    def run(index):
+        mine, other, share, out_new, dx_new = run_experts(
+            place, rank, probs, tokens_own, tokens_peer, cot_own, cot_peer,
+            expert_gate, expert_up, expert_down, near[index], far[index], out_sum, dx_sum, firsts[index], capacity,
         )
         shares.append(share[:, 0])
-        halves.append(pair_half(grads))
-        crossed.append(cross_sum(held(halves[-1], crossed[-1]) if index else halves[-1]))
-
-    shared_pre = shared_pre_own.astype(F32) + shared_pre_peer.astype(F32)
-    shared_back = shared_back_own.astype(F32) + shared_back_peer.astype(F32)
-    shared_hidden, shared_gate_pgrad, shared_up_pgrad = (
-        value.astype(BF16)
-        for value in gated(shared_pre[:, :shared_dev], shared_pre[:, shared_dev:], shared_back)
-    )
-    out_sum = out_sum + matmul(shared_hidden, shared_down, 1, 0)
-    dx_sum = (
-        dx_sum + matmul(shared_gate_pgrad, shared_gate, 1, 1) + matmul(shared_up_pgrad, shared_up, 1, 1)
-    )
-    shared_half = pair_half(
-        jnp.stack(
-            [
-                matmul(normed_all, shared_gate_pgrad, 0, 0).astype(BF16),
-                matmul(normed_all, shared_up_pgrad, 0, 0).astype(BF16),
-                matmul(cot_all, shared_hidden, 0, 0).astype(BF16),
-            ],
-            1,
-        )
-    )
-
-    share_rows = jnp.concatenate(shares, 0).reshape(experts, col_size, tok_rest).transpose(1, 0, 2)
-    dx_blocks = with_rows(dx_sum.astype(BF16).reshape(col_size, tok_rest, feat_dev), share_rows)
-    dx_blocks = col_sum_rows(dx_blocks.reshape(-1, feat_dev))
-    normed_grad, gate_grad = split_rows(dx_blocks, tok_rest, experts, tok_rest)
-    normed_grad = held(normed_grad, crossed[1], shared_half)
+        return mine, other, out_new, dx_new
+
+    far.append(swap(near[1], "dp", 1))
+    weights.append(swap(packed[3], "row"))
+    across = swap(weights[2], "dp", 2)
+    mine, other, out_sum, dx_sum = run(0)
+    near.append(joined(held(weights[2], out_sum), across))
+    far, weights, mine, other, out_sum, dx_sum, packed, near = stage(
+        far, weights, mine, other, out_sum, dx_sum, packed, near
+    )
+    pair_up(firsts[0], mine, swap(other, "dp", 1))
+    launched = launch(1)
+    far.append(swap(near[2], "dp", 1))
+    weights.append(swap(packed[4], "row"))
+    mine, other, out_sum, dx_sum = run(1)
+    near.append(joined(held(weights[3], out_sum), weights[4]))
+    far, mine, other, out_sum, dx_sum, near = land(launched, far, mine, other, out_sum, dx_sum, near)
+    launched = launch(1)
+    far.append(swap(near[3], "dp", 1))
+    theirs = swap(other, "dp", 1)
+    earlier = mine
+    mine, other, out_sum, dx_sum = run(2)
+    pair_up(firsts[1], earlier, theirs, out_sum)
+    follow(out_sum)
+    far, mine, other, out_sum, dx_sum = land(launched, far, mine, other, out_sum, dx_sum)
+    launched = launch(1)
+    theirs = swap(other, "dp", 1)
+    shared_theirs = swap(shared_other, "dp", 1)
+    earlier = mine
+    mine, other, out_sum, dx_sum = run(3)
+    pair_up("shared", shared_mine, shared_theirs, out_sum)
+    pair_up(firsts[2], earlier, theirs, out_sum)
+    follow(out_sum)
+    mine, other, out_sum, dx_sum, shares = land(launched, mine, other, out_sum, dx_sum, shares)
+
+    launched = launch(2)
+    shares = jnp.concatenate(shares, 0)
+    dx_blocks = []
+    for step in range(col_size):
+        rows = slice(step * tok_rest, (step + 1) * tok_rest)
+        dx_blocks.append(with_rows(dx_sum[rows].astype(BF16), shares[:, rows]))
+    dx_blocks = sent_back(dx_blocks)
+    theirs = swap(other, "dp", 1)
+    pair_up(firsts[3], mine, theirs, dx_blocks[1])
+    follow(dx_blocks[1])
+    (dx_blocks,) = land(launched, dx_blocks)
+    launched = launch(2)
+    normed_grad, gate_grad = split_rows(summed_up(dx_blocks), tok_rest, experts, tok_rest)
     prob_grad = gate_grad.T + experts * count_total / (2.0 * tokens_all * tokens_all)
     logit_grad = router_probs * (prob_grad - jnp.sum(router_probs * prob_grad, -1, keepdims=True))
-    router_grad = jnp.einsum("td,te->ed", unit_two * second_gain, logit_grad, precision=HIGHEST)
     two_grad = normed_grad + jnp.einsum("te,de->td", logit_grad, router_weight, precision=HIGHEST)
     gained_two = two_grad * second_gain
-    second_gain_grad = jnp.sum(two_grad * unit_two, 0)
     inner_two = jnp.sum(gained_two * unit_two, 1, keepdims=True)
     inner_two = (inner_two + swap(inner_two, "row")) / feat_full
     cot_f = cotangent.astype(F32)
     mixed_grad = cot_f + scale_two * (gained_two - unit_two * inner_two)
-    mix_all = col_rows(mixed_grad.astype(BF16))
+    mix_parts = col_parts(mixed_grad.astype(BF16))
+    follow(mix_parts[1])
+    mix_parts, logit_grad, two_grad = land(launched, mix_parts, logit_grad, two_grad)
+
+    launched = launch(1)
+    mix_all = in_order(mix_parts, "col").reshape(tok_block, feat_dev)
     attn_own = matmul(mix_all, attend_out, 1, 1).astype(BF16)
     attn_peer = swap(attn_own, "row")
-
-    expert_grads = ()
-    flags = []
-    for index, first in enumerate(firsts):
-        rest = swap(crossed[index], "dp", 1)
-        *expert_grads, flag = spread(core, crossed[index], rest, expert_grads, first, experts)
-        flags.append(flag)
-
-    layer_out = (
-        mixed_one + col_sum_rows(held(out_sum.astype(BF16), mix_all))
-    ).astype(BF16)
-    attn_peer = held(attn_peer, crossed[2], flags[0])
-    one_partial, attend_in_grad = attend_back(
-        attn_own, attn_peer, qkv, attended, log_total, cosine, sine, start, normed_own, attend_in, block
-    )
-    one_partial = held(one_partial, layer_out)
+    out_low = held(out_sum.astype(BF16), mix_all)
+    out_blocks = sent_back([out_low[step * tok_rest : (step + 1) * tok_rest] for step in range(col_size)])
     heads = attended.shape[0]
     attn_rows = attended.astype(BF16)
     attend_out_grad = jnp.concatenate(
         [matmul(attn_rows[head], mix_all, 0, 0) for head in range(heads)], 0
     ).astype(BF16)
+    router_grad = jnp.einsum("td,te->ed", unit_two * second_gain, logit_grad, precision=HIGHEST)
+    second_gain_grad = jnp.sum(two_grad * unit_two, 0)
+    one_partial, attend_in_grad = attend_back(
+        attn_own, attn_peer, qkv, attended, log_total, cosine, sine, start, normed_own, attend_in, block
+    )
+    follow(one_partial)
+    one_partial, attend_in_grad, attend_out_grad, out_blocks, router_grad, second_gain_grad = land(
+        launched, one_partial, attend_in_grad, attend_out_grad, out_blocks, router_grad, second_gain_grad
+    )
+
+    launched = launch(1)
+    one_low = one_partial.astype(BF16)
+    one_blocks = one_low.reshape(col_size, tok_rest, feat_dev)
+    one_blocks = sent_back(
+        [
+            lax.dynamic_index_in_dim(one_blocks, (col_index - step) % col_size, 0, False)
+            for step in range(col_size)
+        ]
+    )
+    layer_out = (mixed_one + summed_up(out_blocks)).astype(BF16)
     width = attend_in_grad.shape[1]
     attend_half = pair_half(
         jnp.concatenate([attend_in_grad, attend_out_grad.reshape(-1, width)], 0)
     )
     first_gain_grad = jnp.sum(one_partial * unit_all, 0)
-    one_grad = col_sum_rows(one_partial.astype(BF16))
+    prob_sums = jnp.pad(jnp.sum(router_probs, 0), (0, feat_dev - experts))
+    totals = jnp.concatenate(
+        [first_gain_grad[None], second_gain_grad[None], prob_sums[None], router_grad], 0
+    )
+    totals = totals + swap(totals, "dp", 1)
+    follow(one_blocks[1])
+    one_blocks, attend_half, totals = land(launched, one_blocks, attend_half, totals)
+
+    totals = totals + swap(totals, "dp", 2)
+    ready.insert(0, ("attend", attend_half[None]))
+    launched = launch(2)
+    one_grad = summed_up(one_blocks)
     own_rows = col_index * tok_rest
     unit_one = rows_of(unit_all, own_rows, tok_rest)
     scale_one = rows_of(scale_all, own_rows, tok_rest)
@@ -1155,18 +1380,19 @@
     inner_one = jnp.sum(gained_one * unit_one, 1, keepdims=True)
     inner_one = (inner_one + swap(inner_one, "row")) / feat_full
     input_grad = (mixed_grad + scale_one * (gained_one - unit_one * inner_one)).astype(BF16)
-
-    prob_sums = jnp.pad(jnp.sum(router_probs, 0), (0, feat_dev - experts))
-    totals = sum_by_swaps(
-        jnp.concatenate(
-            [first_gain_grad[None], second_gain_grad[None], prob_sums[None], router_grad], 0
-        ),
-        ("dp", "col"),
-    )
+    follow()
+    input_grad, totals = land(launched, input_grad, totals)
+    totals = sum_by_swaps(totals, ("col",))
+    while ready or landed or totalled or arrived:
+        follow()
+        (totals,) = land(launch(2), totals)
+
     prob_total = totals[2, :experts]
     balance_loss = experts * jnp.sum(count_total / (2.0 * tokens_all) * prob_total / tokens_all)
-    shared_grads = both_halves(cross_sum(shared_half))
-    attend_grads = both_halves(cross_sum(held(attend_half, crossed[3])))
+    shared_grads = [jnp.concatenate(pair, 3) for pair in (finished["shared"], finished["shared"][::-1])]
+    shared_grads = jnp.where(core == 0, *shared_grads)[0].astype(F32)
+    attend_grads = [jnp.concatenate(pair, 1) for pair in (finished["attend"], finished["attend"][::-1])]
+    attend_grads = jnp.where(core == 0, *attend_grads)[0].astype(F32)
     return (
         layer_out,
         input_grad,
@@ -1175,9 +1401,9 @@
         attend_grads[feat_dev:].reshape(attend_out_grad.shape),
         totals[1],
         totals[3:].T,
-        shared_grads[:, 0],
-        shared_grads[:, 1],
-        shared_grads[:, 2].T,
+        shared_grads[0],
+        shared_grads[1],
+        shared_grads[2].T,
         expert_grads[0],
         expert_grads[1],
         expert_grads[2],
@@ -1190,12 +1416,15 @@
 
 
 def chosen_body(*shards):
-    inputs, cont_lengths = shards[0], shards[3]
+    inputs, cont_lengths, shared_gate = shards[0], shards[3], shards[9]
+    experts, unused, hidden = shards[12].shape
     tok_block = inputs.shape[0] * lax.axis_size("col")
     paired = (
         lax.axis_size("row") == 2
-        and lax.axis_size("dp") >= 2
-        and power_of_two(lax.axis_size("dp"))
+        and lax.axis_size("dp") == 4
+        and experts == 16
+        and shared_gate.shape[1] == hidden
+        and hidden % 256 == 0
         and power_of_two(lax.axis_size("col"))
         and cont_lengths.shape[0] == 1
         and tok_block % 512 == 0

time: 630 us -> 557 us (0.88)
  Pallas kernels: 149 us -> 244 us
  waiting for transfers between devices: 230 us -> 157 us
  other arithmetic: 78.4 us -> 29.8 us
  local copies, waits for them, and re-layouts: 56.5 us -> 36.1 us
  matrix products: 20.6 us -> 3.14 us
  starting transfers between devices: 85.4 us -> 77.6 us
    pallas_call x9 -> x30, Pallas kernels: 88.6 us -> 179 us  [the longest x4 88.2 us: run_experts(): pl.pallas_call(functools.partial(experts_kernel, capacity), grid_spec=plt...]
    ppermute x40 -> x57, waiting for transfers between devices: 192 us -> 117 us  [swap(): return lax.ppermute(value, axis, [(i, i ^ step) for i in range(size)])]
    convert_element_type x12 -> x4, other arithmetic: 25.7 us -> 3.25 us  [the longest x1 2.07 us: paired_body(): shared_grads = jnp.where(core == 0, *shared_grads)[0].astype(F32)]
    dot_general x13 -> x4, matrix products: 17.6 us -> 1.32 us  [matmul(): lax.dot_general(left, right, (((left_dim,), (right_dim,)), ((), ())), pre...]
    convert_element_type x6 -> x1, other arithmetic: 15 us -> 1.87 us  [pair_half(): return (mine.astype(F32) + swap(other, 'dp', 1).astype(F32)).astype(BF16)]
    ppermute x24, starting transfers between devices: 51.1 us -> 38.4 us  [shifted(): lax.ppermute(value, axis, [(i, (i + step) % size) for i in range(size)])]
    squeeze x5 -> x1, local copies, waits for them, and re-layouts: 10.5 us -> 0.81 us  [pair_half(): other = lax.dynamic_index_in_dim(halves, 1 - core, 0, False)]
    unnamed x199 -> x125, local copies, waits for them, and re-layouts: 8.64 us -> 14.4 us
  transfers between devices with their start and end apart: 64 -> 81, of which waited for: 27 -> 25; matrix products, arithmetic and copies ran while one was open for 24% -> 9% of each run, Pallas kernels for 20% -> 43%
where the time goes in v3:
time: 557 us; the launch traced here: 552 us
  Pallas kernels  244 us (44%)
  waiting for transfers between devices  157 us (28%)
  starting transfers between devices  77.6 us (14%)
  local copies, waits for them, and re-layouts  36.1 us (6%)
  other arithmetic  29.8 us (5%)
    ppermute x57, waiting for transfers between devices, swap(): return lax.ppermute(value, axis, [(i, i ^ step) for i in range(size)])  117 us
    pallas_call x4, Pallas kernels, run_experts(): pl.pallas_call(functools.partial(experts_kernel, capacity), grid_spec=plt...  88.2 us
    pallas_call x15, Pallas kernels, added(): pl.pallas_call(add_kernel, grid=(steps,), in_specs=[spec, spec], out_spec...  47.6 us
    ppermute x24, waiting for transfers between devices, shifted(): lax.ppermute(value, axis, [(i, (i + step) % size) for i in range(size)])  39.6 us
    ppermute x57, starting transfers between devices, swap(): return lax.ppermute(value, axis, [(i, i ^ step) for i in range(size)])  39.2 us
    ppermute x24, starting transfers between devices, shifted(): lax.ppermute(value, axis, [(i, (i + step) % size) for i in range(size)])  38.4 us
    pallas_call x8, Pallas kernels, spread(): pl.pallas_call(spread_kernel, grid_spec=pltpu.PrefetchScalarGridSpec(num_...  32.9 us
    pallas_call x6, Pallas kernels, pack(): pl.pallas_call(pack_kernel, grid_spec=pltpu.PrefetchScalarGridSpec(num_sc...  18.7 us
  transfers between devices with their start and end apart: 81, of which 25 were waited for; matrix products, arithmetic and copies ran while one was open for 9% of the time, Pallas kernels for 43%

profile of v3, /device:TPU:0, one launch (start us, length us, event | category | flops | bytes accessed | tf_op | source)
XLA Modules:
  0.0 551.6 jit_solution(12387410501539184323)
XLA Ops:
  25.9 10.9 %collective-permute-done.1 = bf16[256,384]{1,0:T(8,128)(2,1)} collective-permute-done((bf16[256,384]{1,0:T(8,128)(2,1)}, bf16[256,384]{1,0:T(8,128)(2,1)}, u32[]{:S(2)}, u32[]{:S(2)}) %collective-permute-start.1) | collective-permute-done | bytes 196640 | tf_op jit(solution)/shard_map/ppermute | solution.py:528
  62.7 14.7 %attend.1 = (bf16[9,1024,64]{2,1,0:T(8,128)(2,1)}, f32[3,1024,64]{2,1,0:T(8,128)}, f32[3,1024,1]{2,1,0:T(8,128)}, bf16[1024,384]{1,0:T(8,128)(2,1)}) custom-call(bf16[1024,384]{1,0:T(8,128)(2,1)} %get-tuple-element.298.left_ref.normed_ref, bf16[1024,384]{1,0:T(8,128)(2,1)} %get-tuple-element.299.right_ref, bf16[384,576]{1,0:T(8,128)(2,1)} %copy-done.13, ...), custom_call_target="tpu_custom_call" | custom-call | flops 1 | bytes 1 | tf_op jit(solution)/shard_map/attend/pallas_call | solution.py:731
  102.4 7.7 %collective-permute-done.14.one_ref = bf16[1,3,384,512]{3,2,1,0:T(8,128)(2,1)} collective-permute-done((bf16[1,3,384,512]{3,2,1,0:T(8,128)(2,1)}, bf16[1,3,384,512]{3,2,1,0:T(8,128)(2,1)}, u32[]{:S(2)}, u32[]{:S(2)}) %collective-permute-start.14) | collective-permute-done | bytes 1179680 | tf_op jit(solution)/shard_map/ppermute | solution.py:528
  127.5 5.6 %collective-permute-done.21 = bf16[288,384]{1,0:T(8,128)(2,1)} collective-permute-done((bf16[288,384]{1,0:T(8,128)(2,1)S(1)}, bf16[288,384]{1,0:T(8,128)(2,1)}, u32[]{:S(2)}, u32[]{:S(2)}) %collective-permute-start.21) | collective-permute-done | bytes 221216 | tf_op jit(solution)/shard_map/ppermute | solution.py:533
  133.1 11.1 %collective-permute-done.24.near_ref = bf16[1,3,384,256]{3,2,1,0:T(8,128)(2,1)S(1)} collective-permute-done((bf16[1,3,384,256]{3,2,1,0:T(8,128)(2,1)}, bf16[1,3,384,256]{3,2,1,0:T(8,128)(2,1)S(1)}, u32[]{:S(2)}, u32[]{:S(2)}) %collective-permute-start.24) | collective-permute-done | bytes 589856 | tf_op jit(solution)/shard_map/ppermute | solution.py:528
  151.8 15.5 %collective-permute-done.25.token_peer_ref = bf16[1024,384]{1,0:T(8,128)(2,1)S(1)} collective-permute-done((bf16[1024,384]{1,0:T(8,128)(2,1)S(1)}, bf16[1024,384]{1,0:T(8,128)(2,1)S(1)}, u32[]{:S(2)}, u32[]{:S(2)}) %collective-permute-start.25) | collective-permute-done | bytes 786464 | tf_op jit(solution)/shard_map/ppermute | solution.py:528
  168.2 12.2 %run_shared.1 = (bf16[1,3,384,256]{3,2,1,0:T(8,128)(2,1)}, bf16[1,3,384,256]{3,2,1,0:T(8,128)(2,1)}, f32[1024,384]{1,0:T(8,128)}, f32[1024,384]{1,0:T(8,128)}) custom-call(s32[2]{0:T(128)} %pad_add_fusion.2.place_ref, bf16[1024,384]{1,0:T(8,128)(2,1)} %copy-done.2, bf16[1024,384]{1,0:T(8,128)(2,1)} %copy-done.5, bf16[1024,384]{1,0:T(8,128)(2,1)} %copy-done.3, ...), custom_call_target="tpu_custom_call" | custom-call | flops 1 | bytes 1 | tf_op jit(solution)/shard_map/run_shared/pallas_call | solution.py:889
  180.4 14.2 %collective-permute-done.28.one_ref = bf16[1,3,384,512]{3,2,1,0:T(8,128)(2,1)} collective-permute-done((bf16[1,3,384,512]{3,2,1,0:T(8,128)(2,1)}, bf16[1,3,384,512]{3,2,1,0:T(8,128)(2,1)}, u32[]{:S(2)}, u32[]{:S(2)}) %collective-permute-start.28) | collective-permute-done | bytes 1179680 | tf_op jit(solution)/shard_map/ppermute | solution.py:528
  201.6 21.9 %run_experts.4 = (bf16[2,3,384,512]{3,2,1,0:T(8,128)(2,1)}, bf16[2,3,384,512]{3,2,1,0:T(8,128)(2,1)}, f32[4,1,1024]{2,1,0:T(1,128)}, f32[1024,384]{1,0:T(8,128)}, f32[1024,384]{1,0:T(8,128)}) custom-call(s32[4]{0:T(128)} %pad_add_fusion.1.place_ref, s32[16,1,1024]{2,1,0:T(1,128)} %broadcast_in_dim.142.rank_ref, f32[16,1,1024]{2,1,0:T(1,128)} %copy.86.prob_ref, ...), custom_call_target="tpu_custom_call" | custom-call | flops 1 | bytes 1 | tf_op jit(solution)/shard_map/run_experts/pallas_call | solution.py:980
  237.1 4.4 added.15
  243.0 22.1 %run_experts.5 = (bf16[2,3,384,512]{3,2,1,0:T(8,128)(2,1)}, bf16[2,3,384,512]{3,2,1,0:T(8,128)(2,1)}, f32[4,1,1024]{2,1,0:T(1,128)}, f32[1024,384]{1,0:T(8,128)}, f32[1024,384]{1,0:T(8,128)}) custom-call(s32[4]{0:T(128)} %pad_add_fusion.1.place_ref, s32[16,1,1024]{2,1,0:T(1,128)} %broadcast_in_dim.142.rank_ref, f32[16,1,1024]{2,1,0:T(1,128)} %copy.86.prob_ref, ...), custom_call_target="tpu_custom_call" | custom-call | flops 1 | bytes 1 | tf_op jit(solution)/shard_map/run_experts/pallas_call | solution.py:980
  271.7 22.0 %run_experts.6 = (bf16[2,3,384,512]{3,2,1,0:T(8,128)(2,1)}, bf16[2,3,384,512]{3,2,1,0:T(8,128)(2,1)}, f32[4,1,1024]{2,1,0:T(1,128)}, f32[1024,384]{1,0:T(8,128)}, f32[1024,384]{1,0:T(8,128)}) custom-call(s32[4]{0:T(128)} %pad_add_fusion.1.place_ref, s32[16,1,1024]{2,1,0:T(1,128)} %broadcast_in_dim.142.rank_ref, f32[16,1,1024]{2,1,0:T(1,128)} %copy.86.prob_ref, ...), custom_call_target="tpu_custom_call" | custom-call | flops 1 | bytes 1 | tf_op jit(solution)/shard_map/run_experts/pallas_call | solution.py:980
  296.7 4.4 added.16
  302.4 22.2 %run_experts.7 = (bf16[2,3,384,512]{3,2,1,0:T(8,128)(2,1)}, bf16[2,3,384,512]{3,2,1,0:T(8,128)(2,1)}, f32[4,1,1024]{2,1,0:T(1,128)}, f32[1024,384]{1,0:T(8,128)}, f32[1024,384]{1,0:T(8,128)}) custom-call(s32[4]{0:T(128)} %pad_add_fusion.1.place_ref, s32[16,1,1024]{2,1,0:T(1,128)} %broadcast_in_dim.142.rank_ref, f32[16,1,1024]{2,1,0:T(1,128)} %copy.86.prob_ref, ...), custom_call_target="tpu_custom_call" | custom-call | flops 1 | bytes 1 | tf_op jit(solution)/shard_map/run_experts/pallas_call | solution.py:980
  330.5 4.5 added.19
  340.7 5.6 %collective-permute-done.47 = bf16[288,384]{1,0:T(8,128)(2,1)S(1)} collective-permute-done((bf16[288,384]{1,0:T(8,128)(2,1)S(1)}, bf16[288,384]{1,0:T(8,128)(2,1)S(1)}, u32[]{:S(2)}, u32[]{:S(2)}) %collective-permute-start.47) | collective-permute-done | bytes 221216 | tf_op jit(solution)/shard_map/ppermute | solution.py:533
  352.2 4.0 spread.8
  356.3 4.4 added.21
  360.7 3.7 collective-permute-done.49
  364.3 12.1 %collective-permute-done.45.two_ref = bf16[1,3,384,256]{3,2,1,0:T(8,128)(2,1)} collective-permute-done((bf16[1,3,384,256]{3,2,1,0:T(8,128)(2,1)S(1)}, bf16[1,3,384,256]{3,2,1,0:T(8,128)(2,1)}, u32[]{:S(2)}, u32[]{:S(2)}) %collective-permute-start.45) | collective-permute-done | bytes 589856 | tf_op jit(solution)/shard_map/ppermute | solution.py:528
  386.7 8.2 %collective-permute-done.55 = bf16[256,384]{1,0:T(8,128)(2,1)S(1)} collective-permute-done((bf16[256,384]{1,0:T(8,128)(2,1)}, bf16[256,384]{1,0:T(8,128)(2,1)S(1)}, u32[]{:S(2)}, u32[]{:S(2)}) %collective-permute-start.55) | collective-permute-done | bytes 196640 | tf_op jit(solution)/shard_map/ppermute | solution.py:533
  402.2 4.1 spread.9
  406.4 23.0 %collective-permute-done.52.two_ref = bf16[1,3,384,512]{3,2,1,0:T(8,128)(2,1)} collective-permute-done((bf16[1,3,384,512]{3,2,1,0:T(8,128)(2,1)}, bf16[1,3,384,512]{3,2,1,0:T(8,128)(2,1)}, u32[]{:S(2)}, u32[]{:S(2)}) %collective-permute-start.52) | collective-permute-done | bytes 1179680 | tf_op jit(solution)/shard_map/ppermute | solution.py:528
  438.0 6.2 %collective-permute-done.62 = bf16[256,384]{1,0:T(8,128)(2,1)S(1)} collective-permute-done((bf16[256,384]{1,0:T(8,128)(2,1)S(1)}, bf16[256,384]{1,0:T(8,128)(2,1)S(1)}, u32[]{:S(2)}, u32[]{:S(2)}) %collective-permute-start.62) | collective-permute-done | bytes 196640 | tf_op jit(solution)/shard_map/ppermute | solution.py:533
  448.6 17.2 %attend_back.1 = (f32[1024,384]{1,0:T(8,128)}, bf16[384,576]{1,0:T(8,128)(2,1)}) custom-call(bf16[1024,192]{1,0:T(8,128)(2,1)} %copy-done.19, bf16[1024,192]{1,0:T(8,128)(2,1)} %copy-done.38, bf16[9,1024,64]{2,1,0:T(8,128)(2,1)} %get-tuple-element.483.qkv_ref, f32[3,1024,64]{2,1,0:T(8,128)} %get-tuple-element.484.attended_ref, ...), custom_call_target="tpu_custom_call" | custom-call | flops 1 | bytes 1 | tf_op jit(solution)/shard_map/attend_back/pallas_call | solution.py:784
  471.7 4.2 spread.10
  487.4 4.3 collective-permute-done.68
  496.0 4.2 spread.11
  516.1 4.1 spread.12
  520.1 4.2 spread.13
  537.1 4.1 spread.14
  546.2 4.1 spread.15
  (429 shorter events, 236.7 us)
Async XLA Ops:
  18.4 35.2 %collective-permute-start.7 = (bf16[384,576]{1,0:T(8,128)(2,1)S(1)}, bf16[384,576]{1,0:T(8,128)(2,1)S(1)}, u32[]{:S(2)}, u32[]{:S(2)}) collective-permute-start(bf16[384,576]{1,0:T(8,128)(2,1)S(1)} %copy.79.weight_left_ref.weight_ref), channel_id=1, source_target_pairs={{0,4},{4,0},{1,5},{5,1},{2,6},{6,2},{3,7},{7,3},{8,12},{12,8},{9,1... | collective-permute-start | bytes 1327112 | tf_op jit(solution)/shard_map/ppermute | solution.py:528
  53.6 30.2 %collective-permute-start.10 = (bf16[1,3,384,512]{3,2,1,0:T(8,128)(2,1)}, bf16[1,3,384,512]{3,2,1,0:T(8,128)(2,1)}, u32[]{:S(2)}, u32[]{:S(2)}) collective-permute-start(bf16[1,3,384,512]{3,2,1,0:T(8,128)(2,1)} %pack.6), channel_id=1, source_target_pairs={{0,4},{4,0},{1,5},{5,1},{2,6},{6,2},{3,7},{7,3},{8,12},{12,8},{9,1... | collective-permute-start | bytes 3538952 | tf_op jit(solution)/shard_map/ppermute | solution.py:528
  116.3 27.8 %collective-permute-start.23 = (bf16[1024,384]{1,0:T(8,128)(2,1)S(1)}, bf16[1024,384]{1,0:T(8,128)(2,1)S(1)}, u32[]{:S(2)}, u32[]{:S(2)}) collective-permute-start(bf16[1024,384]{1,0:T(8,128)(2,1)S(1)} %constant_dynamic-update-slice_fusion.cot_ref), channel_id=1, source_target_pairs={{0,4},{4,0},{1,5},{5,1},{2,6},{6,2},{3,7},{7,3},{8,12},{12,8},{9,1... | collective-permute-start | bytes 2359304 | tf_op jit(solution)/shard_map/ppermute | solution.py:528
  116.9 27.2 %collective-permute-start.24 = (bf16[1,3,384,256]{3,2,1,0:T(8,128)(2,1)}, bf16[1,3,384,256]{3,2,1,0:T(8,128)(2,1)S(1)}, u32[]{:S(2)}, u32[]{:S(2)}) collective-permute-start(bf16[1,3,384,256]{3,2,1,0:T(8,128)(2,1)} %pack.10), channel_id=1, source_target_pairs={{0,4},{4,0},{1,5},{5,1},{2,6},{6,2},{3,7},{7,3},{8,12},{12,8},{9,1... | collective-permute-start | bytes 1769480 | tf_op jit(solution)/shard_map/ppermute | solution.py:528
  150.1 30.3 %collective-permute-start.29 = (bf16[1,3,384,512]{3,2,1,0:T(8,128)(2,1)}, bf16[1,3,384,512]{3,2,1,0:T(8,128)(2,1)}, u32[]{:S(2)}, u32[]{:S(2)}) collective-permute-start(bf16[1,3,384,512]{3,2,1,0:T(8,128)(2,1)} %collective-permute-done.14.one_ref), channel_id=1, source_target_pairs={{0,16},{8,24},{16,0},{24,8},{1,17},{9,25},{17,1},{25,9},{2,18},{10... | collective-permute-start | bytes 3538952 | tf_op jit(solution)/shard_map/ppermute | solution.py:528
  167.3 27.3 %collective-permute-start.28 = (bf16[1,3,384,512]{3,2,1,0:T(8,128)(2,1)}, bf16[1,3,384,512]{3,2,1,0:T(8,128)(2,1)}, u32[]{:S(2)}, u32[]{:S(2)}) collective-permute-start(bf16[1,3,384,512]{3,2,1,0:T(8,128)(2,1)} %pack.8), channel_id=1, source_target_pairs={{0,4},{4,0},{1,5},{5,1},{2,6},{6,2},{3,7},{7,3},{8,12},{12,8},{9,1... | collective-permute-start | bytes 3538952 | tf_op jit(solution)/shard_map/ppermute | solution.py:528
  197.7 31.8 %collective-permute-start.30 = (bf16[2,3,384,512]{3,2,1,0:T(8,128)(2,1)}, bf16[2,3,384,512]{3,2,1,0:T(8,128)(2,1)S(1)}, u32[]{:S(2)}, u32[]{:S(2)}) collective-permute-start(bf16[2,3,384,512]{3,2,1,0:T(8,128)(2,1)} %joined.5.near_ref), channel_id=1, source_target_pairs={{0,8},{8,0},{16,24},{24,16},{1,9},{9,1},{17,25},{25,17},{2,10},{10... | collective-permute-start | bytes 7077896 | tf_op jit(solution)/shard_map/ppermute | solution.py:528
  197.7 28.7 %collective-permute-start.32 = (bf16[1,3,384,512]{3,2,1,0:T(8,128)(2,1)}, bf16[1,3,384,512]{3,2,1,0:T(8,128)(2,1)}, u32[]{:S(2)}, u32[]{:S(2)}) collective-permute-start(bf16[1,3,384,512]{3,2,1,0:T(8,128)(2,1)} %collective-permute-done.28.one_ref), channel_id=1, source_target_pairs={{0,16},{8,24},{16,0},{24,8},{1,17},{9,25},{17,1},{25,9},{2,18},{10... | collective-permute-start | bytes 3538952 | tf_op jit(solution)/shard_map/ppermute | solution.py:528
  199.2 30.3 %collective-permute-start.31 = (bf16[1,3,384,512]{3,2,1,0:T(8,128)(2,1)}, bf16[1,3,384,512]{3,2,1,0:T(8,128)(2,1)}, u32[]{:S(2)}, u32[]{:S(2)}) collective-permute-start(bf16[1,3,384,512]{3,2,1,0:T(8,128)(2,1)} %pack.9), channel_id=1, source_target_pairs={{0,4},{4,0},{1,5},{5,1},{2,6},{6,2},{3,7},{7,3},{8,12},{12,8},{9,1... | collective-permute-start | bytes 3538952 | tf_op jit(solution)/shard_map/ppermute | solution.py:528
  230.9 37.5 %collective-permute-start.35 = (bf16[2,3,384,512]{3,2,1,0:T(8,128)(2,1)}, bf16[2,3,384,512]{3,2,1,0:T(8,128)(2,1)}, u32[]{:S(2)}, u32[]{:S(2)}) collective-permute-start(bf16[2,3,384,512]{3,2,1,0:T(8,128)(2,1)} %joined.6.near_ref), channel_id=1, source_target_pairs={{0,8},{8,0},{16,24},{24,16},{1,9},{9,1},{17,25},{25,17},{2,10},{10... | collective-permute-start | bytes 7077896 | tf_op jit(solution)/shard_map/ppermute | solution.py:528
  231.4 33.8 %collective-permute-start.36 = (bf16[1,3,384,512]{3,2,1,0:T(8,128)(2,1)}, bf16[1,3,384,512]{3,2,1,0:T(8,128)(2,1)}, u32[]{:S(2)}, u32[]{:S(2)}) collective-permute-start(bf16[1,3,384,512]{3,2,1,0:T(8,128)(2,1)} %pack.11), channel_id=1, source_target_pairs={{0,4},{4,0},{1,5},{5,1},{2,6},{6,2},{3,7},{7,3},{8,12},{12,8},{9,1... | collective-permute-start | bytes 3538952 | tf_op jit(solution)/shard_map/ppermute | solution.py:528
  241.5 28.2 %collective-permute-start.34 = (bf16[1,3,384,512]{3,2,1,0:T(8,128)(2,1)}, bf16[1,3,384,512]{3,2,1,0:T(8,128)(2,1)S(1)}, u32[]{:S(2)}, u32[]{:S(2)}) collective-permute-start(bf16[1,3,384,512]{3,2,1,0:T(8,128)(2,1)} %get-tuple-element.397.one_ref), channel_id=1, source_target_pairs={{0,16},{8,24},{16,0},{24,8},{1,17},{9,25},{17,1},{25,9},{2,18},{10... | collective-permute-start | bytes 3538952 | tf_op jit(solution)/shard_map/ppermute | solution.py:528
  269.7 27.0 %collective-permute-start.38 = (bf16[2,3,384,512]{3,2,1,0:T(8,128)(2,1)}, bf16[2,3,384,512]{3,2,1,0:T(8,128)(2,1)}, u32[]{:S(2)}, u32[]{:S(2)}) collective-permute-start(bf16[2,3,384,512]{3,2,1,0:T(8,128)(2,1)} %get-tuple-element.393), channel_id=1, source_target_pairs={{0,8},{8,0},{16,24},{24,16},{1,9},{9,1},{17,25},{25,17},{2,10},{10... | collective-permute-start | bytes 7077896 | tf_op jit(solution)/shard_map/ppermute | solution.py:528
  269.7 31.5 %collective-permute-start.39 = (bf16[2,3,384,512]{3,2,1,0:T(8,128)(2,1)}, bf16[2,3,384,512]{3,2,1,0:T(8,128)(2,1)}, u32[]{:S(2)}, u32[]{:S(2)}) collective-permute-start(bf16[2,3,384,512]{3,2,1,0:T(8,128)(2,1)} %joined.7.near_ref), channel_id=1, source_target_pairs={{0,8},{8,0},{16,24},{24,16},{1,9},{9,1},{17,25},{25,17},{2,10},{10... | collective-permute-start | bytes 7077896 | tf_op jit(solution)/shard_map/ppermute | solution.py:528
  270.2 31.0 %collective-permute-start.37 = (bf16[1,3,384,512]{3,2,1,0:T(8,128)(2,1)S(1)}, bf16[1,3,384,512]{3,2,1,0:T(8,128)(2,1)}, u32[]{:S(2)}, u32[]{:S(2)}) collective-permute-start(bf16[1,3,384,512]{3,2,1,0:T(8,128)(2,1)S(1)} %copy-done.25), channel_id=1, source_target_pairs={{0,16},{8,24},{16,0},{24,8},{1,17},{9,25},{17,1},{25,9},{2,18},{10... | collective-permute-start | bytes 3538952 | tf_op jit(solution)/shard_map/ppermute | solution.py:528
  301.2 29.3 %collective-permute-start.43 = (bf16[2,3,384,512]{3,2,1,0:T(8,128)(2,1)}, bf16[2,3,384,512]{3,2,1,0:T(8,128)(2,1)}, u32[]{:S(2)}, u32[]{:S(2)}) collective-permute-start(bf16[2,3,384,512]{3,2,1,0:T(8,128)(2,1)} %get-tuple-element.415), channel_id=1, source_target_pairs={{0,8},{8,0},{16,24},{24,16},{1,9},{9,1},{17,25},{25,17},{2,10},{10... | collective-permute-start | bytes 7077896 | tf_op jit(solution)/shard_map/ppermute | solution.py:528
  301.3 33.7 %collective-permute-start.40 = (bf16[1,3,384,512]{3,2,1,0:T(8,128)(2,1)}, bf16[1,3,384,512]{3,2,1,0:T(8,128)(2,1)}, u32[]{:S(2)}, u32[]{:S(2)}) collective-permute-start(bf16[1,3,384,512]{3,2,1,0:T(8,128)(2,1)} %get-tuple-element.444.one_ref), channel_id=1, source_target_pairs={{0,16},{8,24},{16,0},{24,8},{1,17},{9,25},{17,1},{25,9},{2,18},{10... | collective-permute-start | bytes 3538952 | tf_op jit(solution)/shard_map/ppermute | solution.py:528
  301.8 33.2 %collective-permute-start.41 = (bf16[1,3,384,512]{3,2,1,0:T(8,128)(2,1)S(1)}, bf16[1,3,384,512]{3,2,1,0:T(8,128)(2,1)}, u32[]{:S(2)}, u32[]{:S(2)}) collective-permute-start(bf16[1,3,384,512]{3,2,1,0:T(8,128)(2,1)S(1)} %copy-done.12), channel_id=1, source_target_pairs={{0,8},{8,0},{16,24},{24,16},{1,9},{9,1},{17,25},{25,17},{2,10},{10... | collective-permute-start | bytes 3538952 | tf_op jit(solution)/shard_map/ppermute | solution.py:528
  335.2 41.2 %collective-permute-start.44 = (bf16[1,3,384,512]{3,2,1,0:T(8,128)(2,1)}, bf16[1,3,384,512]{3,2,1,0:T(8,128)(2,1)}, u32[]{:S(2)}, u32[]{:S(2)}) collective-permute-start(bf16[1,3,384,512]{3,2,1,0:T(8,128)(2,1)} %get-tuple-element.461.one_ref), channel_id=1, source_target_pairs={{0,16},{8,24},{16,0},{24,8},{1,17},{9,25},{17,1},{25,9},{2,18},{10... | collective-permute-start | bytes 3538952 | tf_op jit(solution)/shard_map/ppermute | solution.py:528
  336.8 39.7 %collective-permute-start.46 = (bf16[1,3,384,512]{3,2,1,0:T(8,128)(2,1)S(1)}, bf16[1,3,384,512]{3,2,1,0:T(8,128)(2,1)}, u32[]{:S(2)}, u32[]{:S(2)}) collective-permute-start(bf16[1,3,384,512]{3,2,1,0:T(8,128)(2,1)S(1)} %copy-done.9), channel_id=1, source_target_pairs={{0,8},{8,0},{16,24},{24,16},{1,9},{9,1},{17,25},{25,17},{2,10},{10... | collective-permute-start | bytes 3538952 | tf_op jit(solution)/shard_map/ppermute | solution.py:528
  339.4 37.0 %collective-permute-start.45 = (bf16[1,3,384,256]{3,2,1,0:T(8,128)(2,1)S(1)}, bf16[1,3,384,256]{3,2,1,0:T(8,128)(2,1)}, u32[]{:S(2)}, u32[]{:S(2)}) collective-permute-start(bf16[1,3,384,256]{3,2,1,0:T(8,128)(2,1)S(1)} %copy-done.16), channel_id=1, source_target_pairs={{0,16},{8,24},{16,0},{24,8},{1,17},{9,25},{17,1},{25,9},{2,18},{10... | collective-permute-start | bytes 1769480 | tf_op jit(solution)/shard_map/ppermute | solution.py:528
  376.4 29.9 %collective-permute-start.51 = (bf16[1,3,384,512]{3,2,1,0:T(8,128)(2,1)}, bf16[1,3,384,512]{3,2,1,0:T(8,128)(2,1)}, u32[]{:S(2)}, u32[]{:S(2)}) collective-permute-start(bf16[1,3,384,512]{3,2,1,0:T(8,128)(2,1)} %get-tuple-element.487.one_ref), channel_id=1, source_target_pairs={{0,16},{8,24},{16,0},{24,8},{1,17},{9,25},{17,1},{25,9},{2,18},{10... | collective-permute-start | bytes 3538952 | tf_op jit(solution)/shard_map/ppermute | solution.py:528
  378.0 51.4 %collective-permute-start.52 = (bf16[1,3,384,512]{3,2,1,0:T(8,128)(2,1)}, bf16[1,3,384,512]{3,2,1,0:T(8,128)(2,1)}, u32[]{:S(2)}, u32[]{:S(2)}) collective-permute-start(bf16[1,3,384,512]{3,2,1,0:T(8,128)(2,1)} %get-tuple-element.490.one_ref), channel_id=1, source_target_pairs={{0,16},{8,24},{16,0},{24,8},{1,17},{9,25},{17,1},{25,9},{2,18},{10... | collective-permute-start | bytes 3538952 | tf_op jit(solution)/shard_map/ppermute | solution.py:528
  378.5 50.9 %collective-permute-start.53 = (bf16[1,3,384,512]{3,2,1,0:T(8,128)(2,1)}, bf16[1,3,384,512]{3,2,1,0:T(8,128)(2,1)}, u32[]{:S(2)}, u32[]{:S(2)}) collective-permute-start(bf16[1,3,384,512]{3,2,1,0:T(8,128)(2,1)} %added.22.half_ref), channel_id=1, source_target_pairs={{0,8},{8,0},{16,24},{24,16},{1,9},{9,1},{17,25},{25,17},{2,10},{10... | collective-permute-start | bytes 3538952 | tf_op jit(solution)/shard_map/ppermute | solution.py:528
  433.9 42.1 %collective-permute-start.58 = (bf16[1,3,384,512]{3,2,1,0:T(8,128)(2,1)}, bf16[1,3,384,512]{3,2,1,0:T(8,128)(2,1)}, u32[]{:S(2)}, u32[]{:S(2)}) collective-permute-start(bf16[1,3,384,512]{3,2,1,0:T(8,128)(2,1)} %get-tuple-element.514.one_ref), channel_id=1, source_target_pairs={{0,16},{8,24},{16,0},{24,8},{1,17},{9,25},{17,1},{25,9},{2,18},{10... | collective-permute-start | bytes 3538952 | tf_op jit(solution)/shard_map/ppermute | solution.py:528
  435.4 40.6 %collective-permute-start.59 = (bf16[1,3,384,512]{3,2,1,0:T(8,128)(2,1)}, bf16[1,3,384,512]{3,2,1,0:T(8,128)(2,1)}, u32[]{:S(2)}, u32[]{:S(2)}) collective-permute-start(bf16[1,3,384,512]{3,2,1,0:T(8,128)(2,1)} %added.23.half_ref), channel_id=1, source_target_pairs={{0,8},{8,0},{16,24},{24,16},{1,9},{9,1},{17,25},{25,17},{2,10},{10... | collective-permute-start | bytes 3538952 | tf_op jit(solution)/shard_map/ppermute | solution.py:528
  435.4 40.6 %collective-permute-start.60 = (bf16[1,3,384,256]{3,2,1,0:T(8,128)(2,1)}, bf16[1,3,384,256]{3,2,1,0:T(8,128)(2,1)}, u32[]{:S(2)}, u32[]{:S(2)}) collective-permute-start(bf16[1,3,384,256]{3,2,1,0:T(8,128)(2,1)} %added.24), channel_id=1, source_target_pairs={{0,8},{8,0},{16,24},{24,16},{1,9},{9,1},{17,25},{25,17},{2,10},{10... | collective-permute-start | bytes 1769480 | tf_op jit(solution)/shard_map/ppermute | solution.py:528
  444.1 31.8 %collective-permute-start.63 = (bf16[256,384]{1,0:T(8,128)(2,1)}, bf16[256,384]{1,0:T(8,128)(2,1)}, u32[]{:S(2)}, u32[]{:S(2)}) collective-permute-start(bf16[256,384]{1,0:T(8,128)(2,1)} %get-tuple-element.644), channel_id=1, source_target_pairs={{0,2},{1,3},{2,0},{3,1},{4,6},{5,7},{6,4},{7,5},{8,10},{9,11},{10,... | collective-permute-start | bytes 589832 | tf_op jit(solution)/shard_map/ppermute | solution.py:533
  446.6 29.4 %collective-permute-start.64 = (bf16[256,384]{1,0:T(8,128)(2,1)}, bf16[256,384]{1,0:T(8,128)(2,1)}, u32[]{:S(2)}, u32[]{:S(2)}) collective-permute-start(bf16[256,384]{1,0:T(8,128)(2,1)} %get-tuple-element.643), channel_id=1, source_target_pairs={{0,1},{1,2},{2,3},{3,0},{4,5},{5,6},{6,7},{7,4},{8,9},{9,10},{10,1... | collective-permute-start | bytes 589832 | tf_op jit(solution)/shard_map/ppermute | solution.py:533
  476.0 32.2 %collective-permute-start.65 = (bf16[1,3,384,512]{3,2,1,0:T(8,128)(2,1)}, bf16[1,3,384,512]{3,2,1,0:T(8,128)(2,1)}, u32[]{:S(2)}, u32[]{:S(2)}) collective-permute-start(bf16[1,3,384,512]{3,2,1,0:T(8,128)(2,1)} %get-tuple-element.530.one_ref), channel_id=1, source_target_pairs={{0,16},{8,24},{16,0},{24,8},{1,17},{9,25},{17,1},{25,9},{2,18},{10... | collective-permute-start | bytes 3538952 | tf_op jit(solution)/shard_map/ppermute | solution.py:528
  476.9 31.3 %collective-permute-start.66 = (bf16[1,3,384,512]{3,2,1,0:T(8,128)(2,1)}, bf16[1,3,384,512]{3,2,1,0:T(8,128)(2,1)}, u32[]{:S(2)}, u32[]{:S(2)}) collective-permute-start(bf16[1,3,384,512]{3,2,1,0:T(8,128)(2,1)} %added.25.half_ref), channel_id=1, source_target_pairs={{0,8},{8,0},{16,24},{24,16},{1,9},{9,1},{17,25},{25,17},{2,10},{10... | collective-permute-start | bytes 3538952 | tf_op jit(solution)/shard_map/ppermute | solution.py:528
  476.9 31.3 %collective-permute-start.67 = (bf16[1,3,384,512]{3,2,1,0:T(8,128)(2,1)S(1)}, bf16[1,3,384,512]{3,2,1,0:T(8,128)(2,1)}, u32[]{:S(2)}, u32[]{:S(2)}) collective-permute-start(bf16[1,3,384,512]{3,2,1,0:T(8,128)(2,1)S(1)} %copy-done.10), channel_id=1, source_target_pairs={{0,8},{8,0},{16,24},{24,16},{1,9},{9,1},{17,25},{25,17},{2,10},{10... | collective-permute-start | bytes 3538952 | tf_op jit(solution)/shard_map/ppermute | solution.py:528
  (106 other events, 1228.6 us)

commit v4 on v3

--- a/solution.py
+++ b/solution.py
@@ -615,23 +615,6 @@
     )(one, two)
 
 
-def join_kernel(one_ref, two_ref, pair_ref):
-    pl.when(pl.program_id(0) == 0)(lambda: pair_ref.__setitem__(Ellipsis, one_ref[...]))
-    pl.when(pl.program_id(0) == 1)(lambda: pair_ref.__setitem__(Ellipsis, two_ref[...]))
-
-
-def joined(one, two):
-    return pl.pallas_call(
-        join_kernel,
-        grid=(2,),
-        in_specs=[whole_block(one.shape)] * 2,
-        out_specs=pl.BlockSpec(one.shape, lambda i: (i,) + (0,) * (one.ndim - 1)),
-        out_shape=jax.ShapeDtypeStruct((2,) + one.shape[1:], BF16),
-        cost_estimate=LIGHT,
-        name="joined",
-    )(one, two)
-
-
 def pair_half(whole):
     core = lax.axis_index("dp") % 2
     halves = whole.reshape((2, whole.shape[0] // 2) + whole.shape[1:])
@@ -844,15 +827,15 @@
 
 def shared_kernel(
     place_ref, token_ref, token_peer_ref, cot_ref, cot_peer_ref, gate_ref, up_ref, down_ref, near_ref, far_ref,
-    own_grad_ref, other_grad_ref, out_ref, dx_ref, peer_ref,
+    out_in_ref, dx_in_ref, own_grad_ref, other_grad_ref, out_ref, dx_ref, peer_ref,
 ):
     step = pl.program_id(0)
 
     @pl.when(step == 0)
     def start():
         peer_ref[...] = near_ref[0]
-        out_ref[...] = jnp.zeros_like(out_ref)
-        dx_ref[...] = jnp.zeros_like(dx_ref)
+        out_ref[...] = out_in_ref[...]
+        dx_ref[...] = dx_in_ref[...]
 
     @pl.when(step > 0)
     def turn():
@@ -881,7 +864,7 @@
     pl.when(step > 0)(lambda: write(other_grad_ref))
 
 
-def run_shared(place, tokens_own, tokens_peer, cot_own, cot_peer, gate, up, down, near, far):
+def run_shared(place, tokens_own, tokens_peer, cot_own, cot_peer, gate, up, down, near, far, out_sum, dx_sum):
     tokens, features = tokens_own.shape
     hidden = gate.shape[2] // 2
     grads = jax.ShapeDtypeStruct((1, 3, features, hidden), BF16)
@@ -897,22 +880,24 @@
                 pl.BlockSpec((1, features, hidden), lambda i, place: (0, 0, place[i])),
                 pl.BlockSpec((1, hidden, features), lambda i, place: (0, place[i], 0)),
             ]
-            + [whole_block((1, 3, features, hidden))] * 2,
+            + [whole_block((1, 3, features, hidden))] * 2
+            + [whole_block((tokens, features))] * 2,
             out_specs=(whole_block(grads.shape),) * 2 + (whole_block(sums.shape),) * 2,
             scratch_shapes=[pltpu.VMEM((3, features, hidden), BF16)],
         ),
         out_shape=(grads, grads, sums, sums),
         cost_estimate=LIGHT,
         name="run_shared",
-    )(place, tokens_own, tokens_peer, cot_own, cot_peer, gate, up, down, near, far)
+    )(place, tokens_own, tokens_peer, cot_own, cot_peer, gate, up, down, near, far, out_sum, dx_sum)
 
 
 def experts_kernel(
     capacity,
     place_ref, rank_ref, prob_ref, token_ref, token_peer_ref, cot_ref, cot_peer_ref,
-    gate_ref, up_ref, down_ref, near_ref, far_ref, out_in_ref, dx_in_ref,
-    own_grad_ref, other_grad_ref, share_ref, out_ref, dx_ref, peer_ref,
+    gate_ref, up_ref, down_ref, *refs,
 ):
+    peer_refs, (out_in_ref, dx_in_ref) = refs[:4], refs[4:-6]
+    own_grad_ref, other_grad_ref, share_ref, out_ref, dx_ref, peer_ref = refs[-6:]
     step = pl.program_id(0)
 
     @pl.when(step == 0)
@@ -920,13 +905,8 @@
         out_ref[...] = out_in_ref[...]
         dx_ref[...] = dx_in_ref[...]
 
-    @pl.when(step < 2)
-    def first_pair():
-        peer_ref[...] = near_ref[0]
-
-    @pl.when(step >= 2)
-    def second_pair():
-        peer_ref[...] = far_ref[0]
+    for index, source_ref in enumerate(peer_refs):
+        pl.when(step == index)(lambda source_ref=source_ref: peer_ref.__setitem__(Ellipsis, source_ref[0]))
 
     mask = picks(rank_ref, capacity)
     chosen = ones_where(mask)
@@ -965,7 +945,7 @@
 
 
 def run_experts(
-    place, rank, probs, tokens_own, tokens_peer, cot_own, cot_peer, gate, up, down, near, far,
+    place, rank, probs, tokens_own, tokens_peer, cot_own, cot_peer, gate, up, down, peers,
     out_sum, dx_sum, first, capacity,
 ):
     tokens, features = out_sum.shape
@@ -988,11 +968,9 @@
                 at((features, hidden), first),
                 at((features, hidden), first),
                 at((hidden, features), first),
-                pl.BlockSpec(block, lambda i, place: (jnp.minimum(i, 1), 0, 0, 0)),
-                pl.BlockSpec(block, lambda i, place: (jnp.maximum(i, 2) - 2, 0, 0, 0)),
-                whole_block((tokens, features)),
-                whole_block((tokens, features)),
-            ],
+            ]
+            + [whole_block(block)] * 4
+            + [whole_block((tokens, features))] * 2,
             out_specs=(
                 pl.BlockSpec(block, lambda i, place: (place[jnp.minimum(i, 1)] // 2, 0, 0, 0)),
                 pl.BlockSpec(block, lambda i, place: (place[jnp.maximum(i, 2)] // 2, 0, 0, 0)),
@@ -1006,7 +984,7 @@
         cost_estimate=LIGHT,
         name="run_experts",
     )(
-        place, rank, probs, tokens_own, tokens_peer, cot_own, cot_peer, gate, up, down, near, far,
+        place, rank, probs, tokens_own, tokens_peer, cot_own, cot_peer, gate, up, down, *peers,
         out_sum, dx_sum,
     )
 
@@ -1096,7 +1074,6 @@
     place = jnp.stack([shards, shards ^ 2, shards ^ 1, shards ^ 3])
     sides = jnp.stack([shards % 2, 1 - shards % 2])
     firsts = list(range(0, experts, 4))
-    by_quarters = 2
 
     own_parts = col_parts(inputs)
     gain_high, gain_low = high_low(first_gain)
@@ -1107,16 +1084,17 @@
     peer_weight = swap(attend_in, "row")
     peer_parts = [peer_first[:tok_rest]] + [swap(part, "row") for part in own_parts[1:]]
     own_all = in_order(own_parts, "col").reshape(tok_block, feat_dev).astype(F32)
-    peer_all = in_order(peer_parts, "col").reshape(tok_block, feat_dev).astype(F32)
 
     shared_gate, shared_up, shared_down = shared_gate[None], shared_up[None], shared_down[None]
 
     def pack_experts(place, index):
         return pack(place, expert_gate, expert_up, expert_down, firsts[index], 1, 1)
 
-    late_place = held(place, peer_parts[1])
+    late_place = held(place, own_parts[1:])
     packed = [pack_experts(late_place, 0), pack_experts(late_place, 1)]
-
+    peer_parts[1] = held(peer_parts[1], packed)
+
+    peer_all = in_order(peer_parts, "col").reshape(tok_block, feat_dev).astype(F32)
     squares_one = jnp.sum(own_all * own_all, 1) + jnp.sum(peer_all * peer_all, 1)
     scale_all = lax.rsqrt(squares_one / feat_full + EPSILON)[:, None]
     unit_all = own_all * scale_all
@@ -1149,8 +1127,8 @@
     )[:, None, :]
     count_total = sum_by_swaps(jnp.sum(named.astype(F32), 1), ("dp",))
 
-    packed, place, sides, normed_own, normed_peer, peer_weight, cot_sent, count_total = stage(
-        packed, place, sides, normed_own, normed_peer, peer_weight, cotangent, count_total
+    packed, place, sides, normed_own, normed_peer, peer_weight, cot_sent, count_total, cosine, sine = stage(
+        packed, place, sides, normed_own, normed_peer, peer_weight, cotangent, count_total, cosine, sine
     )
     weights = [swap(packed[0], "row")]
     cot_parts = col_parts(cot_sent)
@@ -1158,7 +1136,7 @@
         normed_own, normed_peer, attend_in, peer_weight, attend_out, cosine, sine, start, block
     )
     late_place = held(place, out_partial)
-    packed += [pack_experts(late_place, 2), pack_experts(late_place, 3)]
+    packed += [pack_experts(late_place, 2), pack_experts(late_place[1:], 2)]
     weights, cot_parts, out_partial, packed, place = stage(weights, cot_parts, out_partial, packed, place)
 
     weights.append(swap(packed[1], "row"))
@@ -1166,8 +1144,8 @@
     cot_own = jnp.concatenate(cot_parts, 0)
     inputs_f = inputs.astype(F32)
     mixed_one = inputs_f + col_sum_rows(out_partial)
-    late_place, late_sides = held((place[1:], sides), cot_own)
-    packed.append(pack_experts(late_place, 3))
+    late_place, late_sides = held((place, sides), cot_own)
+    packed += [pack_experts(late_place, 3), pack_experts(late_place[1:], 3)]
     shared_packed = pack(late_sides, shared_gate, shared_up, shared_down, 0, 1, 2)
     weights, across, cot_own, mixed_one, shared_packed, packed = stage(
         weights, across, cot_own, mixed_one, shared_packed, packed
@@ -1181,7 +1159,8 @@
         ],
         1,
     )
-    stats = partial_stats + swap(partial_stats, "row")
+    peer_stats = swap(partial_stats, "row")
+    stats = partial_stats + peer_stats
     scale_two = lax.rsqrt(stats[:, :1] / feat_full + EPSILON)
     router_probs = jax.nn.softmax(stats[:, 1:] * scale_two, -1)
     unit_two = mixed_one * scale_two
@@ -1193,21 +1172,17 @@
 
     sent_parts = col_parts(normed_sent)
     cot_peer = swap(cot_own, "row")
-    shared_near = swap(shared_packed, "row")
-    near = [joined(weights[0], across)]
-    sent_parts, cot_peer, shared_near, near, weights, packed = stage(
-        sent_parts, cot_peer, shared_near, near, weights, packed
-    )
+    sent_parts, cot_peer, weights, across, packed = stage(sent_parts, cot_peer, weights, across, packed)
 
     opened = [split_rows(part, tok_rest, experts, tok_rest) for part in sent_parts]
     tokens_own = jnp.concatenate([part[0] for part in opened], 0)
     probs = jnp.concatenate([part[1] for part in opened], 1)[:, None, :]
     tokens_peer = swap(tokens_own, "row")
-    shared_far = swap(shared_near, "dp", 1)
-    far = [swap(near[0], "dp", 1)]
+    far = [swap(weights[0], "dp", 1), swap(across, "dp", 1)]
+    peers = [(weights[0], across)]
     across = swap(weights[1], "dp", 2)
-    tokens_own, tokens_peer, probs, shared_far, far, packed, weights = stage(
-        tokens_own, tokens_peer, probs, shared_far, far, packed, weights
+    tokens_own, tokens_peer, probs, far, packed, weights = stage(
+        tokens_own, tokens_peer, probs, far, packed, weights
     )
 
     ready, landed, totalled, arrived = [], [], [], []
@@ -1219,23 +1194,30 @@
         del ready[:count], totalled[:]
         return flights, returns
 
-    def follow(*values):
+    def follow(*values, flying=None, placing=True):
         for name, mine, theirs in landed:
-            totalled.append((name, added(held(mine, *values) if values else mine, theirs)[0]))
+            total = added(held(mine, *values) if values else mine, theirs)[0]
+            if flying:
+                flying[1].append((name, total, swap(total, "dp", 1)))
+            else:
+                totalled.append((name, total))
+        del landed[:]
+        if not placing:
+            return
         for name, total, rest in arrived:
             if isinstance(name, int):
                 turn = held(core, *values) if values else core
                 expert_grads[:] = spread(turn, total, rest, tuple(expert_grads), name, experts)
             else:
                 finished[name] = (total, rest)
-        del landed[:], arrived[:]
+        del arrived[:]
 
     def land(launched, *values):
         flights, returns = launched
         got = stage(flights_of(flights), flights_of(returns), flights_of(ready), flights_of(totalled),
                     expert_grads[3:], values)
         landed[:] = [(old[0],) + new for old, new in zip(flights, got[0])]
-        arrived[:] = [(old[0],) + new for old, new in zip(returns, got[1])]
+        arrived[:] = arrived + [(old[0],) + new for old, new in zip(returns, got[1])]
         ready[:] = [(old[0],) + new for old, new in zip(ready, got[2])]
         totalled[:] = [(old[0],) + new for old, new in zip(totalled, got[3])]
         expert_grads[3:] = got[4]
@@ -1248,70 +1230,78 @@
         for index, half in enumerate(added(held(mine, *values) if values else mine, theirs)):
             ready.append((name + 2 * index if isinstance(name, int) else name, half))
 
-    weights.append(swap(packed[2], "row"))
+    shares = []
+
+    def run(index, near, far, out_sum, dx_sum):
+        mine, other, share, out_new, dx_new = run_experts(
+            place, rank, probs, tokens_own, tokens_peer, cot_own, cot_peer,
+            expert_gate, expert_up, expert_down, tuple(near) + tuple(far), out_sum, dx_sum, firsts[index], capacity,
+        )
+        shares.append(share[:, 0])
+        return mine, other, out_new, dx_new
+
+    zeros = jnp.zeros((tok_block, feat_dev), F32)
+    third = swap(packed[2], "row")
+    mine, other, out_sum, dx_sum = run(0, peers[0], far, zeros, zeros)
+    third, across, weights, mine, other, out_sum, dx_sum, packed, shared_packed = stage(
+        third, across, weights, mine, other, out_sum, dx_sum, packed, shared_packed
+    )
+    near = (weights[1], across)
+    far = [swap(part, "dp", 1) for part in near]
+    pair_up(firsts[0], mine, swap(other, "dp", 1))
+    launched = launch(1)
+    third = [third, swap(packed[3], "row")]
+    shared_near = swap(shared_packed, "row")
+    mine, other, out_sum, dx_sum = run(1, near, far, out_sum, dx_sum)
+    third, mine, other, out_sum, dx_sum, packed, shared_near = land(
+        launched, third, mine, other, out_sum, dx_sum, packed, shared_near
+    )
+    launched = launch(1)
+    far = [swap(part, "dp", 1) for part in third]
+    fourth = swap(packed[4], "row")
+    shared_far = swap(shared_near, "dp", 1)
+    theirs = swap(other, "dp", 1)
+    earlier = mine
     shared_mine, shared_other, out_sum, dx_sum = run_shared(
         sides, tokens_own, tokens_peer, cot_own, cot_peer,
-        shared_gate, shared_up, shared_down, shared_near, shared_far,
-    )
-    weights, across, packed, out_sum, dx_sum, shared_mine, shared_other = stage(
-        weights, across, packed, out_sum, dx_sum, shared_mine, shared_other
-    )
-    near.append(joined(weights[1], across))
-    shares = []
-
-    def run(index):
-        mine, other, share, out_new, dx_new = run_experts(
-            place, rank, probs, tokens_own, tokens_peer, cot_own, cot_peer,
-            expert_gate, expert_up, expert_down, near[index], far[index], out_sum, dx_sum, firsts[index], capacity,
-        )
-        shares.append(share[:, 0])
-        return mine, other, out_new, dx_new
-
-    far.append(swap(near[1], "dp", 1))
-    weights.append(swap(packed[3], "row"))
-    across = swap(weights[2], "dp", 2)
-    mine, other, out_sum, dx_sum = run(0)
-    near.append(joined(held(weights[2], out_sum), across))
-    far, weights, mine, other, out_sum, dx_sum, packed, near = stage(
-        far, weights, mine, other, out_sum, dx_sum, packed, near
-    )
-    pair_up(firsts[0], mine, swap(other, "dp", 1))
+        shared_gate, shared_up, shared_down, shared_near, shared_far, out_sum, dx_sum,
+    )
+    pair_up(firsts[1], earlier, theirs, out_sum)
+    follow(out_sum, flying=launched)
+    far, third, fourth, out_sum, dx_sum, packed, shared_mine, shared_other = land(
+        launched, far, third, fourth, out_sum, dx_sum, packed, shared_mine, shared_other
+    )
     launched = launch(1)
-    far.append(swap(near[2], "dp", 1))
-    weights.append(swap(packed[4], "row"))
-    mine, other, out_sum, dx_sum = run(1)
-    near.append(joined(held(weights[3], out_sum), weights[4]))
-    far, mine, other, out_sum, dx_sum, near = land(launched, far, mine, other, out_sum, dx_sum, near)
+    fourth = [fourth, swap(packed[5], "row")]
+    fourth_far = [swap(fourth[0], "dp", 1)]
+    mine, other, out_sum, dx_sum = run(2, third, far, out_sum, dx_sum)
+    follow(out_sum)
+    fourth, fourth_far, mine, other, out_sum, dx_sum = land(
+        launched, fourth, fourth_far, mine, other, out_sum, dx_sum
+    )
     launched = launch(1)
-    far.append(swap(near[3], "dp", 1))
+    fourth_far.append(swap(fourth[1], "dp", 1))
     theirs = swap(other, "dp", 1)
     earlier = mine
-    mine, other, out_sum, dx_sum = run(2)
-    pair_up(firsts[1], earlier, theirs, out_sum)
-    follow(out_sum)
-    far, mine, other, out_sum, dx_sum = land(launched, far, mine, other, out_sum, dx_sum)
+    mine, other, out_sum, dx_sum = run(3, fourth, fourth_far, out_sum, dx_sum)
+    pair_up(firsts[2], earlier, theirs, out_sum)
+    follow(out_sum, placing=False)
+    mine, other, out_sum, dx_sum, shares, shared_mine, shared_other = land(
+        launched, mine, other, out_sum, dx_sum, shares, shared_mine, shared_other
+    )
+
     launched = launch(1)
-    theirs = swap(other, "dp", 1)
-    shared_theirs = swap(shared_other, "dp", 1)
-    earlier = mine
-    mine, other, out_sum, dx_sum = run(3)
-    pair_up("shared", shared_mine, shared_theirs, out_sum)
-    pair_up(firsts[2], earlier, theirs, out_sum)
-    follow(out_sum)
-    mine, other, out_sum, dx_sum, shares = land(launched, mine, other, out_sum, dx_sum, shares)
-
-    launched = launch(2)
     shares = jnp.concatenate(shares, 0)
     dx_blocks = []
     for step in range(col_size):
         rows = slice(step * tok_rest, (step + 1) * tok_rest)
         dx_blocks.append(with_rows(dx_sum[rows].astype(BF16), shares[:, rows]))
     dx_blocks = sent_back(dx_blocks)
-    theirs = swap(other, "dp", 1)
-    pair_up(firsts[3], mine, theirs, dx_blocks[1])
-    follow(dx_blocks[1])
-    (dx_blocks,) = land(launched, dx_blocks)
-    launched = launch(2)
+    follow(dx_blocks[1:], flying=launched)
+    dx_blocks, mine, other, shared_mine, shared_other = land(
+        launched, dx_blocks, mine, other, shared_mine, shared_other
+    )
+    launched = launch(1)
     normed_grad, gate_grad = split_rows(summed_up(dx_blocks), tok_rest, experts, tok_rest)
     prob_grad = gate_grad.T + experts * count_total / (2.0 * tokens_all * tokens_all)
     logit_grad = router_probs * (prob_grad - jnp.sum(router_probs * prob_grad, -1, keepdims=True))
@@ -1322,15 +1312,21 @@
     cot_f = cotangent.astype(F32)
     mixed_grad = cot_f + scale_two * (gained_two - unit_two * inner_two)
     mix_parts = col_parts(mixed_grad.astype(BF16))
-    follow(mix_parts[1])
-    mix_parts, logit_grad, two_grad = land(launched, mix_parts, logit_grad, two_grad)
+    theirs = swap(other, "dp", 1)
+    pair_up(firsts[3], mine, theirs, mix_parts[1:])
+    follow(mix_parts[1:], flying=launched)
+    mix_parts, logit_grad, two_grad, out_sum, shared_mine, shared_other = land(
+        launched, mix_parts, logit_grad, two_grad, out_sum, shared_mine, shared_other
+    )
 
     launched = launch(1)
     mix_all = in_order(mix_parts, "col").reshape(tok_block, feat_dev)
     attn_own = matmul(mix_all, attend_out, 1, 1).astype(BF16)
     attn_peer = swap(attn_own, "row")
-    out_low = held(out_sum.astype(BF16), mix_all)
+    out_low = out_sum.astype(BF16)
     out_blocks = sent_back([out_low[step * tok_rest : (step + 1) * tok_rest] for step in range(col_size)])
+    follow(attn_own, flying=launched)
+    attn_peer = held(attn_peer, [item[1] for item in launched[1]], expert_grads[3:])
     heads = attended.shape[0]
     attn_rows = attended.astype(BF16)
     attend_out_grad = jnp.concatenate(
@@ -1341,9 +1337,10 @@
     one_partial, attend_in_grad = attend_back(
         attn_own, attn_peer, qkv, attended, log_total, cosine, sine, start, normed_own, attend_in, block
     )
-    follow(one_partial)
-    one_partial, attend_in_grad, attend_out_grad, out_blocks, router_grad, second_gain_grad = land(
-        launched, one_partial, attend_in_grad, attend_out_grad, out_blocks, router_grad, second_gain_grad
+    shared_half = added(held(shared_mine, one_partial), swap(shared_other, "dp", 1))[0]
+    one_partial, attend_in_grad, attend_out_grad, out_blocks, router_grad, second_gain_grad, shared_half = land(
+        launched, one_partial, attend_in_grad, attend_out_grad, out_blocks, router_grad, second_gain_grad,
+        shared_half,
     )
 
     launched = launch(1)
@@ -1355,7 +1352,6 @@
             for step in range(col_size)
         ]
     )
-    layer_out = (mixed_one + summed_up(out_blocks)).astype(BF16)
     width = attend_in_grad.shape[1]
     attend_half = pair_half(
         jnp.concatenate([attend_in_grad, attend_out_grad.reshape(-1, width)], 0)
@@ -1366,12 +1362,13 @@
         [first_gain_grad[None], second_gain_grad[None], prob_sums[None], router_grad], 0
     )
     totals = totals + swap(totals, "dp", 1)
-    follow(one_blocks[1])
+    layer_out = (mixed_one + summed_up(out_blocks)).astype(BF16)
+    follow(one_blocks[1:], flying=launched)
     one_blocks, attend_half, totals = land(launched, one_blocks, attend_half, totals)
 
     totals = totals + swap(totals, "dp", 2)
-    ready.insert(0, ("attend", attend_half[None]))
-    launched = launch(2)
+    ready += [("attend", attend_half[None]), ("shared", shared_half)]
+    launched = launch(9)
     one_grad = summed_up(one_blocks)
     own_rows = col_index * tok_rest
     unit_one = rows_of(unit_all, own_rows, tok_rest)
@@ -1380,12 +1377,13 @@
     inner_one = jnp.sum(gained_one * unit_one, 1, keepdims=True)
     inner_one = (inner_one + swap(inner_one, "row")) / feat_full
     input_grad = (mixed_grad + scale_one * (gained_one - unit_one * inner_one)).astype(BF16)
-    follow()
+    follow(flying=launched)
     input_grad, totals = land(launched, input_grad, totals)
     totals = sum_by_swaps(totals, ("col",))
     while ready or landed or totalled or arrived:
         follow()
-        (totals,) = land(launch(2), totals)
+        launched = launch(9)
+        landed, arrived = landed + launched[0], arrived + launched[1]
 
     prob_total = totals[2, :experts]
     balance_loss = experts * jnp.sum(count_total / (2.0 * tokens_all) * prob_total / tokens_all)

time: 557 us -> 524 us (0.941)
  waiting for transfers between devices: 157 us -> 135 us
  local copies, waits for them, and re-layouts: 36.1 us -> 25.9 us
  starting transfers between devices: 77.6 us -> 86.2 us
  Pallas kernels: 244 us -> 237 us
    ppermute x57 -> x61, waiting for transfers between devices: 117 us -> 87.2 us  [swap(): return lax.ppermute(value, axis, [(i, i ^ step) for i in range(size)])]
    pallas_call x4 -> x0, Pallas kernels: 12.5 us -> none  [joined(): pl.pallas_call(join_kernel, grid=(2,), in_specs=[whole_block(one.shape)]...]
    dynamic_update_slice x12, local copies, waits for them, and re-layouts: 8.77 us -> 0.41 us  [in_order(): whole = lax.dynamic_update_index_in_dim(whole, part, (me - step) % size, 0)]
    ppermute x24, waiting for transfers between devices: 39.6 us -> 47.7 us  [shifted(): lax.ppermute(value, axis, [(i, (i + step) % size) for i in range(size)])]
    ppermute x57 -> x61, starting transfers between devices: 39.2 us -> 43 us  [swap(): return lax.ppermute(value, axis, [(i, i ^ step) for i in range(size)])]
    unnamed x125 -> x133, local copies, waits for them, and re-layouts: 14.4 us -> 11.2 us
    pallas_call x6 -> x7, Pallas kernels: 18.7 us -> 21.7 us  [pack(): pl.pallas_call(pack_kernel, grid_spec=pltpu.PrefetchScalarGridSpec(num_sc...]
  transfers between devices with their start and end apart: 81 -> 85, of which waited for: 25 -> 28; matrix products, arithmetic and copies ran while one was open for 9% -> 8% of each run, Pallas kernels for 43% -> 45%
where the time goes in v4:
time: 524 us; the launch traced here: 519 us
  Pallas kernels  237 us (45%)
  waiting for transfers between devices  135 us (26%)
  starting transfers between devices  86.2 us (16%)
  other arithmetic  27.2 us (5%)
  local copies, waits for them, and re-layouts  25.9 us (5%)
    pallas_call x4, Pallas kernels, run_experts(): pl.pallas_call(functools.partial(experts_kernel, capacity), grid_spec=plt...  89.5 us
    ppermute x61, waiting for transfers between devices, swap(): return lax.ppermute(value, axis, [(i, i ^ step) for i in range(size)])  87.2 us
    pallas_call x15, Pallas kernels, added(): pl.pallas_call(add_kernel, grid=(steps,), in_specs=[spec, spec], out_spec...  47.9 us
    ppermute x24, waiting for transfers between devices, shifted(): lax.ppermute(value, axis, [(i, (i + step) % size) for i in range(size)])  47.7 us
    ppermute x24, starting transfers between devices, shifted(): lax.ppermute(value, axis, [(i, (i + step) % size) for i in range(size)])  43.1 us
    ppermute x61, starting transfers between devices, swap(): return lax.ppermute(value, axis, [(i, i ^ step) for i in range(size)])  43 us
    pallas_call x8, Pallas kernels, spread(): pl.pallas_call(spread_kernel, grid_spec=pltpu.PrefetchScalarGridSpec(num_...  32.7 us
    pallas_call x7, Pallas kernels, pack(): pl.pallas_call(pack_kernel, grid_spec=pltpu.PrefetchScalarGridSpec(num_sc...  21.7 us
  transfers between devices with their start and end apart: 85, of which 28 were waited for; matrix products, arithmetic and copies ran while one was open for 8% of the time, Pallas kernels for 45%

profile of v4, /device:TPU:0, one launch (start us, length us, event | category | flops | bytes accessed | tf_op | source)
XLA Modules:
  0.0 518.9 jit_solution(18184458161657557749)
XLA Ops:
  33.9 6.9 %collective-permute-done.4 = bf16[256,384]{1,0:T(8,128)(2,1)S(1)} collective-permute-done((bf16[256,384]{1,0:T(8,128)(2,1)S(1)}, bf16[256,384]{1,0:T(8,128)(2,1)S(1)}, u32[]{:S(2)}, u32[]{:S(2)}) %collective-permute-start.4) | collective-permute-done | bytes 196640 | tf_op jit(solution)/shard_map/ppermute | solution.py:528
  40.9 4.2 collective-permute-done.5
  55.7 14.7 %attend.1 = (bf16[9,1024,64]{2,1,0:T(8,128)(2,1)}, f32[3,1024,64]{2,1,0:T(8,128)}, f32[3,1024,1]{2,1,0:T(8,128)}, bf16[1024,384]{1,0:T(8,128)(2,1)}) custom-call(bf16[1024,384]{1,0:T(8,128)(2,1)} %get-tuple-element.305.left_ref.normed_ref, bf16[1024,384]{1,0:T(8,128)(2,1)} %get-tuple-element.306.right_ref, bf16[384,576]{1,0:T(8,128)(2,1)} %copy-done.11, ...), custom_call_target="tpu_custom_call" | custom-call | flops 1 | bytes 1 | tf_op jit(solution)/shard_map/attend/pallas_call | solution.py:714
  98.4 4.8 collective-permute-done.14.refs_0_
  119.3 5.3 %collective-permute-done.21 = bf16[288,384]{1,0:T(8,128)(2,1)S(1)} collective-permute-done((bf16[288,384]{1,0:T(8,128)(2,1)S(1)}, bf16[288,384]{1,0:T(8,128)(2,1)S(1)}, u32[]{:S(2)}, u32[]{:S(2)}) %collective-permute-start.21) | collective-permute-done | bytes 221216 | tf_op jit(solution)/shard_map/ppermute | solution.py:533
  129.2 13.7 %collective-permute-done.24.token_peer_ref = bf16[1024,384]{1,0:T(8,128)(2,1)S(1)} collective-permute-done((bf16[1024,384]{1,0:T(8,128)(2,1)S(1)}, bf16[1024,384]{1,0:T(8,128)(2,1)S(1)}, u32[]{:S(2)}, u32[]{:S(2)}) %collective-permute-start.24) | collective-permute-done | bytes 786464 | tf_op jit(solution)/shard_map/ppermute | solution.py:528
  149.1 22.5 %run_experts.4 = (bf16[2,3,384,512]{3,2,1,0:T(8,128)(2,1)}, bf16[2,3,384,512]{3,2,1,0:T(8,128)(2,1)}, f32[4,1,1024]{2,1,0:T(1,128)}, f32[1024,384]{1,0:T(8,128)}, f32[1024,384]{1,0:T(8,128)}) custom-call(s32[4]{0:T(128)} %pad_add_fusion.1.place_ref, s32[16,1,1024]{2,1,0:T(1,128)} %broadcast_in_dim.145.rank_ref, f32[16,1,1024]{2,1,0:T(1,128)} %copy.86.prob_ref, ...), custom_call_target="tpu_custom_call" | custom-call | flops 1 | bytes 1 | tf_op jit(solution)/shard_map/run_experts/pallas_call | solution.py:960
  177.8 4.4 added.15
  184.2 22.3 %run_experts.5 = (bf16[2,3,384,512]{3,2,1,0:T(8,128)(2,1)}, bf16[2,3,384,512]{3,2,1,0:T(8,128)(2,1)}, f32[4,1,1024]{2,1,0:T(1,128)}, f32[1024,384]{1,0:T(8,128)}, f32[1024,384]{1,0:T(8,128)}) custom-call(s32[4]{0:T(128)} %pad_add_fusion.1.place_ref, s32[16,1,1024]{2,1,0:T(1,128)} %broadcast_in_dim.145.rank_ref, f32[16,1,1024]{2,1,0:T(1,128)} %copy.86.prob_ref, ...), custom_call_target="tpu_custom_call" | custom-call | flops 1 | bytes 1 | tf_op jit(solution)/shard_map/run_experts/pallas_call | solution.py:960
  206.5 6.8 %collective-permute-done.34.near_ref = bf16[1,3,384,256]{3,2,1,0:T(8,128)(2,1)S(1)} collective-permute-done((bf16[1,3,384,256]{3,2,1,0:T(8,128)(2,1)}, bf16[1,3,384,256]{3,2,1,0:T(8,128)(2,1)S(1)}, u32[]{:S(2)}, u32[]{:S(2)}) %collective-permute-start.34) | collective-permute-done | bytes 589856 | tf_op jit(solution)/shard_map/ppermute | solution.py:528
  220.8 13.3 %run_shared.1 = (bf16[1,3,384,256]{3,2,1,0:T(8,128)(2,1)}, bf16[1,3,384,256]{3,2,1,0:T(8,128)(2,1)}, f32[1024,384]{1,0:T(8,128)}, f32[1024,384]{1,0:T(8,128)}) custom-call(s32[2]{0:T(128)} %pad_add_fusion.2.place_ref, bf16[1024,384]{1,0:T(8,128)(2,1)} %copy-done.2, bf16[1024,384]{1,0:T(8,128)(2,1)} %copy-done.5, bf16[1024,384]{1,0:T(8,128)(2,1)} %copy-done.3, ...), custom_call_target="tpu_custom_call" | custom-call | flops 1 | bytes 1 | tf_op jit(solution)/shard_map/run_shared/pallas_call | solution.py:872
  238.5 4.4 added.17
  243.3 5.3 %collective-permute-done.41.refs_0_ = bf16[1,3,384,512]{3,2,1,0:T(8,128)(2,1)} collective-permute-done((bf16[1,3,384,512]{3,2,1,0:T(8,128)(2,1)}, bf16[1,3,384,512]{3,2,1,0:T(8,128)(2,1)}, u32[]{:S(2)}, u32[]{:S(2)}) %collective-permute-start.41) | collective-permute-done | bytes 1179680 | tf_op jit(solution)/shard_map/ppermute | solution.py:528
  250.7 22.2 %run_experts.6 = (bf16[2,3,384,512]{3,2,1,0:T(8,128)(2,1)}, bf16[2,3,384,512]{3,2,1,0:T(8,128)(2,1)}, f32[4,1,1024]{2,1,0:T(1,128)}, f32[1024,384]{1,0:T(8,128)}, f32[1024,384]{1,0:T(8,128)}) custom-call(s32[4]{0:T(128)} %pad_add_fusion.1.place_ref, s32[16,1,1024]{2,1,0:T(1,128)} %broadcast_in_dim.145.rank_ref, f32[16,1,1024]{2,1,0:T(1,128)} %copy.86.prob_ref, ...), custom_call_target="tpu_custom_call" | custom-call | flops 1 | bytes 1 | tf_op jit(solution)/shard_map/run_experts/pallas_call | solution.py:960
  275.9 4.2 spread.8
  281.5 5.4 %collective-permute-done.47.refs_3_ = bf16[1,3,384,512]{3,2,1,0:T(8,128)(2,1)} collective-permute-done((bf16[1,3,384,512]{3,2,1,0:T(8,128)(2,1)S(1)}, bf16[1,3,384,512]{3,2,1,0:T(8,128)(2,1)}, u32[]{:S(2)}, u32[]{:S(2)}) %collective-permute-start.47) | collective-permute-done | bytes 1179680 | tf_op jit(solution)/shard_map/ppermute | solution.py:528
  286.9 22.5 %run_experts.7 = (bf16[2,3,384,512]{3,2,1,0:T(8,128)(2,1)}, bf16[2,3,384,512]{3,2,1,0:T(8,128)(2,1)}, f32[4,1,1024]{2,1,0:T(1,128)}, f32[1024,384]{1,0:T(8,128)}, f32[1024,384]{1,0:T(8,128)}) custom-call(s32[4]{0:T(128)} %pad_add_fusion.1.place_ref, s32[16,1,1024]{2,1,0:T(1,128)} %broadcast_in_dim.145.rank_ref, f32[16,1,1024]{2,1,0:T(1,128)} %copy.86.prob_ref, ...), custom_call_target="tpu_custom_call" | custom-call | flops 1 | bytes 1 | tf_op jit(solution)/shard_map/run_experts/pallas_call | solution.py:960
  312.4 4.5 added.19
  317.8 4.8 collective-permute-start.53
  329.0 9.1 %collective-permute-done.52 = bf16[288,384]{1,0:T(8,128)(2,1)S(1)} collective-permute-done((bf16[288,384]{1,0:T(8,128)(2,1)S(1)}, bf16[288,384]{1,0:T(8,128)(2,1)S(1)}, u32[]{:S(2)}, u32[]{:S(2)}) %collective-permute-start.52) | collective-permute-done | bytes 221216 | tf_op jit(solution)/shard_map/ppermute | solution.py:533
  342.7 4.1 spread.9
  346.8 6.4 %collective-permute-done.49.two_ref = bf16[1,3,384,512]{3,2,1,0:T(8,128)(2,1)} collective-permute-done((bf16[1,3,384,512]{3,2,1,0:T(8,128)(2,1)}, bf16[1,3,384,512]{3,2,1,0:T(8,128)(2,1)}, u32[]{:S(2)}, u32[]{:S(2)}) %collective-permute-start.49) | collective-permute-done | bytes 1179680 | tf_op jit(solution)/shard_map/ppermute | solution.py:528
  364.0 5.3 %collective-permute-done.57 = bf16[256,384]{1,0:T(8,128)(2,1)S(1)} collective-permute-done((bf16[256,384]{1,0:T(8,128)(2,1)S(1)}, bf16[256,384]{1,0:T(8,128)(2,1)S(1)}, u32[]{:S(2)}, u32[]{:S(2)}) %collective-permute-start.57) | collective-permute-done | bytes 196640 | tf_op jit(solution)/shard_map/ppermute | solution.py:533
  369.4 6.5 %collective-permute-done.58 = bf16[256,384]{1,0:T(8,128)(2,1)S(1)} collective-permute-done((bf16[256,384]{1,0:T(8,128)(2,1)S(1)}, bf16[256,384]{1,0:T(8,128)(2,1)S(1)}, u32[]{:S(2)}, u32[]{:S(2)}) %collective-permute-start.58) | collective-permute-done | bytes 196640 | tf_op jit(solution)/shard_map/ppermute | solution.py:533
  379.2 4.1 spread.10
  387.4 4.4 added.23
  413.0 17.0 %attend_back.1 = (f32[1024,384]{1,0:T(8,128)}, bf16[384,576]{1,0:T(8,128)(2,1)}) custom-call(bf16[1024,192]{1,0:T(8,128)(2,1)} %copy-done.17, bf16[1024,192]{1,0:T(8,128)(2,1)} %collective-permute-done.64.peer_ref, bf16[9,1024,64]{2,1,0:T(8,128)(2,1)} %get-tuple-element.525.qkv_ref, f32[3,1024,64]{2,1,0:T(8,128)} %get-tuple-element.526.attended_ref, ...), custom_call_target="tpu_custom_call" | custom-call | flops 1 | bytes 1 | tf_op jit(solution)/shard_map/attend_back/pallas_call | solution.py:767
  443.7 10.8 %collective-permute-done.71 = bf16[256,384]{1,0:T(8,128)(2,1)S(1)} collective-permute-done((bf16[256,384]{1,0:T(8,128)(2,1)S(1)}, bf16[256,384]{1,0:T(8,128)(2,1)S(1)}, u32[]{:S(2)}, u32[]{:S(2)}) %collective-permute-start.71) | collective-permute-done | bytes 196640 | tf_op jit(solution)/shard_map/ppermute | solution.py:533
  461.8 4.1 spread.13
  483.3 4.9 collective-permute-done.80
  488.2 6.3 %collective-permute-done.76.two_ref = bf16[1,256,576]{2,1,0:T(8,128)(2,1)} collective-permute-done((bf16[1,256,576]{2,1,0:T(8,128)(2,1)}, bf16[1,256,576]{2,1,0:T(8,128)(2,1)}, u32[]{:S(2)}, u32[]{:S(2)}) %collective-permute-start.76) | collective-permute-done | bytes 294944 | tf_op jit(solution)/shard_map/ppermute | solution.py:528
  505.6 4.1 spread.15
  (444 shorter events, 235.5 us)
Async XLA Ops:
  9.5 24.2 %collective-permute-start.3 = (bf16[264,384]{1,0:T(8,128)(2,1)S(1)}, bf16[264,384]{1,0:T(8,128)(2,1)S(1)}, u32[]{:S(2)}, u32[]{:S(2)}) collective-permute-start(bf16[264,384]{1,0:T(8,128)(2,1)S(1)} %pad_maximum_fusion.7), channel_id=1, source_target_pairs={{0,4},{4,0},{1,5},{5,1},{2,6},{6,2},{3,7},{7,3},{8,12},{12,8},{9,1... | collective-permute-start | bytes 608264 | tf_op jit(solution)/shard_map/ppermute | solution.py:528
  22.5 27.5 %collective-permute-start.7 = (bf16[384,576]{1,0:T(8,128)(2,1)S(1)}, bf16[384,576]{1,0:T(8,128)(2,1)}, u32[]{:S(2)}, u32[]{:S(2)}) collective-permute-start(bf16[384,576]{1,0:T(8,128)(2,1)S(1)} %copy.79.weight_left_ref.weight_ref), channel_id=1, source_target_pairs={{0,4},{4,0},{1,5},{5,1},{2,6},{6,2},{3,7},{7,3},{8,12},{12,8},{9,1... | collective-permute-start | bytes 1327112 | tf_op jit(solution)/shard_map/ppermute | solution.py:528
  50.0 27.5 %collective-permute-start.10 = (bf16[1,3,384,512]{3,2,1,0:T(8,128)(2,1)S(1)}, bf16[1,3,384,512]{3,2,1,0:T(8,128)(2,1)}, u32[]{:S(2)}, u32[]{:S(2)}) collective-permute-start(bf16[1,3,384,512]{3,2,1,0:T(8,128)(2,1)S(1)} %copy-done.26), channel_id=1, source_target_pairs={{0,4},{4,0},{1,5},{5,1},{2,6},{6,2},{3,7},{7,3},{8,12},{12,8},{9,1... | collective-permute-start | bytes 3538952 | tf_op jit(solution)/shard_map/ppermute | solution.py:528
  50.7 26.7 %collective-permute-start.11 = (bf16[256,384]{1,0:T(8,128)(2,1)S(1)}, bf16[256,384]{1,0:T(8,128)(2,1)S(1)}, u32[]{:S(2)}, u32[]{:S(2)}) collective-permute-start(bf16[256,384]{1,0:T(8,128)(2,1)S(1)} %copy-done.18), channel_id=1, source_target_pairs={{0,1},{1,2},{2,3},{3,0},{4,5},{5,6},{6,7},{7,4},{8,9},{9,10},{10,1... | collective-permute-start | bytes 589832 | tf_op jit(solution)/shard_map/ppermute | solution.py:533
  51.8 25.6 %collective-permute-start.12 = (bf16[256,384]{1,0:T(8,128)(2,1)S(1)}, bf16[256,384]{1,0:T(8,128)(2,1)S(1)}, u32[]{:S(2)}, u32[]{:S(2)}) collective-permute-start(bf16[256,384]{1,0:T(8,128)(2,1)S(1)} %copy-done.18), channel_id=1, source_target_pairs={{0,2},{1,3},{2,0},{3,1},{4,6},{5,7},{6,4},{7,5},{8,10},{9,11},{10,... | collective-permute-start | bytes 589832 | tf_op jit(solution)/shard_map/ppermute | solution.py:533
  51.9 25.6 %collective-permute-start.13 = (bf16[256,384]{1,0:T(8,128)(2,1)S(1)}, bf16[256,384]{1,0:T(8,128)(2,1)S(1)}, u32[]{:S(2)}, u32[]{:S(2)}) collective-permute-start(bf16[256,384]{1,0:T(8,128)(2,1)S(1)} %copy-done.18), channel_id=1, source_target_pairs={{0,3},{1,0},{2,1},{3,2},{4,7},{5,4},{6,5},{7,6},{8,11},{9,8},{10,9... | collective-permute-start | bytes 589832 | tf_op jit(solution)/shard_map/ppermute | solution.py:533
  77.5 25.7 %collective-permute-start.14 = (bf16[1,3,384,512]{3,2,1,0:T(8,128)(2,1)}, bf16[1,3,384,512]{3,2,1,0:T(8,128)(2,1)S(1)}, u32[]{:S(2)}, u32[]{:S(2)}) collective-permute-start(bf16[1,3,384,512]{3,2,1,0:T(8,128)(2,1)} %pack.8), channel_id=1, source_target_pairs={{0,4},{4,0},{1,5},{5,1},{2,6},{6,2},{3,7},{7,3},{8,12},{12,8},{9,1... | collective-permute-start | bytes 3538952 | tf_op jit(solution)/shard_map/ppermute | solution.py:528
  79.0 25.5 %collective-permute-start.15 = (bf16[1,3,384,512]{3,2,1,0:T(8,128)(2,1)}, bf16[1,3,384,512]{3,2,1,0:T(8,128)(2,1)}, u32[]{:S(2)}, u32[]{:S(2)}) collective-permute-start(bf16[1,3,384,512]{3,2,1,0:T(8,128)(2,1)} %collective-permute-done.10.refs_0_), channel_id=1, source_target_pairs={{0,16},{8,24},{16,0},{24,8},{1,17},{9,25},{17,1},{25,9},{2,18},{10... | collective-permute-start | bytes 3538952 | tf_op jit(solution)/shard_map/ppermute | solution.py:528
  127.6 43.9 %collective-permute-start.28 = (bf16[1,3,384,512]{3,2,1,0:T(8,128)(2,1)S(1)}, bf16[1,3,384,512]{3,2,1,0:T(8,128)(2,1)}, u32[]{:S(2)}, u32[]{:S(2)}) collective-permute-start(bf16[1,3,384,512]{3,2,1,0:T(8,128)(2,1)S(1)} %copy-done.23), channel_id=1, source_target_pairs={{0,16},{8,24},{16,0},{24,8},{1,17},{9,25},{17,1},{25,9},{2,18},{10... | collective-permute-start | bytes 3538952 | tf_op jit(solution)/shard_map/ppermute | solution.py:528
  142.9 28.6 %collective-permute-start.27 = (bf16[1,3,384,512]{3,2,1,0:T(8,128)(2,1)}, bf16[1,3,384,512]{3,2,1,0:T(8,128)(2,1)}, u32[]{:S(2)}, u32[]{:S(2)}) collective-permute-start(bf16[1,3,384,512]{3,2,1,0:T(8,128)(2,1)} %pack.9), channel_id=1, source_target_pairs={{0,4},{4,0},{1,5},{5,1},{2,6},{6,2},{3,7},{7,3},{8,12},{12,8},{9,1... | collective-permute-start | bytes 3538952 | tf_op jit(solution)/shard_map/ppermute | solution.py:528
  172.2 41.2 %collective-permute-start.31 = (bf16[1,3,384,512]{3,2,1,0:T(8,128)(2,1)}, bf16[1,3,384,512]{3,2,1,0:T(8,128)(2,1)}, u32[]{:S(2)}, u32[]{:S(2)}) collective-permute-start(bf16[1,3,384,512]{3,2,1,0:T(8,128)(2,1)} %pack.10), channel_id=1, source_target_pairs={{0,4},{4,0},{1,5},{5,1},{2,6},{6,2},{3,7},{7,3},{8,12},{12,8},{9,1... | collective-permute-start | bytes 3538952 | tf_op jit(solution)/shard_map/ppermute | solution.py:528
  182.1 31.2 %collective-permute-start.30 = (bf16[1,3,384,512]{3,2,1,0:T(8,128)(2,1)}, bf16[1,3,384,512]{3,2,1,0:T(8,128)(2,1)S(1)}, u32[]{:S(2)}, u32[]{:S(2)}) collective-permute-start(bf16[1,3,384,512]{3,2,1,0:T(8,128)(2,1)} %get-tuple-element.392.one_ref), channel_id=1, source_target_pairs={{0,16},{8,24},{16,0},{24,8},{1,17},{9,25},{17,1},{25,9},{2,18},{10... | collective-permute-start | bytes 3538952 | tf_op jit(solution)/shard_map/ppermute | solution.py:528
  183.7 29.7 %collective-permute-start.34 = (bf16[1,3,384,256]{3,2,1,0:T(8,128)(2,1)}, bf16[1,3,384,256]{3,2,1,0:T(8,128)(2,1)S(1)}, u32[]{:S(2)}, u32[]{:S(2)}) collective-permute-start(bf16[1,3,384,256]{3,2,1,0:T(8,128)(2,1)} %pack.11), channel_id=1, source_target_pairs={{0,4},{4,0},{1,5},{5,1},{2,6},{6,2},{3,7},{7,3},{8,12},{12,8},{9,1... | collective-permute-start | bytes 1769480 | tf_op jit(solution)/shard_map/ppermute | solution.py:528
  215.1 28.2 %collective-permute-start.35 = (bf16[1,3,384,512]{3,2,1,0:T(8,128)(2,1)}, bf16[1,3,384,512]{3,2,1,0:T(8,128)(2,1)}, u32[]{:S(2)}, u32[]{:S(2)}) collective-permute-start(bf16[1,3,384,512]{3,2,1,0:T(8,128)(2,1)} %get-tuple-element.416.one_ref), channel_id=1, source_target_pairs={{0,16},{8,24},{16,0},{24,8},{1,17},{9,25},{17,1},{25,9},{2,18},{10... | collective-permute-start | bytes 3538952 | tf_op jit(solution)/shard_map/ppermute | solution.py:528
  216.6 26.7 %collective-permute-start.39 = (bf16[1,3,384,512]{3,2,1,0:T(8,128)(2,1)}, bf16[1,3,384,512]{3,2,1,0:T(8,128)(2,1)}, u32[]{:S(2)}, u32[]{:S(2)}) collective-permute-start(bf16[1,3,384,512]{3,2,1,0:T(8,128)(2,1)} %collective-permute-done.27.refs_0_), channel_id=1, source_target_pairs={{0,8},{8,0},{16,24},{24,16},{1,9},{9,1},{17,25},{25,17},{2,10},{10... | collective-permute-start | bytes 3538952 | tf_op jit(solution)/shard_map/ppermute | solution.py:528
  216.6 26.7 %collective-permute-start.40 = (bf16[1,3,384,512]{3,2,1,0:T(8,128)(2,1)}, bf16[1,3,384,512]{3,2,1,0:T(8,128)(2,1)}, u32[]{:S(2)}, u32[]{:S(2)}) collective-permute-start(bf16[1,3,384,512]{3,2,1,0:T(8,128)(2,1)} %collective-permute-done.31.refs_1_), channel_id=1, source_target_pairs={{0,8},{8,0},{16,24},{24,16},{1,9},{9,1},{17,25},{25,17},{2,10},{10... | collective-permute-start | bytes 3538952 | tf_op jit(solution)/shard_map/ppermute | solution.py:528
  220.3 28.3 %collective-permute-start.41 = (bf16[1,3,384,512]{3,2,1,0:T(8,128)(2,1)}, bf16[1,3,384,512]{3,2,1,0:T(8,128)(2,1)}, u32[]{:S(2)}, u32[]{:S(2)}) collective-permute-start(bf16[1,3,384,512]{3,2,1,0:T(8,128)(2,1)} %pack.12), channel_id=1, source_target_pairs={{0,4},{4,0},{1,5},{5,1},{2,6},{6,2},{3,7},{7,3},{8,12},{12,8},{9,1... | collective-permute-start | bytes 3538952 | tf_op jit(solution)/shard_map/ppermute | solution.py:528
  248.6 31.4 %collective-permute-start.42 = (bf16[1,3,384,512]{3,2,1,0:T(8,128)(2,1)}, bf16[1,3,384,512]{3,2,1,0:T(8,128)(2,1)}, u32[]{:S(2)}, u32[]{:S(2)}) collective-permute-start(bf16[1,3,384,512]{3,2,1,0:T(8,128)(2,1)} %get-tuple-element.441.one_ref), channel_id=1, source_target_pairs={{0,16},{8,24},{16,0},{24,8},{1,17},{9,25},{17,1},{25,9},{2,18},{10... | collective-permute-start | bytes 3538952 | tf_op jit(solution)/shard_map/ppermute | solution.py:528
  250.2 29.9 %collective-permute-start.43 = (bf16[1,3,384,512]{3,2,1,0:T(8,128)(2,1)}, bf16[1,3,384,512]{3,2,1,0:T(8,128)(2,1)S(1)}, u32[]{:S(2)}, u32[]{:S(2)}) collective-permute-start(bf16[1,3,384,512]{3,2,1,0:T(8,128)(2,1)} %pack.13), channel_id=1, source_target_pairs={{0,4},{4,0},{1,5},{5,1},{2,6},{6,2},{3,7},{7,3},{8,12},{12,8},{9,1... | collective-permute-start | bytes 3538952 | tf_op jit(solution)/shard_map/ppermute | solution.py:528
  250.7 29.4 %collective-permute-start.44 = (bf16[1,3,384,512]{3,2,1,0:T(8,128)(2,1)}, bf16[1,3,384,512]{3,2,1,0:T(8,128)(2,1)}, u32[]{:S(2)}, u32[]{:S(2)}) collective-permute-start(bf16[1,3,384,512]{3,2,1,0:T(8,128)(2,1)} %collective-permute-done.41.refs_0_), channel_id=1, source_target_pairs={{0,8},{8,0},{16,24},{24,16},{1,9},{9,1},{17,25},{25,17},{2,10},{10... | collective-permute-start | bytes 3538952 | tf_op jit(solution)/shard_map/ppermute | solution.py:528
  280.1 32.3 %collective-permute-start.48 = (bf16[2,3,384,512]{3,2,1,0:T(8,128)(2,1)}, bf16[2,3,384,512]{3,2,1,0:T(8,128)(2,1)}, u32[]{:S(2)}, u32[]{:S(2)}) collective-permute-start(bf16[2,3,384,512]{3,2,1,0:T(8,128)(2,1)} %get-tuple-element.437), channel_id=1, source_target_pairs={{0,8},{8,0},{16,24},{24,16},{1,9},{9,1},{17,25},{25,17},{2,10},{10... | collective-permute-start | bytes 7077896 | tf_op jit(solution)/shard_map/ppermute | solution.py:528
  280.7 36.1 %collective-permute-start.45 = (bf16[1,3,384,512]{3,2,1,0:T(8,128)(2,1)}, bf16[1,3,384,512]{3,2,1,0:T(8,128)(2,1)}, u32[]{:S(2)}, u32[]{:S(2)}) collective-permute-start(bf16[1,3,384,512]{3,2,1,0:T(8,128)(2,1)} %get-tuple-element.461.one_ref), channel_id=1, source_target_pairs={{0,16},{8,24},{16,0},{24,8},{1,17},{9,25},{17,1},{25,9},{2,18},{10... | collective-permute-start | bytes 3538952 | tf_op jit(solution)/shard_map/ppermute | solution.py:528
  281.3 35.6 %collective-permute-start.46 = (bf16[1,3,384,512]{3,2,1,0:T(8,128)(2,1)S(1)}, bf16[1,3,384,512]{3,2,1,0:T(8,128)(2,1)}, u32[]{:S(2)}, u32[]{:S(2)}) collective-permute-start(bf16[1,3,384,512]{3,2,1,0:T(8,128)(2,1)S(1)} %copy-done.10), channel_id=1, source_target_pairs={{0,8},{8,0},{16,24},{24,16},{1,9},{9,1},{17,25},{25,17},{2,10},{10... | collective-permute-start | bytes 3538952 | tf_op jit(solution)/shard_map/ppermute | solution.py:528
  325.2 28.0 %collective-permute-start.49 = (bf16[1,3,384,512]{3,2,1,0:T(8,128)(2,1)}, bf16[1,3,384,512]{3,2,1,0:T(8,128)(2,1)}, u32[]{:S(2)}, u32[]{:S(2)}) collective-permute-start(bf16[1,3,384,512]{3,2,1,0:T(8,128)(2,1)} %get-tuple-element.483.one_ref), channel_id=1, source_target_pairs={{0,16},{8,24},{16,0},{24,8},{1,17},{9,25},{17,1},{25,9},{2,18},{10... | collective-permute-start | bytes 3538952 | tf_op jit(solution)/shard_map/ppermute | solution.py:528
  325.7 27.5 %collective-permute-start.50 = (bf16[1,3,384,512]{3,2,1,0:T(8,128)(2,1)S(1)}, bf16[1,3,384,512]{3,2,1,0:T(8,128)(2,1)S(1)}, u32[]{:S(2)}, u32[]{:S(2)}) collective-permute-start(bf16[1,3,384,512]{3,2,1,0:T(8,128)(2,1)S(1)} %copy-done.9), channel_id=1, source_target_pairs={{0,8},{8,0},{16,24},{24,16},{1,9},{9,1},{17,25},{25,17},{2,10},{10... | collective-permute-start | bytes 3538952 | tf_op jit(solution)/shard_map/ppermute | solution.py:528
  353.2 34.2 %collective-permute-start.61 = (bf16[2,3,384,512]{3,2,1,0:T(8,128)(2,1)}, bf16[2,3,384,512]{3,2,1,0:T(8,128)(2,1)}, u32[]{:S(2)}, u32[]{:S(2)}) collective-permute-start(bf16[2,3,384,512]{3,2,1,0:T(8,128)(2,1)} %get-tuple-element.487), channel_id=1, source_target_pairs={{0,8},{8,0},{16,24},{24,16},{1,9},{9,1},{17,25},{25,17},{2,10},{10... | collective-permute-start | bytes 7077896 | tf_op jit(solution)/shard_map/ppermute | solution.py:528
  363.5 28.3 %collective-permute-start.55 = (bf16[1,3,384,512]{3,2,1,0:T(8,128)(2,1)}, bf16[1,3,384,512]{3,2,1,0:T(8,128)(2,1)}, u32[]{:S(2)}, u32[]{:S(2)}) collective-permute-start(bf16[1,3,384,512]{3,2,1,0:T(8,128)(2,1)} %get-tuple-element.513.one_ref), channel_id=1, source_target_pairs={{0,16},{8,24},{16,0},{24,8},{1,17},{9,25},{17,1},{25,9},{2,18},{10... | collective-permute-start | bytes 3538952 | tf_op jit(solution)/shard_map/ppermute | solution.py:528
  398.3 34.0 %collective-permute-start.63 = (bf16[1,3,384,512]{3,2,1,0:T(8,128)(2,1)}, bf16[1,3,384,512]{3,2,1,0:T(8,128)(2,1)}, u32[]{:S(2)}, u32[]{:S(2)}) collective-permute-start(bf16[1,3,384,512]{3,2,1,0:T(8,128)(2,1)} %added.24.half_ref), channel_id=1, source_target_pairs={{0,8},{8,0},{16,24},{24,16},{1,9},{9,1},{17,25},{25,17},{2,10},{10... | collective-permute-start | bytes 3538952 | tf_op jit(solution)/shard_map/ppermute | solution.py:528
  400.1 32.2 %collective-permute-start.62 = (bf16[1,3,384,512]{3,2,1,0:T(8,128)(2,1)}, bf16[1,3,384,512]{3,2,1,0:T(8,128)(2,1)}, u32[]{:S(2)}, u32[]{:S(2)}) collective-permute-start(bf16[1,3,384,512]{3,2,1,0:T(8,128)(2,1)} %get-tuple-element.543.one_ref), channel_id=1, source_target_pairs={{0,16},{8,24},{16,0},{24,8},{1,17},{9,25},{17,1},{25,9},{2,18},{10... | collective-permute-start | bytes 3538952 | tf_op jit(solution)/shard_map/ppermute | solution.py:528
  401.9 30.4 %collective-permute-start.65 = (bf16[256,384]{1,0:T(8,128)(2,1)}, bf16[256,384]{1,0:T(8,128)(2,1)}, u32[]{:S(2)}, u32[]{:S(2)}) collective-permute-start(bf16[256,384]{1,0:T(8,128)(2,1)} %get-tuple-element.657), channel_id=1, source_target_pairs={{0,3},{1,0},{2,1},{3,2},{4,7},{5,4},{6,5},{7,6},{8,11},{9,8},{10,9... | collective-permute-start | bytes 589832 | tf_op jit(solution)/shard_map/ppermute | solution.py:533
  439.4 27.3 %collective-permute-start.69 = (bf16[1,3,384,512]{3,2,1,0:T(8,128)(2,1)}, bf16[1,3,384,512]{3,2,1,0:T(8,128)(2,1)}, u32[]{:S(2)}, u32[]{:S(2)}) collective-permute-start(bf16[1,3,384,512]{3,2,1,0:T(8,128)(2,1)} %get-tuple-element.559.one_ref), channel_id=1, source_target_pairs={{0,16},{8,24},{16,0},{24,8},{1,17},{9,25},{17,1},{25,9},{2,18},{10... | collective-permute-start | bytes 3538952 | tf_op jit(solution)/shard_map/ppermute | solution.py:528
  470.8 23.7 %collective-permute-start.78 = (bf16[1,3,384,512]{3,2,1,0:T(8,128)(2,1)}, bf16[1,3,384,512]{3,2,1,0:T(8,128)(2,1)}, u32[]{:S(2)}, u32[]{:S(2)}) collective-permute-start(bf16[1,3,384,512]{3,2,1,0:T(8,128)(2,1)} %added.27.half_ref), channel_id=1, source_target_pairs={{0,8},{8,0},{16,24},{24,16},{1,9},{9,1},{17,25},{25,17},{2,10},{10... | collective-permute-start | bytes 3538952 | tf_op jit(solution)/shard_map/ppermute | solution.py:528
  (114 other events, 1172.9 us)

commit v5 on v4

--- a/solution.py
+++ b/solution.py
@@ -1366,7 +1366,7 @@
     follow(one_blocks[1:], flying=launched)
     one_blocks, attend_half, totals = land(launched, one_blocks, attend_half, totals)
 
-    totals = totals + swap(totals, "dp", 2)
+    totals = sum_by_swaps(totals, ("col",))
     ready += [("attend", attend_half[None]), ("shared", shared_half)]
     launched = launch(9)
     one_grad = summed_up(one_blocks)
@@ -1378,8 +1378,11 @@
     inner_one = (inner_one + swap(inner_one, "row")) / feat_full
     input_grad = (mixed_grad + scale_one * (gained_one - unit_one * inner_one)).astype(BF16)
     follow(flying=launched)
+    arrived += launched[1]
+    del launched[1][:]
+    follow()
     input_grad, totals = land(launched, input_grad, totals)
-    totals = sum_by_swaps(totals, ("col",))
+    totals = totals + swap(totals, "dp", 2)
     while ready or landed or totalled or arrived:
         follow()
         launched = launch(9)

time: 524 us -> 517 us (0.987)
  waiting for transfers between devices: 135 us -> 126 us
    ppermute x61, waiting for transfers between devices: 87.2 us -> 78.6 us  [swap(): return lax.ppermute(value, axis, [(i, i ^ step) for i in range(size)])]
    unnamed x133 -> x137, local copies, waits for them, and re-layouts: 11.2 us -> 10.9 us
  transfers between devices with their start and end apart: 85 -> 85, of which waited for: 28 -> 29; matrix products, arithmetic and copies ran while one was open for 8% -> 9% of each run, Pallas kernels for 45% -> 45%
where the time goes in v5:
time: 517 us; the launch traced here: 512 us
  Pallas kernels  237 us (46%)
  waiting for transfers between devices  126 us (24%)
  starting transfers between devices  86.2 us (17%)
  other arithmetic  28.1 us (5%)
  local copies, waits for them, and re-layouts  26.3 us (5%)
    pallas_call x4, Pallas kernels, run_experts(): pl.pallas_call(functools.partial(experts_kernel, capacity), grid_spec=plt...  89.5 us
    ppermute x61, waiting for transfers between devices, swap(): return lax.ppermute(value, axis, [(i, i ^ step) for i in range(size)])  78.6 us
    pallas_call x15, Pallas kernels, added(): pl.pallas_call(add_kernel, grid=(steps,), in_specs=[spec, spec], out_spec...  47.8 us
    ppermute x24, waiting for transfers between devices, shifted(): lax.ppermute(value, axis, [(i, (i + step) % size) for i in range(size)])  47.8 us
    ppermute x61, starting transfers between devices, swap(): return lax.ppermute(value, axis, [(i, i ^ step) for i in range(size)])  43.1 us
    ppermute x24, starting transfers between devices, shifted(): lax.ppermute(value, axis, [(i, (i + step) % size) for i in range(size)])  43.1 us
    pallas_call x8, Pallas kernels, spread(): pl.pallas_call(spread_kernel, grid_spec=pltpu.PrefetchScalarGridSpec(num_...  32.7 us
    pallas_call x7, Pallas kernels, pack(): pl.pallas_call(pack_kernel, grid_spec=pltpu.PrefetchScalarGridSpec(num_sc...  21.7 us
  transfers between devices with their start and end apart: 85, of which 29 were waited for; matrix products, arithmetic and copies ran while one was open for 9% of the time, Pallas kernels for 45%

profile of v5, /device:TPU:0, one launch (start us, length us, event | category | flops | bytes accessed | tf_op | source)
XLA Modules:
  0.0 511.6 jit_solution(12627236396542307910)
XLA Ops:
  33.9 6.9 %collective-permute-done.4 = bf16[256,384]{1,0:T(8,128)(2,1)S(1)} collective-permute-done((bf16[256,384]{1,0:T(8,128)(2,1)S(1)}, bf16[256,384]{1,0:T(8,128)(2,1)S(1)}, u32[]{:S(2)}, u32[]{:S(2)}) %collective-permute-start.4) | collective-permute-done | bytes 196640 | tf_op jit(solution)/shard_map/ppermute | solution.py:528
  40.8 4.2 collective-permute-done.5
  55.7 14.7 %attend.1 = (bf16[9,1024,64]{2,1,0:T(8,128)(2,1)}, f32[3,1024,64]{2,1,0:T(8,128)}, f32[3,1024,1]{2,1,0:T(8,128)}, bf16[1024,384]{1,0:T(8,128)(2,1)}) custom-call(bf16[1024,384]{1,0:T(8,128)(2,1)} %get-tuple-element.302.left_ref.normed_ref, bf16[1024,384]{1,0:T(8,128)(2,1)} %get-tuple-element.303.right_ref, bf16[384,576]{1,0:T(8,128)(2,1)} %copy-done.11, ...), custom_call_target="tpu_custom_call" | custom-call | flops 1 | bytes 1 | tf_op jit(solution)/shard_map/attend/pallas_call | solution.py:714
  98.3 4.8 collective-permute-done.14.refs_0_
  119.2 5.3 %collective-permute-done.21 = bf16[288,384]{1,0:T(8,128)(2,1)S(1)} collective-permute-done((bf16[288,384]{1,0:T(8,128)(2,1)S(1)}, bf16[288,384]{1,0:T(8,128)(2,1)S(1)}, u32[]{:S(2)}, u32[]{:S(2)}) %collective-permute-start.21) | collective-permute-done | bytes 221216 | tf_op jit(solution)/shard_map/ppermute | solution.py:533
  129.1 13.7 %collective-permute-done.24.token_peer_ref = bf16[1024,384]{1,0:T(8,128)(2,1)S(1)} collective-permute-done((bf16[1024,384]{1,0:T(8,128)(2,1)S(1)}, bf16[1024,384]{1,0:T(8,128)(2,1)S(1)}, u32[]{:S(2)}, u32[]{:S(2)}) %collective-permute-start.24) | collective-permute-done | bytes 786464 | tf_op jit(solution)/shard_map/ppermute | solution.py:528
  149.0 22.4 %run_experts.4 = (bf16[2,3,384,512]{3,2,1,0:T(8,128)(2,1)}, bf16[2,3,384,512]{3,2,1,0:T(8,128)(2,1)}, f32[4,1,1024]{2,1,0:T(1,128)}, f32[1024,384]{1,0:T(8,128)}, f32[1024,384]{1,0:T(8,128)}) custom-call(s32[4]{0:T(128)} %pad_add_fusion.1.place_ref, s32[16,1,1024]{2,1,0:T(1,128)} %broadcast_in_dim.145.rank_ref, f32[16,1,1024]{2,1,0:T(1,128)} %copy.86.prob_ref, ...), custom_call_target="tpu_custom_call" | custom-call | flops 1 | bytes 1 | tf_op jit(solution)/shard_map/run_experts/pallas_call | solution.py:960
  177.7 4.3 added.15
  184.1 22.3 %run_experts.5 = (bf16[2,3,384,512]{3,2,1,0:T(8,128)(2,1)}, bf16[2,3,384,512]{3,2,1,0:T(8,128)(2,1)}, f32[4,1,1024]{2,1,0:T(1,128)}, f32[1024,384]{1,0:T(8,128)}, f32[1024,384]{1,0:T(8,128)}) custom-call(s32[4]{0:T(128)} %pad_add_fusion.1.place_ref, s32[16,1,1024]{2,1,0:T(1,128)} %broadcast_in_dim.145.rank_ref, f32[16,1,1024]{2,1,0:T(1,128)} %copy.86.prob_ref, ...), custom_call_target="tpu_custom_call" | custom-call | flops 1 | bytes 1 | tf_op jit(solution)/shard_map/run_experts/pallas_call | solution.py:960
  206.4 6.9 %collective-permute-done.34.near_ref = bf16[1,3,384,256]{3,2,1,0:T(8,128)(2,1)S(1)} collective-permute-done((bf16[1,3,384,256]{3,2,1,0:T(8,128)(2,1)}, bf16[1,3,384,256]{3,2,1,0:T(8,128)(2,1)S(1)}, u32[]{:S(2)}, u32[]{:S(2)}) %collective-permute-start.34) | collective-permute-done | bytes 589856 | tf_op jit(solution)/shard_map/ppermute | solution.py:528
  220.7 13.3 %run_shared.1 = (bf16[1,3,384,256]{3,2,1,0:T(8,128)(2,1)}, bf16[1,3,384,256]{3,2,1,0:T(8,128)(2,1)}, f32[1024,384]{1,0:T(8,128)}, f32[1024,384]{1,0:T(8,128)}) custom-call(s32[2]{0:T(128)} %pad_add_fusion.2.place_ref, bf16[1024,384]{1,0:T(8,128)(2,1)} %copy-done.2, bf16[1024,384]{1,0:T(8,128)(2,1)} %copy-done.5, bf16[1024,384]{1,0:T(8,128)(2,1)} %copy-done.3, ...), custom_call_target="tpu_custom_call" | custom-call | flops 1 | bytes 1 | tf_op jit(solution)/shard_map/run_shared/pallas_call | solution.py:872
  238.4 4.4 added.17
  243.2 5.3 %collective-permute-done.41.refs_0_ = bf16[1,3,384,512]{3,2,1,0:T(8,128)(2,1)} collective-permute-done((bf16[1,3,384,512]{3,2,1,0:T(8,128)(2,1)}, bf16[1,3,384,512]{3,2,1,0:T(8,128)(2,1)}, u32[]{:S(2)}, u32[]{:S(2)}) %collective-permute-start.41) | collective-permute-done | bytes 1179680 | tf_op jit(solution)/shard_map/ppermute | solution.py:528
  250.6 22.2 %run_experts.6 = (bf16[2,3,384,512]{3,2,1,0:T(8,128)(2,1)}, bf16[2,3,384,512]{3,2,1,0:T(8,128)(2,1)}, f32[4,1,1024]{2,1,0:T(1,128)}, f32[1024,384]{1,0:T(8,128)}, f32[1024,384]{1,0:T(8,128)}) custom-call(s32[4]{0:T(128)} %pad_add_fusion.1.place_ref, s32[16,1,1024]{2,1,0:T(1,128)} %broadcast_in_dim.145.rank_ref, f32[16,1,1024]{2,1,0:T(1,128)} %copy.86.prob_ref, ...), custom_call_target="tpu_custom_call" | custom-call | flops 1 | bytes 1 | tf_op jit(solution)/shard_map/run_experts/pallas_call | solution.py:960
  275.8 4.2 spread.8
  281.4 5.4 %collective-permute-done.47.refs_3_ = bf16[1,3,384,512]{3,2,1,0:T(8,128)(2,1)} collective-permute-done((bf16[1,3,384,512]{3,2,1,0:T(8,128)(2,1)S(1)}, bf16[1,3,384,512]{3,2,1,0:T(8,128)(2,1)}, u32[]{:S(2)}, u32[]{:S(2)}) %collective-permute-start.47) | collective-permute-done | bytes 1179680 | tf_op jit(solution)/shard_map/ppermute | solution.py:528
  286.8 22.5 %run_experts.7 = (bf16[2,3,384,512]{3,2,1,0:T(8,128)(2,1)}, bf16[2,3,384,512]{3,2,1,0:T(8,128)(2,1)}, f32[4,1,1024]{2,1,0:T(1,128)}, f32[1024,384]{1,0:T(8,128)}, f32[1024,384]{1,0:T(8,128)}) custom-call(s32[4]{0:T(128)} %pad_add_fusion.1.place_ref, s32[16,1,1024]{2,1,0:T(1,128)} %broadcast_in_dim.145.rank_ref, f32[16,1,1024]{2,1,0:T(1,128)} %copy.86.prob_ref, ...), custom_call_target="tpu_custom_call" | custom-call | flops 1 | bytes 1 | tf_op jit(solution)/shard_map/run_experts/pallas_call | solution.py:960
  312.3 4.5 added.19
  317.7 4.8 collective-permute-start.53
  328.9 9.1 %collective-permute-done.52 = bf16[288,384]{1,0:T(8,128)(2,1)S(1)} collective-permute-done((bf16[288,384]{1,0:T(8,128)(2,1)S(1)}, bf16[288,384]{1,0:T(8,128)(2,1)S(1)}, u32[]{:S(2)}, u32[]{:S(2)}) %collective-permute-start.52) | collective-permute-done | bytes 221216 | tf_op jit(solution)/shard_map/ppermute | solution.py:533
  342.6 4.1 spread.9
  346.7 6.4 %collective-permute-done.49.two_ref = bf16[1,3,384,512]{3,2,1,0:T(8,128)(2,1)} collective-permute-done((bf16[1,3,384,512]{3,2,1,0:T(8,128)(2,1)}, bf16[1,3,384,512]{3,2,1,0:T(8,128)(2,1)}, u32[]{:S(2)}, u32[]{:S(2)}) %collective-permute-start.49) | collective-permute-done | bytes 1179680 | tf_op jit(solution)/shard_map/ppermute | solution.py:528
  363.9 5.3 %collective-permute-done.57 = bf16[256,384]{1,0:T(8,128)(2,1)S(1)} collective-permute-done((bf16[256,384]{1,0:T(8,128)(2,1)S(1)}, bf16[256,384]{1,0:T(8,128)(2,1)S(1)}, u32[]{:S(2)}, u32[]{:S(2)}) %collective-permute-start.57) | collective-permute-done | bytes 196640 | tf_op jit(solution)/shard_map/ppermute | solution.py:533
  369.2 6.5 %collective-permute-done.58 = bf16[256,384]{1,0:T(8,128)(2,1)S(1)} collective-permute-done((bf16[256,384]{1,0:T(8,128)(2,1)S(1)}, bf16[256,384]{1,0:T(8,128)(2,1)S(1)}, u32[]{:S(2)}, u32[]{:S(2)}) %collective-permute-start.58) | collective-permute-done | bytes 196640 | tf_op jit(solution)/shard_map/ppermute | solution.py:533
  379.1 4.1 spread.10
  383.1 4.1 spread.11
  387.2 4.4 added.23
  412.8 17.0 %attend_back.1 = (f32[1024,384]{1,0:T(8,128)}, bf16[384,576]{1,0:T(8,128)(2,1)}) custom-call(bf16[1024,192]{1,0:T(8,128)(2,1)} %copy-done.16, bf16[1024,192]{1,0:T(8,128)(2,1)} %collective-permute-done.64.peer_ref, bf16[9,1024,64]{2,1,0:T(8,128)(2,1)} %get-tuple-element.522.qkv_ref, f32[3,1024,64]{2,1,0:T(8,128)} %get-tuple-element.523.attended_ref, ...), custom_call_target="tpu_custom_call" | custom-call | flops 1 | bytes 1 | tf_op jit(solution)/shard_map/attend_back/pallas_call | solution.py:767
  444.2 10.8 %collective-permute-done.71 = bf16[256,384]{1,0:T(8,128)(2,1)S(1)} collective-permute-done((bf16[256,384]{1,0:T(8,128)(2,1)S(1)}, bf16[256,384]{1,0:T(8,128)(2,1)S(1)}, u32[]{:S(2)}, u32[]{:S(2)}) %collective-permute-start.71) | collective-permute-done | bytes 196640 | tf_op jit(solution)/shard_map/ppermute | solution.py:533
  461.9 4.2 spread.13
  488.7 4.1 spread.14
  506.2 4.1 spread.15
  (448 shorter events, 231.2 us)
Async XLA Ops:
  22.4 27.5 %collective-permute-start.7 = (bf16[384,576]{1,0:T(8,128)(2,1)S(1)}, bf16[384,576]{1,0:T(8,128)(2,1)}, u32[]{:S(2)}, u32[]{:S(2)}) collective-permute-start(bf16[384,576]{1,0:T(8,128)(2,1)S(1)} %copy.79.weight_left_ref.weight_ref), channel_id=1, source_target_pairs={{0,4},{4,0},{1,5},{5,1},{2,6},{6,2},{3,7},{7,3},{8,12},{12,8},{9,1... | collective-permute-start | bytes 1327112 | tf_op jit(solution)/shard_map/ppermute | solution.py:528
  49.9 27.5 %collective-permute-start.10 = (bf16[1,3,384,512]{3,2,1,0:T(8,128)(2,1)S(1)}, bf16[1,3,384,512]{3,2,1,0:T(8,128)(2,1)}, u32[]{:S(2)}, u32[]{:S(2)}) collective-permute-start(bf16[1,3,384,512]{3,2,1,0:T(8,128)(2,1)S(1)} %copy-done.25), channel_id=1, source_target_pairs={{0,4},{4,0},{1,5},{5,1},{2,6},{6,2},{3,7},{7,3},{8,12},{12,8},{9,1... | collective-permute-start | bytes 3538952 | tf_op jit(solution)/shard_map/ppermute | solution.py:528
  50.7 26.6 %collective-permute-start.11 = (bf16[256,384]{1,0:T(8,128)(2,1)S(1)}, bf16[256,384]{1,0:T(8,128)(2,1)S(1)}, u32[]{:S(2)}, u32[]{:S(2)}) collective-permute-start(bf16[256,384]{1,0:T(8,128)(2,1)S(1)} %copy-done.17), channel_id=1, source_target_pairs={{0,1},{1,2},{2,3},{3,0},{4,5},{5,6},{6,7},{7,4},{8,9},{9,10},{10,1... | collective-permute-start | bytes 589832 | tf_op jit(solution)/shard_map/ppermute | solution.py:533
  51.7 25.6 %collective-permute-start.12 = (bf16[256,384]{1,0:T(8,128)(2,1)S(1)}, bf16[256,384]{1,0:T(8,128)(2,1)S(1)}, u32[]{:S(2)}, u32[]{:S(2)}) collective-permute-start(bf16[256,384]{1,0:T(8,128)(2,1)S(1)} %copy-done.17), channel_id=1, source_target_pairs={{0,2},{1,3},{2,0},{3,1},{4,6},{5,7},{6,4},{7,5},{8,10},{9,11},{10,... | collective-permute-start | bytes 589832 | tf_op jit(solution)/shard_map/ppermute | solution.py:533
  51.8 25.6 %collective-permute-start.13 = (bf16[256,384]{1,0:T(8,128)(2,1)S(1)}, bf16[256,384]{1,0:T(8,128)(2,1)S(1)}, u32[]{:S(2)}, u32[]{:S(2)}) collective-permute-start(bf16[256,384]{1,0:T(8,128)(2,1)S(1)} %copy-done.17), channel_id=1, source_target_pairs={{0,3},{1,0},{2,1},{3,2},{4,7},{5,4},{6,5},{7,6},{8,11},{9,8},{10,9... | collective-permute-start | bytes 589832 | tf_op jit(solution)/shard_map/ppermute | solution.py:533
  77.4 25.7 %collective-permute-start.14 = (bf16[1,3,384,512]{3,2,1,0:T(8,128)(2,1)}, bf16[1,3,384,512]{3,2,1,0:T(8,128)(2,1)S(1)}, u32[]{:S(2)}, u32[]{:S(2)}) collective-permute-start(bf16[1,3,384,512]{3,2,1,0:T(8,128)(2,1)} %pack.8), channel_id=1, source_target_pairs={{0,4},{4,0},{1,5},{5,1},{2,6},{6,2},{3,7},{7,3},{8,12},{12,8},{9,1... | collective-permute-start | bytes 3538952 | tf_op jit(solution)/shard_map/ppermute | solution.py:528
  78.9 25.5 %collective-permute-start.15 = (bf16[1,3,384,512]{3,2,1,0:T(8,128)(2,1)}, bf16[1,3,384,512]{3,2,1,0:T(8,128)(2,1)}, u32[]{:S(2)}, u32[]{:S(2)}) collective-permute-start(bf16[1,3,384,512]{3,2,1,0:T(8,128)(2,1)} %collective-permute-done.10.refs_0_), channel_id=1, source_target_pairs={{0,16},{8,24},{16,0},{24,8},{1,17},{9,25},{17,1},{25,9},{2,18},{10... | collective-permute-start | bytes 3538952 | tf_op jit(solution)/shard_map/ppermute | solution.py:528
  127.5 43.9 %collective-permute-start.28 = (bf16[1,3,384,512]{3,2,1,0:T(8,128)(2,1)S(1)}, bf16[1,3,384,512]{3,2,1,0:T(8,128)(2,1)}, u32[]{:S(2)}, u32[]{:S(2)}) collective-permute-start(bf16[1,3,384,512]{3,2,1,0:T(8,128)(2,1)S(1)} %copy-done.23), channel_id=1, source_target_pairs={{0,16},{8,24},{16,0},{24,8},{1,17},{9,25},{17,1},{25,9},{2,18},{10... | collective-permute-start | bytes 3538952 | tf_op jit(solution)/shard_map/ppermute | solution.py:528
  142.9 28.6 %collective-permute-start.27 = (bf16[1,3,384,512]{3,2,1,0:T(8,128)(2,1)}, bf16[1,3,384,512]{3,2,1,0:T(8,128)(2,1)}, u32[]{:S(2)}, u32[]{:S(2)}) collective-permute-start(bf16[1,3,384,512]{3,2,1,0:T(8,128)(2,1)} %pack.9), channel_id=1, source_target_pairs={{0,4},{4,0},{1,5},{5,1},{2,6},{6,2},{3,7},{7,3},{8,12},{12,8},{9,1... | collective-permute-start | bytes 3538952 | tf_op jit(solution)/shard_map/ppermute | solution.py:528
  172.1 41.2 %collective-permute-start.31 = (bf16[1,3,384,512]{3,2,1,0:T(8,128)(2,1)}, bf16[1,3,384,512]{3,2,1,0:T(8,128)(2,1)}, u32[]{:S(2)}, u32[]{:S(2)}) collective-permute-start(bf16[1,3,384,512]{3,2,1,0:T(8,128)(2,1)} %pack.10), channel_id=1, source_target_pairs={{0,4},{4,0},{1,5},{5,1},{2,6},{6,2},{3,7},{7,3},{8,12},{12,8},{9,1... | collective-permute-start | bytes 3538952 | tf_op jit(solution)/shard_map/ppermute | solution.py:528
  182.0 31.3 %collective-permute-start.30 = (bf16[1,3,384,512]{3,2,1,0:T(8,128)(2,1)}, bf16[1,3,384,512]{3,2,1,0:T(8,128)(2,1)S(1)}, u32[]{:S(2)}, u32[]{:S(2)}) collective-permute-start(bf16[1,3,384,512]{3,2,1,0:T(8,128)(2,1)} %get-tuple-element.389.one_ref), channel_id=1, source_target_pairs={{0,16},{8,24},{16,0},{24,8},{1,17},{9,25},{17,1},{25,9},{2,18},{10... | collective-permute-start | bytes 3538952 | tf_op jit(solution)/shard_map/ppermute | solution.py:528
  183.6 29.7 %collective-permute-start.34 = (bf16[1,3,384,256]{3,2,1,0:T(8,128)(2,1)}, bf16[1,3,384,256]{3,2,1,0:T(8,128)(2,1)S(1)}, u32[]{:S(2)}, u32[]{:S(2)}) collective-permute-start(bf16[1,3,384,256]{3,2,1,0:T(8,128)(2,1)} %pack.11), channel_id=1, source_target_pairs={{0,4},{4,0},{1,5},{5,1},{2,6},{6,2},{3,7},{7,3},{8,12},{12,8},{9,1... | collective-permute-start | bytes 1769480 | tf_op jit(solution)/shard_map/ppermute | solution.py:528
  215.0 28.2 %collective-permute-start.35 = (bf16[1,3,384,512]{3,2,1,0:T(8,128)(2,1)}, bf16[1,3,384,512]{3,2,1,0:T(8,128)(2,1)}, u32[]{:S(2)}, u32[]{:S(2)}) collective-permute-start(bf16[1,3,384,512]{3,2,1,0:T(8,128)(2,1)} %get-tuple-element.413.one_ref), channel_id=1, source_target_pairs={{0,16},{8,24},{16,0},{24,8},{1,17},{9,25},{17,1},{25,9},{2,18},{10... | collective-permute-start | bytes 3538952 | tf_op jit(solution)/shard_map/ppermute | solution.py:528
  216.5 26.7 %collective-permute-start.39 = (bf16[1,3,384,512]{3,2,1,0:T(8,128)(2,1)}, bf16[1,3,384,512]{3,2,1,0:T(8,128)(2,1)}, u32[]{:S(2)}, u32[]{:S(2)}) collective-permute-start(bf16[1,3,384,512]{3,2,1,0:T(8,128)(2,1)} %collective-permute-done.27.refs_0_), channel_id=1, source_target_pairs={{0,8},{8,0},{16,24},{24,16},{1,9},{9,1},{17,25},{25,17},{2,10},{10... | collective-permute-start | bytes 3538952 | tf_op jit(solution)/shard_map/ppermute | solution.py:528
  216.5 26.7 %collective-permute-start.40 = (bf16[1,3,384,512]{3,2,1,0:T(8,128)(2,1)}, bf16[1,3,384,512]{3,2,1,0:T(8,128)(2,1)}, u32[]{:S(2)}, u32[]{:S(2)}) collective-permute-start(bf16[1,3,384,512]{3,2,1,0:T(8,128)(2,1)} %collective-permute-done.31.refs_1_), channel_id=1, source_target_pairs={{0,8},{8,0},{16,24},{24,16},{1,9},{9,1},{17,25},{25,17},{2,10},{10... | collective-permute-start | bytes 3538952 | tf_op jit(solution)/shard_map/ppermute | solution.py:528
  220.2 28.3 %collective-permute-start.41 = (bf16[1,3,384,512]{3,2,1,0:T(8,128)(2,1)}, bf16[1,3,384,512]{3,2,1,0:T(8,128)(2,1)}, u32[]{:S(2)}, u32[]{:S(2)}) collective-permute-start(bf16[1,3,384,512]{3,2,1,0:T(8,128)(2,1)} %pack.12), channel_id=1, source_target_pairs={{0,4},{4,0},{1,5},{5,1},{2,6},{6,2},{3,7},{7,3},{8,12},{12,8},{9,1... | collective-permute-start | bytes 3538952 | tf_op jit(solution)/shard_map/ppermute | solution.py:528
  248.5 31.5 %collective-permute-start.42 = (bf16[1,3,384,512]{3,2,1,0:T(8,128)(2,1)}, bf16[1,3,384,512]{3,2,1,0:T(8,128)(2,1)}, u32[]{:S(2)}, u32[]{:S(2)}) collective-permute-start(bf16[1,3,384,512]{3,2,1,0:T(8,128)(2,1)} %get-tuple-element.438.one_ref), channel_id=1, source_target_pairs={{0,16},{8,24},{16,0},{24,8},{1,17},{9,25},{17,1},{25,9},{2,18},{10... | collective-permute-start | bytes 3538952 | tf_op jit(solution)/shard_map/ppermute | solution.py:528
  250.1 29.9 %collective-permute-start.43 = (bf16[1,3,384,512]{3,2,1,0:T(8,128)(2,1)}, bf16[1,3,384,512]{3,2,1,0:T(8,128)(2,1)S(1)}, u32[]{:S(2)}, u32[]{:S(2)}) collective-permute-start(bf16[1,3,384,512]{3,2,1,0:T(8,128)(2,1)} %pack.13), channel_id=1, source_target_pairs={{0,4},{4,0},{1,5},{5,1},{2,6},{6,2},{3,7},{7,3},{8,12},{12,8},{9,1... | collective-permute-start | bytes 3538952 | tf_op jit(solution)/shard_map/ppermute | solution.py:528
  250.6 29.4 %collective-permute-start.44 = (bf16[1,3,384,512]{3,2,1,0:T(8,128)(2,1)}, bf16[1,3,384,512]{3,2,1,0:T(8,128)(2,1)}, u32[]{:S(2)}, u32[]{:S(2)}) collective-permute-start(bf16[1,3,384,512]{3,2,1,0:T(8,128)(2,1)} %collective-permute-done.41.refs_0_), channel_id=1, source_target_pairs={{0,8},{8,0},{16,24},{24,16},{1,9},{9,1},{17,25},{25,17},{2,10},{10... | collective-permute-start | bytes 3538952 | tf_op jit(solution)/shard_map/ppermute | solution.py:528
  280.0 32.2 %collective-permute-start.48 = (bf16[2,3,384,512]{3,2,1,0:T(8,128)(2,1)}, bf16[2,3,384,512]{3,2,1,0:T(8,128)(2,1)}, u32[]{:S(2)}, u32[]{:S(2)}) collective-permute-start(bf16[2,3,384,512]{3,2,1,0:T(8,128)(2,1)} %get-tuple-element.434), channel_id=1, source_target_pairs={{0,8},{8,0},{16,24},{24,16},{1,9},{9,1},{17,25},{25,17},{2,10},{10... | collective-permute-start | bytes 7077896 | tf_op jit(solution)/shard_map/ppermute | solution.py:528
  280.7 36.1 %collective-permute-start.45 = (bf16[1,3,384,512]{3,2,1,0:T(8,128)(2,1)}, bf16[1,3,384,512]{3,2,1,0:T(8,128)(2,1)}, u32[]{:S(2)}, u32[]{:S(2)}) collective-permute-start(bf16[1,3,384,512]{3,2,1,0:T(8,128)(2,1)} %get-tuple-element.458.one_ref), channel_id=1, source_target_pairs={{0,16},{8,24},{16,0},{24,8},{1,17},{9,25},{17,1},{25,9},{2,18},{10... | collective-permute-start | bytes 3538952 | tf_op jit(solution)/shard_map/ppermute | solution.py:528
  281.2 35.6 %collective-permute-start.46 = (bf16[1,3,384,512]{3,2,1,0:T(8,128)(2,1)S(1)}, bf16[1,3,384,512]{3,2,1,0:T(8,128)(2,1)}, u32[]{:S(2)}, u32[]{:S(2)}) collective-permute-start(bf16[1,3,384,512]{3,2,1,0:T(8,128)(2,1)S(1)} %copy-done.10), channel_id=1, source_target_pairs={{0,8},{8,0},{16,24},{24,16},{1,9},{9,1},{17,25},{25,17},{2,10},{10... | collective-permute-start | bytes 3538952 | tf_op jit(solution)/shard_map/ppermute | solution.py:528
  325.0 28.0 %collective-permute-start.49 = (bf16[1,3,384,512]{3,2,1,0:T(8,128)(2,1)}, bf16[1,3,384,512]{3,2,1,0:T(8,128)(2,1)}, u32[]{:S(2)}, u32[]{:S(2)}) collective-permute-start(bf16[1,3,384,512]{3,2,1,0:T(8,128)(2,1)} %get-tuple-element.480.one_ref), channel_id=1, source_target_pairs={{0,16},{8,24},{16,0},{24,8},{1,17},{9,25},{17,1},{25,9},{2,18},{10... | collective-permute-start | bytes 3538952 | tf_op jit(solution)/shard_map/ppermute | solution.py:528
  325.6 27.5 %collective-permute-start.50 = (bf16[1,3,384,512]{3,2,1,0:T(8,128)(2,1)S(1)}, bf16[1,3,384,512]{3,2,1,0:T(8,128)(2,1)S(1)}, u32[]{:S(2)}, u32[]{:S(2)}) collective-permute-start(bf16[1,3,384,512]{3,2,1,0:T(8,128)(2,1)S(1)} %copy-done.9), channel_id=1, source_target_pairs={{0,8},{8,0},{16,24},{24,16},{1,9},{9,1},{17,25},{25,17},{2,10},{10... | collective-permute-start | bytes 3538952 | tf_op jit(solution)/shard_map/ppermute | solution.py:528
  353.1 34.2 %collective-permute-start.61 = (bf16[2,3,384,512]{3,2,1,0:T(8,128)(2,1)}, bf16[2,3,384,512]{3,2,1,0:T(8,128)(2,1)}, u32[]{:S(2)}, u32[]{:S(2)}) collective-permute-start(bf16[2,3,384,512]{3,2,1,0:T(8,128)(2,1)} %get-tuple-element.484), channel_id=1, source_target_pairs={{0,8},{8,0},{16,24},{24,16},{1,9},{9,1},{17,25},{25,17},{2,10},{10... | collective-permute-start | bytes 7077896 | tf_op jit(solution)/shard_map/ppermute | solution.py:528
  363.4 28.3 %collective-permute-start.55 = (bf16[1,3,384,512]{3,2,1,0:T(8,128)(2,1)}, bf16[1,3,384,512]{3,2,1,0:T(8,128)(2,1)}, u32[]{:S(2)}, u32[]{:S(2)}) collective-permute-start(bf16[1,3,384,512]{3,2,1,0:T(8,128)(2,1)} %get-tuple-element.510.one_ref), channel_id=1, source_target_pairs={{0,16},{8,24},{16,0},{24,8},{1,17},{9,25},{17,1},{25,9},{2,18},{10... | collective-permute-start | bytes 3538952 | tf_op jit(solution)/shard_map/ppermute | solution.py:528
  398.2 34.0 %collective-permute-start.63 = (bf16[1,3,384,512]{3,2,1,0:T(8,128)(2,1)}, bf16[1,3,384,512]{3,2,1,0:T(8,128)(2,1)}, u32[]{:S(2)}, u32[]{:S(2)}) collective-permute-start(bf16[1,3,384,512]{3,2,1,0:T(8,128)(2,1)} %added.24.half_ref), channel_id=1, source_target_pairs={{0,8},{8,0},{16,24},{24,16},{1,9},{9,1},{17,25},{25,17},{2,10},{10... | collective-permute-start | bytes 3538952 | tf_op jit(solution)/shard_map/ppermute | solution.py:528
  400.0 32.2 %collective-permute-start.62 = (bf16[1,3,384,512]{3,2,1,0:T(8,128)(2,1)}, bf16[1,3,384,512]{3,2,1,0:T(8,128)(2,1)}, u32[]{:S(2)}, u32[]{:S(2)}) collective-permute-start(bf16[1,3,384,512]{3,2,1,0:T(8,128)(2,1)} %get-tuple-element.540.one_ref), channel_id=1, source_target_pairs={{0,16},{8,24},{16,0},{24,8},{1,17},{9,25},{17,1},{25,9},{2,18},{10... | collective-permute-start | bytes 3538952 | tf_op jit(solution)/shard_map/ppermute | solution.py:528
  401.7 30.4 %collective-permute-start.65 = (bf16[256,384]{1,0:T(8,128)(2,1)}, bf16[256,384]{1,0:T(8,128)(2,1)}, u32[]{:S(2)}, u32[]{:S(2)}) collective-permute-start(bf16[256,384]{1,0:T(8,128)(2,1)} %get-tuple-element.651), channel_id=1, source_target_pairs={{0,3},{1,0},{2,1},{3,2},{4,7},{5,4},{6,5},{7,6},{8,11},{9,8},{10,9... | collective-permute-start | bytes 589832 | tf_op jit(solution)/shard_map/ppermute | solution.py:533
  439.9 29.2 %collective-permute-start.69 = (bf16[1,3,384,512]{3,2,1,0:T(8,128)(2,1)}, bf16[1,3,384,512]{3,2,1,0:T(8,128)(2,1)}, u32[]{:S(2)}, u32[]{:S(2)}) collective-permute-start(bf16[1,3,384,512]{3,2,1,0:T(8,128)(2,1)} %get-tuple-element.567.one_ref), channel_id=1, source_target_pairs={{0,16},{8,24},{16,0},{24,8},{1,17},{9,25},{17,1},{25,9},{2,18},{10... | collective-permute-start | bytes 3538952 | tf_op jit(solution)/shard_map/ppermute | solution.py:528
  459.9 24.1 %collective-permute-start.77 = (bf16[1,3,384,256]{3,2,1,0:T(8,128)(2,1)}, bf16[1,3,384,256]{3,2,1,0:T(8,128)(2,1)}, u32[]{:S(2)}, u32[]{:S(2)}) collective-permute-start(bf16[1,3,384,256]{3,2,1,0:T(8,128)(2,1)} %added.25.one_ref), channel_id=1, source_target_pairs={{0,16},{8,24},{16,0},{24,8},{1,17},{9,25},{17,1},{25,9},{2,18},{10... | collective-permute-start | bytes 1769480 | tf_op jit(solution)/shard_map/ppermute | solution.py:528
  475.1 31.1 %collective-permute-start.84 = (bf16[1,3,384,512]{3,2,1,0:T(8,128)(2,1)}, bf16[1,3,384,512]{3,2,1,0:T(8,128)(2,1)}, u32[]{:S(2)}, u32[]{:S(2)}) collective-permute-start(bf16[1,3,384,512]{3,2,1,0:T(8,128)(2,1)} %added.29.half_ref), channel_id=1, source_target_pairs={{0,8},{8,0},{16,24},{24,16},{1,9},{9,1},{17,25},{25,17},{2,10},{10... | collective-permute-start | bytes 3538952 | tf_op jit(solution)/shard_map/ppermute | solution.py:528
  (116 other events, 1191.4 us)
